TPU v7x, 256 devices: a whole 4x4x8 slice. The times are simulated.
256 devices in a mesh: row: 8 (over y, z_lo), col: 32 (over x, z_hi, core).
Axes of the slice: x: 4, y: 4, z: 8 (z_hi: 4, z_lo: 2; z = z_hi * 2 + z_lo), core: 2. Of those that a mesh axis runs over, the one named last changes fastest.
Arguments:
- x_init: float32 [4096, 64, 128], P(('row', 'col')), may hold values from -6 to 6
- gen_blocks: bfloat16 [8, 32, 256, 128, 128], P('row', 'col'), may hold values from -0.09375 to 0.09375
- blk_src: int32 [8, 32, 256], P('row', 'col'), may hold values from 0 to 511, as said below
- blk_dst: int32 [8, 32, 256], P('row', 'col'), may hold values from 0 to 127
- reward: int32 [4096, 128], P(('row', 'col')), may hold values 0 or 1
- horizon: float32 [1], replicated, may hold values from 1.5 to 4
Outputs:
- state: float32 [4096, 64, 128], P(('row', 'col'))
- accumulated: float32 [4096, 64, 128], P(('row', 'col'))
Inputs may be any that keep to these rules, and one draw needn't show every extreme that they name: `blk_src`: on each device, slot j names a block-row in [(j // 8) * 16, (j // 8 + 1) * 16), and the 8 slots of one such group name distinct block-rows.
All inputs are finite; a program needn't handle non-finite values. No bound on the sum of `reward` on one device may be relied on, other than what follows from the above.
Results may differ from a plain program's by a relative error of at most 0.0021.
Values may be sent and summed in bfloat16 or wider, within the bound.
No kernel may reach another device: no remote copies, remote signals or barrier semaphores. Data moves between devices by JAX's collectives and lax.ppermute only.
A program may use at most 64 MiB of HBM per device.

v0:
```python
import jax
import jax.numpy as jnp
from jax import lax
from jax.sharding import PartitionSpec as P

STEPS = 3


def poisson_weights(horizon):
    rate_time = horizon[0]
    poisson_term = jnp.exp(-rate_time)
    cumulated = poisson_term
    weights = [(1.0 - cumulated) / rate_time]
    for iteration in range(STEPS):
        poisson_term = poisson_term * rate_time / (iteration + 1.0)
        cumulated = cumulated + poisson_term
        weights.append((1.0 - cumulated) / rate_time)
    return weights


def shards(x_init, gen_blocks, blk_src, blk_dst, reward, horizon):
    blocks = gen_blocks[0, 0]
    source_ids = blk_src[0, 0]
    target_ids = blk_dst[0, 0]
    row_count = lax.axis_size("row")
    span_len = x_init.shape[0]
    configs = x_init.shape[1]
    block_len = x_init.shape[2]
    weights = poisson_weights(horizon)
    reward_f = reward.astype(jnp.float32)[:, None, :]
    state = x_init
    accumulated = weights[0] * reward_f * state
    for iteration in range(STEPS):
        rounded = state.astype(jnp.bfloat16)
        whole_group = lax.all_gather(rounded, "col", axis=0, tiled=True)
        gathered_rows = whole_group[source_ids]
        products = jnp.einsum(
            "ncb,nbk->nck", gathered_rows, blocks, preferred_element_type=jnp.float32
        )
        partial_sum = (
            jnp.zeros((row_count * span_len, configs, block_len), jnp.float32)
            .at[target_ids]
            .add(products)
        )
        mine = lax.psum_scatter(partial_sum, "row", scatter_dimension=0, tiled=True)
        state = state + mine
        accumulated = accumulated + weights[iteration + 1] * reward_f * state
    return (state, accumulated)


def solution(mesh):
    in_specs = (
        P(("row", "col"), None, None),
        P("row", "col", None, None, None),
        P("row", "col", None),
        P("row", "col", None),
        P(("row", "col"), None),
        P(),
    )
    out_specs = (P(("row", "col"), None, None), P(("row", "col"), None, None))
    return jax.shard_map(shards, mesh=mesh, in_specs=in_specs, out_specs=out_specs, check_vma=False)
```

profile of v0, /device:TPU:1, one launch (start us, length us, event | category | flops | bytes accessed | tf_op | source)
XLA Modules:
  0.0 719.8 jit_solution(7048467292129157278)
XLA Ops:
  7.2 0.0 all-gather.4.cloned.1.call-start
  7.2 1.8 convert_element_type.12
  9.0 0.0 all-gather.4.cloned.1.call-update
  9.0 0.0 reduce-scatter.4.cloned.1.call-start
  9.1 0.7 compare_select_fusion
  9.8 0.7 compare_select_fusion.1
  10.4 81.0 %all-gather.4.cloned.1.call-done = bf16[512,64,128]{2,1,0:T(8,128)(2,1)} async-done(((bf16[16,64,128]{2,1,0:T(8,128)(2,1)}), bf16[512,64,128]{2,1,0:T(8,128)(2,1)}) %all-gather.4.cloned.1.call-update) | async-done | bytes 8388624 | tf_op jit(solution)/shard_map/all_gather | solution.py:35
  91.5 6.4 gather_fusion
  97.9 10.2 %fusion.4 = f32[256,64,128]{2,1,0:T(8,128)} fusion(bf16[256,64,128]{2,1,0:T(8,128)(2,1)} %gather_fusion, bf16[1,1,256,128,128]{4,3,2,1,0:T(8,128)(2,1)} %param.7), kind=kOutput, calls=%fused_computation.10 | convolution fusion | flops 536870912 | bytes 20971520 | tf_op jit(solution)/shard_map/ncb,nbk->nck/dot_general | solution.py:37
  108.1 2.5 broadcast.48.clone
  110.6 39.7 %scatter_fusion = f32[128,64,128]{2,1,0:T(8,128)} fusion(f32[128,64,128]{2,1,0:T(8,128)} %broadcast.48.clone, s32[256]{0:T(256)S(1)} %bitcast.25, f32[256,64,128]{2,1,0:T(8,128)} %fusion.4), kind=kCustom, calls=%fused_computation.3 | custom fusion | flops 2097152 | bytes 25166848 | tf_op jit(solution)/shard_map/scatter-add | solution.py:43
  150.3 0.0 copy-start
  150.3 0.0 reduce-scatter.4.cloned.1.call-update
  150.3 0.0 all-gather.6.cloned.1.call-start
  150.4 94.3 %reduce-scatter.4.cloned.1.call-done = f32[16,64,128]{2,1,0:T(8,128)} async-done(((f32[128,64,128]{2,1,0:T(8,128)}), f32[16,64,128]{2,1,0:T(8,128)}) %reduce-scatter.4.cloned.1.call-update) | async-done | bytes 524304 | tf_op jit(solution)/shard_map/reduce_scatter | solution.py:45
  244.7 0.0 copy-done
  244.7 1.8 fusion.7
  246.6 0.0 all-gather.6.cloned.1.call-update
  246.6 0.0 reduce-scatter.6.cloned.1.call-start
  246.6 77.9 %all-gather.6.cloned.1.call-done = bf16[512,64,128]{2,1,0:T(8,128)(2,1)} async-done(((bf16[16,64,128]{2,1,0:T(8,128)(2,1)}), bf16[512,64,128]{2,1,0:T(8,128)(2,1)}) %all-gather.6.cloned.1.call-update) | async-done | bytes 8388624 | tf_op jit(solution)/shard_map/all_gather | solution.py:35
  324.5 6.4 gather_fusion.1
  331.0 10.2 %fusion.2 = f32[256,64,128]{2,1,0:T(8,128)} fusion(bf16[256,64,128]{2,1,0:T(8,128)(2,1)} %gather_fusion.1, bf16[1,1,256,128,128]{4,3,2,1,0:T(8,128)(2,1)} %param.7), kind=kOutput, calls=%fused_computation.8 | convolution fusion | flops 536870912 | bytes 20971520 | tf_op jit(solution)/shard_map/ncb,nbk->nck/dot_general | solution.py:37
  341.2 2.5 broadcast.48.clone.1
  343.7 39.7 %scatter_fusion.1 = f32[128,64,128]{2,1,0:T(8,128)} fusion(f32[128,64,128]{2,1,0:T(8,128)} %broadcast.48.clone.1, s32[256]{0:T(256)S(1)} %bitcast.26, f32[256,64,128]{2,1,0:T(8,128)} %fusion.2), kind=kCustom, calls=%fused_computation.4 | custom fusion | flops 2097152 | bytes 25166848 | tf_op jit(solution)/shard_map/scatter-add | solution.py:43
  383.4 0.0 reduce-scatter.6.cloned.1.call-update
  383.4 0.0 all-gather.8.cloned.1.call-start
  383.4 94.3 %reduce-scatter.6.cloned.1.call-done = f32[16,64,128]{2,1,0:T(8,128)} async-done(((f32[128,64,128]{2,1,0:T(8,128)}), f32[16,64,128]{2,1,0:T(8,128)}) %reduce-scatter.6.cloned.1.call-update) | async-done | bytes 524304 | tf_op jit(solution)/shard_map/reduce_scatter | solution.py:45
  477.8 1.8 fusion.6
  479.6 0.0 all-gather.8.cloned.1.call-update
  479.6 0.2 reduce-scatter.8.cloned.1.call-start
  479.8 77.5 %all-gather.8.cloned.1.call-done = bf16[512,64,128]{2,1,0:T(8,128)(2,1)} async-done(((bf16[16,64,128]{2,1,0:T(8,128)(2,1)}), bf16[512,64,128]{2,1,0:T(8,128)(2,1)}) %all-gather.8.cloned.1.call-update) | async-done | bytes 8388624 | tf_op jit(solution)/shard_map/all_gather | solution.py:35
  557.4 6.4 gather_fusion.2
  563.8 10.2 %fusion = f32[256,64,128]{2,1,0:T(8,128)} fusion(bf16[256,64,128]{2,1,0:T(8,128)(2,1)} %gather_fusion.2, bf16[1,1,256,128,128]{4,3,2,1,0:T(8,128)(2,1)} %param.7), kind=kOutput, calls=%fused_computation.6 | convolution fusion | flops 536870912 | bytes 20971520 | tf_op jit(solution)/shard_map/ncb,nbk->nck/dot_general | solution.py:37
  574.0 2.5 broadcast.48
  576.5 39.7 %scatter_fusion.2 = f32[128,64,128]{2,1,0:T(8,128)} fusion(f32[128,64,128]{2,1,0:T(8,128)} %broadcast.48, s32[256]{0:T(256)S(1)} %bitcast.27, f32[256,64,128]{2,1,0:T(8,128)} %fusion), kind=kCustom, calls=%fused_computation.5 | custom fusion | flops 2097152 | bytes 25166848 | tf_op jit(solution)/shard_map/scatter-add | solution.py:43
  616.2 0.0 copy-start.1
  616.2 0.0 reduce-scatter.8.cloned.1.call-update
  617.1 0.0 copy-done.1
  617.1 93.5 %reduce-scatter.8.cloned.1.call-done = f32[16,64,128]{2,1,0:T(8,128)} async-done(((f32[128,64,128]{2,1,0:T(8,128)}), f32[16,64,128]{2,1,0:T(8,128)}) %reduce-scatter.8.cloned.1.call-update) | async-done | bytes 524304 | tf_op jit(solution)/shard_map/reduce_scatter | solution.py:45
  710.6 2.3 multiply_add_fusion
  (2 shorter events, 0.0 us)
Async XLA Ops:
  7.2 84.3 %all-gather.4.cloned.1.call-start = ((), (), s32[]{:S(2)}) async-start(), calls=%async_computation.3 | async-start | bytes 8650752 | tf_op jit(solution)/shard_map/all_gather | solution.py:35
  9.0 235.7 %reduce-scatter.4.cloned.1.call-start = ((), (), s32[]{:S(2)}) async-start(), calls=%async_computation.4 | async-start | bytes 4718592 | tf_op jit(solution)/shard_map/reduce_scatter | solution.py:45
  150.3 94.4 %copy-start = (f32[16,64,128]{2,1,0:T(8,128)S(1)}, f32[16,64,128]{2,1,0:T(8,128)}, u32[]{:S(2)}) copy-start(f32[16,64,128]{2,1,0:T(8,128)} %param.6) | copy-start | bytes 1572868
  150.3 174.2 %all-gather.6.cloned.1.call-start = ((), (), s32[]{:S(2)}) async-start(), calls=%async_computation.5 | async-start | bytes 8650752 | tf_op jit(solution)/shard_map/all_gather | solution.py:35
  246.6 231.2 %reduce-scatter.6.cloned.1.call-start = ((), (), s32[]{:S(2)}) async-start(), calls=%async_computation.6 | async-start | bytes 4718592 | tf_op jit(solution)/shard_map/reduce_scatter | solution.py:45
  383.4 174.0 %all-gather.8.cloned.1.call-start = ((), (), s32[]{:S(2)}) async-start(), calls=%async_computation.7 | async-start | bytes 8650752 | tf_op jit(solution)/shard_map/all_gather | solution.py:35
  479.6 231.0 %reduce-scatter.8.cloned.1.call-start = ((), (), s32[]{:S(2)}) async-start(), calls=%async_computation.8 | async-start | bytes 4718592 | tf_op jit(solution)/shard_map/reduce_scatter | solution.py:45
  616.2 0.9 copy-start.1
Sparse Core Ops, SparseCore 0:
  11.1 80.3 all-gather.3
  150.5 94.2 reduce-scatter.3
  247.9 76.6 all-gather.5
  383.5 94.2 reduce-scatter.5
  480.7 76.6 all-gather.7
  616.4 94.2 reduce-scatter.7
where the time goes:
time: 721 us; the launch traced here: 720 us
  waiting for transfers between devices  519 us (72%)
  other arithmetic  128 us (18%)
  matrix products  30.6 us (4%)
  local copies, waits for them, and re-layouts  26.8 us (4%)
  between operations  15 us (2%)
    reduce_scatter x3, waiting for transfers between devices, shards(): mine = lax.psum_scatter(partial_sum, 'row', scatter_dimension=0, tiled=True)  282 us
    all_gather x3, waiting for transfers between devices, shards(): whole_group = lax.all_gather(rounded, 'col', axis=0, tiled=True)  236 us
    scatter-add x3, other arithmetic, shards(): partial_sum = jnp.zeros((row_count * span_len, configs, block_len), jnp.f...  119 us
    dot_general x3, matrix products, shards(): jnp.einsum('ncb,nbk->nck', gathered_rows, blocks, preferred_element_type=...  30.6 us
    gather x3, local copies, waits for them, and re-layouts, shards(): gathered_rows = whole_group[source_ids]  19.3 us
  transfers between devices with their start and end apart: 6, of which 6 were waited for; matrix products, arithmetic and copies ran while one was open for 0% of the time, Pallas kernels for 0%

commit v1 on v0

v1 whole, which is shorter than its diff:
```python
import jax
import jax.numpy as jnp
from jax import lax
from jax.experimental import pallas as pl
from jax.experimental.pallas import tpu as pltpu
from jax.sharding import Mesh, PartitionSpec as P

STEPS = 3
AXES = ("y", "zl", "x", "zh", "core")
SHAPE = (4, 2, 4, 4, 2)
ROW = ("y", "zl")
COL = ("x", "zh", "core")
GROUPS = 8


def poisson_weights(horizon):
    rate_time = horizon[0]
    poisson_term = jnp.exp(-rate_time)
    cumulated = poisson_term
    weights = [(1.0 - cumulated) / rate_time]
    for iteration in range(STEPS):
        poisson_term = poisson_term * rate_time / (iteration + 1.0)
        cumulated = cumulated + poisson_term
        weights.append((1.0 - cumulated) / rate_time)
    return weights


def product_body(src, dst, order, x_ref, blk_ref, own_ref, *rest):
    sends, acc = rest[:-1], rest[-1]
    step = pl.program_id(0)
    slots = blk_ref.shape[0]
    held = x_ref.shape[0]
    span = own_ref.shape[0]

    @pl.when(step == 0)
    def _():
        acc[...] = jnp.zeros_like(acc)

    for slot in range(slots):
        at = step * slots + slot
        vectors = x_ref[src[at] - step * held]
        into = dst[at]
        acc[into] += jnp.dot(vectors, blk_ref[slot], preferred_element_type=jnp.float32)

    @pl.when(step == pl.num_programs(0) - 1)
    def _():
        own_ref[...] = acc[pl.ds(order[0] * span, span)]
        for place, send in enumerate(sends):
            send[...] = acc[pl.ds(order[place + 1] * span, span)].astype(send.dtype)


def products(src, dst, order, whole, blocks, rows, span):
    n, block_len, _ = blocks.shape
    configs = whole.shape[1]
    piece = (span, configs, block_len)
    outs = [jax.ShapeDtypeStruct(piece, jnp.float32)]
    outs += [jax.ShapeDtypeStruct(piece, jnp.bfloat16)] * (rows - 1)
    return pl.pallas_call(
        product_body,
        out_shape=outs,
        grid_spec=pltpu.PrefetchScalarGridSpec(
            num_scalar_prefetch=3,
            grid=(GROUPS,),
            in_specs=[
                pl.BlockSpec((whole.shape[0] // GROUPS, configs, block_len), lambda i, *_: (i, 0, 0)),
                pl.BlockSpec((n // GROUPS, block_len, block_len), lambda i, *_: (i, 0, 0)),
            ],
            out_specs=[pl.BlockSpec(piece, lambda i, *_: (0, 0, 0))] * rows,
            scratch_shapes=[pltpu.VMEM((rows * span, configs, block_len), jnp.float32)],
        ),
        compiler_params=pltpu.CompilerParams(vmem_limit_bytes=40 << 20),
        cost_estimate=pl.CostEstimate(
            flops=2 * n * configs * block_len * block_len,
            bytes_accessed=2 * (whole.size + blocks.size + rows * span * configs * block_len),
            transcendentals=0,
        ),
        name="products",
    )(src, dst, order, whole, blocks)


def shifted(dy, dzl):
    ny, nzl = SHAPE[0], SHAPE[1]
    return [
        (y * nzl + zl, (y + dy) % ny * nzl + (zl + dzl) % nzl)
        for y in range(ny)
        for zl in range(nzl)
    ]


def shards(x_init, gen_blocks, blk_src, blk_dst, reward, horizon):
    blocks = gen_blocks[0, 0]
    src = blk_src[0, 0]
    dst = blk_dst[0, 0]
    span = x_init.shape[0]
    ny, nzl = SHAPE[0], SHAPE[1]
    rows = ny * nzl
    weights = poisson_weights(horizon)
    reward_f = reward.astype(jnp.float32)[:, None, :]
    moves = [(dy, dzl) for dy in range(ny) for dzl in range(nzl)]
    y, zl = lax.axis_index("y"), lax.axis_index("zl")
    order = jnp.stack([(y + dy) % ny * nzl + (zl + dzl) % nzl for dy, dzl in moves]).astype(jnp.int32)
    state = x_init
    accumulated = weights[0] * reward_f * state
    for iteration in range(STEPS):
        rounded = state.astype(jnp.bfloat16)
        whole = lax.all_gather(rounded, COL, axis=0, tiled=True)
        own, *sends = products(src, dst, order, whole, blocks, rows, span)
        mine = own
        for (dy, dzl), send in zip(moves[1:], sends):
            mine = mine + lax.ppermute(send, ROW, shifted(dy, dzl)).astype(jnp.float32)
        state = state + mine
        accumulated = accumulated + weights[iteration + 1] * reward_f * state
    return (state, accumulated)


def solution(mesh):
    fine = Mesh(mesh.devices.reshape(SHAPE), AXES)
    rc = P((*ROW, *COL), None, None)
    in_specs = (
        rc,
        P(ROW, COL, None, None, None),
        P(ROW, COL, None),
        P(ROW, COL, None),
        P((*ROW, *COL), None),
        P(),
    )
    return jax.shard_map(shards, mesh=fine, in_specs=in_specs, out_specs=(rc, rc), check_vma=False)
```

time: 721 us -> 394 us (0.55)
  waiting for transfers between devices: 519 us -> 288 us
  other arithmetic: 128 us -> 6.84 us
  starting transfers between devices: 0.43 us -> 45.1 us
  matrix products: 30.6 us -> 0 us
  Pallas kernels: 0 us -> 24.9 us
  local copies, waits for them, and re-layouts: 26.8 us -> 12.3 us
    reduce_scatter x3 -> x0, waiting for transfers between devices: 282 us -> none  [shards(): mine = lax.psum_scatter(partial_sum, 'row', scatter_dimension=0, tiled=True)]
    scatter-add x3 -> x0, other arithmetic: 119 us -> none  [shards(): partial_sum = jnp.zeros((row_count * span_len, configs, block_len), jnp.f...]
    ppermute x0 -> x21, waiting for transfers between devices: none -> 49.8 us  [shards(): mine = mine + lax.ppermute(send, ROW, shifted(dy, dzl)).astype(jnp.float32)]
    ppermute x0 -> x21, starting transfers between devices: none -> 44.9 us  [shards(): mine = mine + lax.ppermute(send, ROW, shifted(dy, dzl)).astype(jnp.float32)]
    dot_general x3 -> x0, matrix products: 30.6 us -> none  [shards(): jnp.einsum('ncb,nbk->nck', gathered_rows, blocks, preferred_element_type=...]
    pallas_call x0 -> x3, Pallas kernels: none -> 24.9 us  [products(): pl.pallas_call(product_body, out_shape=outs, grid_spec=pltpu.PrefetchScal...]
    gather x3 -> x0, local copies, waits for them, and re-layouts: 19.3 us -> none  [shards(): gathered_rows = whole_group[source_ids]]
    unnamed x4 -> x22, local copies, waits for them, and re-layouts: 0.01 us -> 12.2 us
  transfers between devices with their start and end apart: 6 -> 24, of which waited for: 6 -> 10; matrix products, arithmetic and copies ran while one was open for 0% -> 0% of each run, Pallas kernels for 0% -> 0%
where the time goes in v1:
time: 394 us; the launch traced here: 392 us
  waiting for transfers between devices  288 us (73%)
  starting transfers between devices  45.1 us (11%)
  Pallas kernels  24.9 us (6%)
  between operations  14.8 us (4%)
  local copies, waits for them, and re-layouts  12.3 us (3%)
  other arithmetic  6.84 us (2%)
    all_gather x3, waiting for transfers between devices, shards(): whole = lax.all_gather(rounded, COL, axis=0, tiled=True)  238 us
    ppermute x21, waiting for transfers between devices, shards(): mine = mine + lax.ppermute(send, ROW, shifted(dy, dzl)).astype(jnp.float32)  49.8 us
    ppermute x21, starting transfers between devices, shards(): mine = mine + lax.ppermute(send, ROW, shifted(dy, dzl)).astype(jnp.float32)  44.9 us
    pallas_call x3, Pallas kernels, products(): pl.pallas_call(product_body, out_shape=outs, grid_spec=pltpu.PrefetchScal...  24.9 us
    unnamed x22, local copies, waits for them, and re-layouts  12.2 us
  transfers between devices with their start and end apart: 24, of which 10 were waited for; matrix products, arithmetic and copies ran while one was open for 0% of the time, Pallas kernels for 0%

profile of v1, /device:TPU:1, one launch (start us, length us, event | category | flops | bytes accessed | tf_op | source)
XLA Modules:
  0.0 391.6 jit_solution(8351540385292382671)
XLA Ops:
  7.2 0.0 all-gather.4.cloned.1.call-start
  7.2 1.8 convert_element_type.75
  9.0 0.0 all-gather.4.cloned.1.call-update
  9.0 0.0 all-gather.6.cloned.1.call-start
  9.1 0.1 stack.35.order
  9.2 82.3 %all-gather.4.cloned.1.call-done.x_ref = bf16[512,64,128]{2,1,0:T(8,128)(2,1)} async-done(((bf16[16,64,128]{2,1,0:T(8,128)(2,1)}), bf16[512,64,128]{2,1,0:T(8,128)(2,1)}) %all-gather.4.cloned.1.call-update) | async-done | bytes 8388624 | tf_op jit(solution)/shard_map/all_gather | solution.py:106
  91.5 3.4 copy-done
  94.9 0.7 copy-done.3
  95.5 0.7 copy-done.5
  96.2 8.3 %products.3 = (f32[16,64,128]{2,1,0:T(8,128)S(1)}, bf16[16,64,128]{2,1,0:T(8,128)(2,1)S(1)}, bf16[16,64,128]{2,1,0:T(8,128)(2,1)S(1)}, bf16[16,64,128]{2,1,0:T(8...) custom-call(s32[256]{0:T(256)S(1)} %bitcast.20, ...), custom_call_target="tpu_custom_call" | custom-call | flops 536870912 | bytes 18874368 | tf_op jit(solution)/shard_map/products/pallas_call | solution.py:58
  104.5 3.7 collective-permute-start
  108.2 1.5 collective-permute-start.1
  109.7 1.0 collective-permute-start.2
  110.7 1.4 collective-permute-start.3
  112.1 2.7 collective-permute-start.4
  114.8 2.7 collective-permute-start.5
  117.5 8.5 %collective-permute-done.1 = bf16[16,64,128]{2,1,0:T(8,128)(2,1)S(1)} collective-permute-done((bf16[16,64,128]{2,1,0:T(8,128)(2,1)S(1)}, bf16[16,64,128]{2,1,0:T(8,128)(2,1)S(1)}, u32[]{:S(2)}, u32[]{:S(2)}) %collective-permute-start.1) | collective-permute-done | bytes 262176 | tf_op jit(solution)/shard_map/ppermute | solution.py:110
  125.9 8.9 %collective-permute-done.3 = bf16[16,64,128]{2,1,0:T(8,128)(2,1)S(1)} collective-permute-done((bf16[16,64,128]{2,1,0:T(8,128)(2,1)S(1)}, bf16[16,64,128]{2,1,0:T(8,128)(2,1)S(1)}, u32[]{:S(2)}, u32[]{:S(2)}) %collective-permute-start.3) | collective-permute-done | bytes 262176 | tf_op jit(solution)/shard_map/ppermute | solution.py:110
  134.9 1.1 fusion.1
  135.9 0.0 all-gather.6.cloned.1.call-update
  136.0 0.0 all-gather.8.cloned.1.call-start
  136.0 79.6 %all-gather.6.cloned.1.call-done.x_ref = bf16[512,64,128]{2,1,0:T(8,128)(2,1)} async-done(((bf16[16,64,128]{2,1,0:T(8,128)(2,1)}), bf16[512,64,128]{2,1,0:T(8,128)(2,1)}) %all-gather.6.cloned.1.call-update) | async-done | bytes 8388624 | tf_op jit(solution)/shard_map/all_gather | solution.py:106
  215.7 3.4 copy-done.1
  219.0 8.3 %products.4 = (f32[16,64,128]{2,1,0:T(8,128)S(1)}, bf16[16,64,128]{2,1,0:T(8,128)(2,1)S(1)}, bf16[16,64,128]{2,1,0:T(8,128)(2,1)S(1)}, bf16[16,64,128]{2,1,0:T(8...) custom-call(s32[256]{0:T(256)S(1)} %bitcast.21, ...), custom_call_target="tpu_custom_call" | custom-call | flops 536870912 | bytes 18874368 | tf_op jit(solution)/shard_map/products/pallas_call | solution.py:58
  227.4 5.0 %collective-permute-start.10 = (bf16[16,64,128]{2,1,0:T(8,128)(2,1)S(1)}, bf16[16,64,128]{2,1,0:T(8,128)(2,1)S(1)}, u32[]{:S(2)}, u32[]{:S(2)}) collective-permute-start(bf16[16,64,128]{2,1,0:T(8,128)(2,1)S(1)} %get-tuple-element.38), channel_id=1, source_target_pairs={{0,128},{32,160},{64,192},{96,224},{128,0},{160,32},{192,64},{224,... | collective-permute-start | bytes 786440 | tf_op jit(solution)/shard_map/ppermute | solution.py:110
  232.3 1.5 collective-permute-start.11
  233.9 2.6 collective-permute-start.12
  236.4 0.0 collective-permute-start.13
  236.5 1.7 collective-permute-start.7
  238.2 6.3 %collective-permute-done.10 = bf16[16,64,128]{2,1,0:T(8,128)(2,1)S(1)} collective-permute-done((bf16[16,64,128]{2,1,0:T(8,128)(2,1)S(1)}, bf16[16,64,128]{2,1,0:T(8,128)(2,1)S(1)}, u32[]{:S(2)}, u32[]{:S(2)}) %collective-permute-start.10) | collective-permute-done | bytes 262176 | tf_op jit(solution)/shard_map/ppermute | solution.py:110
  244.5 6.7 %collective-permute-start.8 = (bf16[16,64,128]{2,1,0:T(8,128)(2,1)S(1)}, bf16[16,64,128]{2,1,0:T(8,128)(2,1)S(1)}, u32[]{:S(2)}, u32[]{:S(2)}) collective-permute-start(bf16[16,64,128]{2,1,0:T(8,128)(2,1)S(1)} %get-tuple-element.36), channel_id=1, source_target_pairs={{0,64},{32,96},{64,128},{96,160},{128,192},{160,224},{192,0},{224,... | collective-permute-start | bytes 786440 | tf_op jit(solution)/shard_map/ppermute | solution.py:110
  251.2 1.5 collective-permute-start.9
  252.7 3.0 collective-permute-done.12
  255.7 7.3 %collective-permute-done.8 = bf16[16,64,128]{2,1,0:T(8,128)(2,1)S(1)} collective-permute-done((bf16[16,64,128]{2,1,0:T(8,128)(2,1)S(1)}, bf16[16,64,128]{2,1,0:T(8,128)(2,1)S(1)}, u32[]{:S(2)}, u32[]{:S(2)}) %collective-permute-start.8) | collective-permute-done | bytes 262176 | tf_op jit(solution)/shard_map/ppermute | solution.py:110
  263.0 1.0 fusion
  264.0 76.0 %all-gather.8.cloned.1.call-done.x_ref = bf16[512,64,128]{2,1,0:T(8,128)(2,1)} async-done(((bf16[16,64,128]{2,1,0:T(8,128)(2,1)}), bf16[512,64,128]{2,1,0:T(8,128)(2,1)}) %all-gather.8.cloned.1.call-update) | async-done | bytes 8388624 | tf_op jit(solution)/shard_map/all_gather | solution.py:106
  340.0 3.4 copy-done.2
  343.4 8.3 %products.5 = (f32[16,64,128]{2,1,0:T(8,128)S(1)}, bf16[16,64,128]{2,1,0:T(8,128)(2,1)S(1)}, bf16[16,64,128]{2,1,0:T(8,128)(2,1)S(1)}, bf16[16,64,128]{2,1,0:T(8...) custom-call(s32[256]{0:T(256)S(1)} %bitcast.22, ...), custom_call_target="tpu_custom_call" | custom-call | flops 536870912 | bytes 18874368 | tf_op jit(solution)/shard_map/products/pallas_call | solution.py:58
  351.7 3.7 collective-permute-start.14
  355.4 1.5 collective-permute-start.15
  356.8 1.0 collective-permute-start.16
  357.9 1.4 collective-permute-start.17
  359.3 2.7 collective-permute-start.18
  361.9 2.7 collective-permute-start.19
  364.6 8.5 %collective-permute-done.15 = bf16[16,64,128]{2,1,0:T(8,128)(2,1)S(1)} collective-permute-done((bf16[16,64,128]{2,1,0:T(8,128)(2,1)S(1)}, bf16[16,64,128]{2,1,0:T(8,128)(2,1)S(1)}, u32[]{:S(2)}, u32[]{:S(2)}) %collective-permute-start.15) | collective-permute-done | bytes 262176 | tf_op jit(solution)/shard_map/ppermute | solution.py:110
  373.1 0.7 copy-done.9
  374.7 7.4 %collective-permute-done.17 = bf16[16,64,128]{2,1,0:T(8,128)(2,1)} collective-permute-done((bf16[16,64,128]{2,1,0:T(8,128)(2,1)S(1)}, bf16[16,64,128]{2,1,0:T(8,128)(2,1)}, u32[]{:S(2)}, u32[]{:S(2)}) %collective-permute-start.17) | collective-permute-done | bytes 262176 | tf_op jit(solution)/shard_map/ppermute | solution.py:110
  382.1 2.9 multiply_add_fusion
  (34 shorter events, 0.1 us)
Async XLA Ops:
  7.2 84.3 %all-gather.4.cloned.1.call-start = ((), (), s32[]{:S(2)}) async-start(), calls=%async_computation | async-start | bytes 8650752 | tf_op jit(solution)/shard_map/all_gather | solution.py:106
  9.0 206.6 %all-gather.6.cloned.1.call-start = ((), (), s32[]{:S(2)}) async-start(), calls=%async_computation.1 | async-start | bytes 8650752 | tf_op jit(solution)/shard_map/all_gather | solution.py:106
  91.5 3.4 copy-start
  94.9 0.7 copy-start.3
  95.5 0.7 copy-start.5
  96.2 38.7 %copy-start.7 = (f32[16,64,128]{2,1,0:T(8,128)S(1)}, f32[16,64,128]{2,1,0:T(8,128)}, u32[]{:S(2)}) copy-start(f32[16,64,128]{2,1,0:T(8,128)} %param.6) | copy-start | bytes 1572868
  96.2 119.4 %copy-start.4 = (s32[1,1,256]{2,1,0:T(1,128)S(1)}, s32[1,1,256]{2,1,0:T(1,128)}, u32[]{:S(2)}) copy-start(s32[1,1,256]{2,1,0:T(1,128)} %param.8) | copy-start | bytes 3076
  96.2 119.4 %copy-start.6 = (s32[1,1,256]{2,1,0:T(1,128)S(1)}, s32[1,1,256]{2,1,0:T(1,128)}, u32[]{:S(2)}) copy-start(s32[1,1,256]{2,1,0:T(1,128)} %param.9) | copy-start | bytes 3076
  104.5 10.3 %collective-permute-start = (bf16[16,64,128]{2,1,0:T(8,128)(2,1)S(1)}, bf16[16,64,128]{2,1,0:T(8,128)(2,1)S(1)}, u32[]{:S(2)}, u32[]{:S(2)}) collective-permute-start(bf16[16,64,128]{2,1,0:T(8,128)(2,1)S(1)} %get-tuple-element.27), channel_id=1, source_target_pairs={{0,32},{32,0},{64,96},{96,64},{128,160},{160,128},{192,224},{224,1... | collective-permute-start | bytes 786440 | tf_op jit(solution)/shard_map/ppermute | solution.py:110
  108.2 17.7 %collective-permute-start.1 = (bf16[16,64,128]{2,1,0:T(8,128)(2,1)S(1)}, bf16[16,64,128]{2,1,0:T(8,128)(2,1)S(1)}, u32[]{:S(2)}, u32[]{:S(2)}) collective-permute-start(bf16[16,64,128]{2,1,0:T(8,128)(2,1)S(1)} %get-tuple-element.28), channel_id=1, source_target_pairs={{0,64},{32,96},{64,128},{96,160},{128,192},{160,224},{192,0},{224,... | collective-permute-start | bytes 786440 | tf_op jit(solution)/shard_map/ppermute | solution.py:110
  109.7 16.2 %collective-permute-start.2 = (bf16[16,64,128]{2,1,0:T(8,128)(2,1)S(1)}, bf16[16,64,128]{2,1,0:T(8,128)(2,1)S(1)}, u32[]{:S(2)}, u32[]{:S(2)}) collective-permute-start(bf16[16,64,128]{2,1,0:T(8,128)(2,1)S(1)} %get-tuple-element.29), channel_id=1, source_target_pairs={{0,96},{32,64},{64,160},{96,128},{128,224},{160,192},{192,32},{224... | collective-permute-start | bytes 786440 | tf_op jit(solution)/shard_map/ppermute | solution.py:110
  110.7 24.1 %collective-permute-start.3 = (bf16[16,64,128]{2,1,0:T(8,128)(2,1)S(1)}, bf16[16,64,128]{2,1,0:T(8,128)(2,1)S(1)}, u32[]{:S(2)}, u32[]{:S(2)}) collective-permute-start(bf16[16,64,128]{2,1,0:T(8,128)(2,1)S(1)} %get-tuple-element.30), channel_id=1, source_target_pairs={{0,128},{32,160},{64,192},{96,224},{128,0},{160,32},{192,64},{224,... | collective-permute-start | bytes 786440 | tf_op jit(solution)/shard_map/ppermute | solution.py:110
  112.1 22.7 %collective-permute-start.4 = (bf16[16,64,128]{2,1,0:T(8,128)(2,1)S(1)}, bf16[16,64,128]{2,1,0:T(8,128)(2,1)S(1)}, u32[]{:S(2)}, u32[]{:S(2)}) collective-permute-start(bf16[16,64,128]{2,1,0:T(8,128)(2,1)S(1)} %get-tuple-element.31), channel_id=1, source_target_pairs={{0,160},{32,128},{64,224},{96,192},{128,32},{160,0},{192,96},{224,... | collective-permute-start | bytes 786440 | tf_op jit(solution)/shard_map/ppermute | solution.py:110
  114.8 20.1 %collective-permute-start.5 = (bf16[16,64,128]{2,1,0:T(8,128)(2,1)S(1)}, bf16[16,64,128]{2,1,0:T(8,128)(2,1)S(1)}, u32[]{:S(2)}, u32[]{:S(2)}) collective-permute-start(bf16[16,64,128]{2,1,0:T(8,128)(2,1)S(1)} %get-tuple-element.32), channel_id=1, source_target_pairs={{0,192},{32,224},{64,0},{96,32},{128,64},{160,96},{192,128},{224,1... | collective-permute-start | bytes 786440 | tf_op jit(solution)/shard_map/ppermute | solution.py:110
  125.9 8.9 %collective-permute-start.6 = (bf16[16,64,128]{2,1,0:T(8,128)(2,1)S(1)}, bf16[16,64,128]{2,1,0:T(8,128)(2,1)S(1)}, u32[]{:S(2)}, u32[]{:S(2)}) collective-permute-start(bf16[16,64,128]{2,1,0:T(8,128)(2,1)S(1)} %get-tuple-element.33), channel_id=1, source_target_pairs={{0,224},{32,192},{64,32},{96,0},{128,96},{160,64},{192,160},{224,1... | collective-permute-start | bytes 786440 | tf_op jit(solution)/shard_map/ppermute | solution.py:110
  136.0 204.0 %all-gather.8.cloned.1.call-start = ((), (), s32[]{:S(2)}) async-start(), calls=%async_computation.2 | async-start | bytes 8650752 | tf_op jit(solution)/shard_map/all_gather | solution.py:106
  215.7 3.4 copy-start.1
  227.4 17.1 %collective-permute-start.10 = (bf16[16,64,128]{2,1,0:T(8,128)(2,1)S(1)}, bf16[16,64,128]{2,1,0:T(8,128)(2,1)S(1)}, u32[]{:S(2)}, u32[]{:S(2)}) collective-permute-start(bf16[16,64,128]{2,1,0:T(8,128)(2,1)S(1)} %get-tuple-element.38), channel_id=1, source_target_pairs={{0,128},{32,160},{64,192},{96,224},{128,0},{160,32},{192,64},{224,... | collective-permute-start | bytes 786440 | tf_op jit(solution)/shard_map/ppermute | solution.py:110
  232.3 18.9 %collective-permute-start.11 = (bf16[16,64,128]{2,1,0:T(8,128)(2,1)S(1)}, bf16[16,64,128]{2,1,0:T(8,128)(2,1)S(1)}, u32[]{:S(2)}, u32[]{:S(2)}) collective-permute-start(bf16[16,64,128]{2,1,0:T(8,128)(2,1)S(1)} %get-tuple-element.39), channel_id=1, source_target_pairs={{0,160},{32,128},{64,224},{96,192},{128,32},{160,0},{192,96},{224,... | collective-permute-start | bytes 786440 | tf_op jit(solution)/shard_map/ppermute | solution.py:110
  233.9 21.8 %collective-permute-start.12 = (bf16[16,64,128]{2,1,0:T(8,128)(2,1)S(1)}, bf16[16,64,128]{2,1,0:T(8,128)(2,1)S(1)}, u32[]{:S(2)}, u32[]{:S(2)}) collective-permute-start(bf16[16,64,128]{2,1,0:T(8,128)(2,1)S(1)} %get-tuple-element.40), channel_id=1, source_target_pairs={{0,192},{32,224},{64,0},{96,32},{128,64},{160,96},{192,128},{224,1... | collective-permute-start | bytes 786440 | tf_op jit(solution)/shard_map/ppermute | solution.py:110
  236.4 19.2 %collective-permute-start.13 = (bf16[16,64,128]{2,1,0:T(8,128)(2,1)S(1)}, bf16[16,64,128]{2,1,0:T(8,128)(2,1)S(1)}, u32[]{:S(2)}, u32[]{:S(2)}) collective-permute-start(bf16[16,64,128]{2,1,0:T(8,128)(2,1)S(1)} %get-tuple-element.41), channel_id=1, source_target_pairs={{0,224},{32,192},{64,32},{96,0},{128,96},{160,64},{192,160},{224,1... | collective-permute-start | bytes 786440 | tf_op jit(solution)/shard_map/ppermute | solution.py:110
  236.5 19.2 %collective-permute-start.7 = (bf16[16,64,128]{2,1,0:T(8,128)(2,1)S(1)}, bf16[16,64,128]{2,1,0:T(8,128)(2,1)S(1)}, u32[]{:S(2)}, u32[]{:S(2)}) collective-permute-start(bf16[16,64,128]{2,1,0:T(8,128)(2,1)S(1)} %get-tuple-element.35), channel_id=1, source_target_pairs={{0,32},{32,0},{64,96},{96,64},{128,160},{160,128},{192,224},{224,1... | collective-permute-start | bytes 786440 | tf_op jit(solution)/shard_map/ppermute | solution.py:110
  244.5 18.5 %collective-permute-start.8 = (bf16[16,64,128]{2,1,0:T(8,128)(2,1)S(1)}, bf16[16,64,128]{2,1,0:T(8,128)(2,1)S(1)}, u32[]{:S(2)}, u32[]{:S(2)}) collective-permute-start(bf16[16,64,128]{2,1,0:T(8,128)(2,1)S(1)} %get-tuple-element.36), channel_id=1, source_target_pairs={{0,64},{32,96},{64,128},{96,160},{128,192},{160,224},{192,0},{224,... | collective-permute-start | bytes 786440 | tf_op jit(solution)/shard_map/ppermute | solution.py:110
  251.2 11.7 %collective-permute-start.9 = (bf16[16,64,128]{2,1,0:T(8,128)(2,1)S(1)}, bf16[16,64,128]{2,1,0:T(8,128)(2,1)S(1)}, u32[]{:S(2)}, u32[]{:S(2)}) collective-permute-start(bf16[16,64,128]{2,1,0:T(8,128)(2,1)S(1)} %get-tuple-element.37), channel_id=1, source_target_pairs={{0,96},{32,64},{64,160},{96,128},{128,224},{160,192},{192,32},{224... | collective-permute-start | bytes 786440 | tf_op jit(solution)/shard_map/ppermute | solution.py:110
  340.0 3.4 copy-start.2
  343.4 31.3 %copy-start.10 = (s32[16,128]{1,0:T(8,128)S(1)}, s32[16,128]{1,0:T(8,128)}, u32[]{:S(2)}) copy-start(s32[16,128]{1,0:T(8,128)} %param.10) | copy-start | bytes 24580
  351.7 10.3 %collective-permute-start.14 = (bf16[16,64,128]{2,1,0:T(8,128)(2,1)S(1)}, bf16[16,64,128]{2,1,0:T(8,128)(2,1)S(1)}, u32[]{:S(2)}, u32[]{:S(2)}) collective-permute-start(bf16[16,64,128]{2,1,0:T(8,128)(2,1)S(1)} %get-tuple-element.43), channel_id=1, source_target_pairs={{0,32},{32,0},{64,96},{96,64},{128,160},{160,128},{192,224},{224,1... | collective-permute-start | bytes 786440 | tf_op jit(solution)/shard_map/ppermute | solution.py:110
  355.4 17.7 %collective-permute-start.15 = (bf16[16,64,128]{2,1,0:T(8,128)(2,1)S(1)}, bf16[16,64,128]{2,1,0:T(8,128)(2,1)S(1)}, u32[]{:S(2)}, u32[]{:S(2)}) collective-permute-start(bf16[16,64,128]{2,1,0:T(8,128)(2,1)S(1)} %get-tuple-element.44), channel_id=1, source_target_pairs={{0,64},{32,96},{64,128},{96,160},{128,192},{160,224},{192,0},{224,... | collective-permute-start | bytes 786440 | tf_op jit(solution)/shard_map/ppermute | solution.py:110
  356.8 17.9 %collective-permute-start.16 = (bf16[16,64,128]{2,1,0:T(8,128)(2,1)S(1)}, bf16[16,64,128]{2,1,0:T(8,128)(2,1)}, u32[]{:S(2)}, u32[]{:S(2)}) collective-permute-start(bf16[16,64,128]{2,1,0:T(8,128)(2,1)S(1)} %get-tuple-element.45), channel_id=1, source_target_pairs={{0,96},{32,64},{64,160},{96,128},{128,224},{160,192},{192,32},{224... | collective-permute-start | bytes 786440 | tf_op jit(solution)/shard_map/ppermute | solution.py:110
  357.9 24.2 %collective-permute-start.17 = (bf16[16,64,128]{2,1,0:T(8,128)(2,1)S(1)}, bf16[16,64,128]{2,1,0:T(8,128)(2,1)}, u32[]{:S(2)}, u32[]{:S(2)}) collective-permute-start(bf16[16,64,128]{2,1,0:T(8,128)(2,1)S(1)} %get-tuple-element.46), channel_id=1, source_target_pairs={{0,128},{32,160},{64,192},{96,224},{128,0},{160,32},{192,64},{224,... | collective-permute-start | bytes 786440 | tf_op jit(solution)/shard_map/ppermute | solution.py:110
  359.3 22.8 %collective-permute-start.18 = (bf16[16,64,128]{2,1,0:T(8,128)(2,1)S(1)}, bf16[16,64,128]{2,1,0:T(8,128)(2,1)}, u32[]{:S(2)}, u32[]{:S(2)}) collective-permute-start(bf16[16,64,128]{2,1,0:T(8,128)(2,1)S(1)} %get-tuple-element.47), channel_id=1, source_target_pairs={{0,160},{32,128},{64,224},{96,192},{128,32},{160,0},{192,96},{224,... | collective-permute-start | bytes 786440 | tf_op jit(solution)/shard_map/ppermute | solution.py:110
  361.9 11.9 %copy-start.8 = (bf16[16,64,128]{2,1,0:T(8,128)(2,1)}, bf16[16,64,128]{2,1,0:T(8,128)(2,1)S(1)}, u32[]{:S(2)}) copy-start(bf16[16,64,128]{2,1,0:T(8,128)(2,1)S(1)} %collective-permute-done.14) | copy-start | bytes 786436
  361.9 20.2 %collective-permute-start.19 = (bf16[16,64,128]{2,1,0:T(8,128)(2,1)S(1)}, bf16[16,64,128]{2,1,0:T(8,128)(2,1)}, u32[]{:S(2)}, u32[]{:S(2)}) collective-permute-start(bf16[16,64,128]{2,1,0:T(8,128)(2,1)S(1)} %get-tuple-element.48), channel_id=1, source_target_pairs={{0,192},{32,224},{64,0},{96,32},{128,64},{160,96},{192,128},{224,1... | collective-permute-start | bytes 786440 | tf_op jit(solution)/shard_map/ppermute | solution.py:110
  373.1 0.7 copy-start.9
  373.8 8.3 %collective-permute-start.20 = (bf16[16,64,128]{2,1,0:T(8,128)(2,1)S(1)}, bf16[16,64,128]{2,1,0:T(8,128)(2,1)}, u32[]{:S(2)}, u32[]{:S(2)}) collective-permute-start(bf16[16,64,128]{2,1,0:T(8,128)(2,1)S(1)} %get-tuple-element.49), channel_id=1, source_target_pairs={{0,224},{32,192},{64,32},{96,0},{128,96},{160,64},{192,160},{224,1... | collective-permute-start | bytes 786440 | tf_op jit(solution)/shard_map/ppermute | solution.py:110
Sparse Core Ops, SparseCore 0:
  11.1 80.3 all-gather.3
  136.1 79.5 all-gather.5
  264.1 75.7 all-gather.7

commit v2 on v1

v2 whole, which is shorter than its diff:
```python
import jax
import jax.numpy as jnp
from jax import lax
from jax.experimental import pallas as pl
from jax.experimental.pallas import tpu as pltpu
from jax.sharding import Mesh, PartitionSpec as P

STEPS = 3
AXES = ("y", "zl", "x", "zh", "core")
SHAPE = (4, 2, 4, 4, 2)
ROW = ("y", "zl")
COL = ("x", "zh", "core")
GROUPS = 8
TURNS = (0, 1, 3, 2)


def poisson_weights(horizon):
    rate_time = horizon[0]
    poisson_term = jnp.exp(-rate_time)
    cumulated = poisson_term
    weights = [(1.0 - cumulated) / rate_time]
    for iteration in range(STEPS):
        poisson_term = poisson_term * rate_time / (iteration + 1.0)
        cumulated = cumulated + poisson_term
        weights.append((1.0 - cumulated) / rate_time)
    return weights


def add_products(step, base, src, dst, x_ref, blk_ref, acc):
    slots = blk_ref.shape[0]
    for slot in range(slots):
        at = step * slots + slot
        vectors = x_ref[src[at] - base]
        into = dst[at]
        acc[into] += jnp.dot(vectors, blk_ref[slot], preferred_element_type=jnp.float32)


def hand_out(place, own_ref, send_ref, acc):
    span = own_ref.shape[0]
    mine = pl.ds(place[0] * span, span)
    own_ref[...] = acc[mine]
    send_ref[...] = acc[...].astype(send_ref.dtype)
    send_ref[mine] = jnp.zeros(own_ref.shape, send_ref.dtype)


def whole_body(src, dst, place, x_ref, blk_ref, own_ref, send_ref, acc):
    step = pl.program_id(0)

    @pl.when(step == 0)
    def _():
        acc[...] = jnp.zeros_like(acc)

    add_products(step, step * x_ref.shape[0], src, dst, x_ref, blk_ref, acc)

    @pl.when(step == pl.num_programs(0) - 1)
    def _():
        hand_out(place, own_ref, send_ref, acc)


def pieces_body(src, dst, place, *refs):
    pieces, (blk_ref, own_ref, send_ref, acc, whole, sems) = refs[:8], refs[8:]
    span = own_ref.shape[0]
    step = pl.program_id(0)

    @pl.when(step == 0)
    def _():
        copies = []
        for core in range(2):
            for at_x in range(4):
                for at_z in range(4):
                    shard = len(copies)
                    copies.append(
                        pltpu.make_async_copy(
                            pieces[core * 4 + at_x].at[pl.ds(at_z * span, span)],
                            whole.at[pl.ds(place[1 + shard] * span, span)],
                            sems.at[shard],
                        )
                    )
        for copy in copies:
            copy.start()
        acc[...] = jnp.zeros_like(acc)
        for copy in copies:
            copy.wait()

    add_products(step, 0, src, dst, whole, blk_ref, acc)

    @pl.when(step == pl.num_programs(0) - 1)
    def _():
        hand_out(place, own_ref, send_ref, acc)


def products(src, dst, place, given, blocks, span):
    n, block_len, _ = blocks.shape
    configs = given[0].shape[1]
    targets = SHAPE[0] * SHAPE[1] * span
    sources = SHAPE[2] * SHAPE[3] * SHAPE[4] * span
    piece = (span, configs, block_len)
    send = (targets, configs, block_len)
    scratch = [pltpu.VMEM(send, jnp.float32)]
    if len(given) == 1:
        body = whole_body
        specs = [pl.BlockSpec((sources // GROUPS, configs, block_len), lambda i, *_: (i, 0, 0))]
    else:
        body = pieces_body
        specs = [pl.BlockSpec(memory_space=pl.ANY)] * len(given)
        scratch += [pltpu.VMEM((sources, configs, block_len), jnp.bfloat16), pltpu.SemaphoreType.DMA((32,))]
    return pl.pallas_call(
        body,
        out_shape=[jax.ShapeDtypeStruct(piece, jnp.float32), jax.ShapeDtypeStruct(send, jnp.bfloat16)],
        grid_spec=pltpu.PrefetchScalarGridSpec(
            num_scalar_prefetch=3,
            grid=(GROUPS,),
            in_specs=specs + [pl.BlockSpec((n // GROUPS, block_len, block_len), lambda i, *_: (i, 0, 0))],
            out_specs=[pl.BlockSpec(piece, lambda i, *_: (0, 0, 0)), pl.BlockSpec(send, lambda i, *_: (0, 0, 0))],
            scratch_shapes=scratch,
        ),
        compiler_params=pltpu.CompilerParams(vmem_limit_bytes=32 << 20),
        cost_estimate=pl.CostEstimate(
            flops=2 * n * configs * block_len * block_len,
            bytes_accessed=2 * (sources * configs * block_len + blocks.size + targets * configs * block_len),
            transcendentals=0,
        ),
        name="products",
    )(src, dst, place, *given, blocks)


def turn(value, axis, by):
    n = lax.axis_size(axis)
    return lax.ppermute(value, axis, [(i, (i + by) % n) for i in range(n)])


def after(value, *others):
    return lax.optimization_barrier((value, *others))[0]


def spread_z(mine):
    return [turn(mine, "zh", by) for by in TURNS[1:]]


def spread_x(mine, from_z):
    column = jnp.concatenate([mine, *from_z], axis=0)
    return [column] + [turn(column, "x", by) for by in TURNS[1:]]


def reduce_rows(own, send):
    got = lax.all_to_all(send, ROW, 0, 0, tiled=True)
    got = got.reshape(SHAPE[0] * SHAPE[1], *own.shape).astype(jnp.float32)
    return own + jnp.sum(got, axis=0)


def shards(x_init, gen_blocks, blk_src, blk_dst, reward, horizon):
    blocks = gen_blocks[0, 0]
    src = blk_src[0, 0]
    dst = blk_dst[0, 0]
    span = x_init.shape[0]
    half = x_init.shape[1] // 2
    weights = poisson_weights(horizon)
    reward_f = reward.astype(jnp.float32)[:, None, :]
    x, zh, core = (lax.axis_index(a) for a in COL)
    row = lax.axis_index("y") * SHAPE[1] + lax.axis_index("zl")
    place = [row]
    for other in range(2):
        for by_x in TURNS:
            for by_z in TURNS:
                place.append((((x - by_x) % 4) * 4 + (zh - by_z) % 4) * 2 + (core + other) % 2)
    place = jnp.stack(place).astype(jnp.int32)
    state_a, state_b = x_init[:, :half], x_init[:, half:]
    sum_a = weights[0] * reward_f * state_a
    sum_b = weights[0] * reward_f * state_b
    for iteration in range(STEPS):
        low_a = state_a.astype(jnp.bfloat16)
        low_b = state_b.astype(jnp.bfloat16)
        whole = lax.all_gather(low_a, COL, axis=0, tiled=True)
        near = spread_x(low_b, spread_z(low_b))
        far = [turn(piece, "core", 1) for piece in near]
        state_b = state_b + reduce_rows(*products(src, dst, place, near + far, blocks, span))
        state_a = state_a + reduce_rows(*products(src, dst, place, [whole], blocks, span))
        sum_a = sum_a + weights[iteration + 1] * reward_f * state_a
        sum_b = sum_b + weights[iteration + 1] * reward_f * state_b
    return (
        jnp.concatenate([state_a, state_b], axis=1),
        jnp.concatenate([sum_a, sum_b], axis=1),
    )


def solution(mesh):
    fine = Mesh(mesh.devices.reshape(SHAPE), AXES)
    rc = P((*ROW, *COL), None, None)
    in_specs = (
        rc,
        P(ROW, COL, None, None, None),
        P(ROW, COL, None),
        P(ROW, COL, None),
        P((*ROW, *COL), None),
        P(),
    )
    return jax.shard_map(shards, mesh=fine, in_specs=in_specs, out_specs=(rc, rc), check_vma=False)
```

time: 394 us -> 396 us (level)
  waiting for transfers between devices: 288 us -> 144 us
  starting transfers between devices: 45.1 us -> 114 us
  blocking collectives: 0 us -> 40.9 us
  Pallas kernels: 24.9 us -> 47.2 us
  local copies, waits for them, and re-layouts: 12.3 us -> 25.5 us
    all_gather x3, waiting for transfers between devices: 238 us -> 57.1 us  [shards(): whole = lax.all_gather(low_a, COL, axis=0, tiled=True)]
    ppermute x21 -> x30, starting transfers between devices: 44.9 us -> 89.2 us  [turn(): return lax.ppermute(value, axis, [(i, (i + by) % n) for i in range(n)])]
    all_to_all x0 -> x2, blocking collectives: none -> 40.9 us  [reduce_rows(): got = lax.all_to_all(send, ROW, 0, 0, tiled=True)]
    all_to_all x0 -> x4, waiting for transfers between devices: none -> 34.8 us  [reduce_rows(): got = lax.all_to_all(send, ROW, 0, 0, tiled=True)]
    all_to_all x0 -> x4, starting transfers between devices: none -> 24.7 us  [reduce_rows(): got = lax.all_to_all(send, ROW, 0, 0, tiled=True)]
    pallas_call x3 -> x6, Pallas kernels: 24.9 us -> 47.2 us  [products(): pl.pallas_call(body, out_shape=[jax.ShapeDtypeStruct(piece, jnp.float32),...]
    unnamed x22 -> x30, local copies, waits for them, and re-layouts: 12.2 us -> 23.7 us
    ppermute x21 -> x30, waiting for transfers between devices: 49.8 us -> 52.4 us  [turn(): return lax.ppermute(value, axis, [(i, (i + by) % n) for i in range(n)])]
  transfers between devices with their start and end apart: 24 -> 37, of which waited for: 10 -> 20; matrix products, arithmetic and copies ran while one was open for 0% -> 1% of each run, Pallas kernels for 0% -> 11%
where the time goes in v2:
time: 396 us; the launch traced here: 394 us
  waiting for transfers between devices  144 us (36%)
  starting transfers between devices  114 us (29%)
  Pallas kernels  47.2 us (12%)
  blocking collectives  40.9 us (10%)
  local copies, waits for them, and re-layouts  25.5 us (6%)
  between operations  14.8 us (4%)
  other arithmetic  6.8 us (2%)
    ppermute x30, starting transfers between devices, turn(): return lax.ppermute(value, axis, [(i, (i + by) % n) for i in range(n)])  89.2 us
    all_gather x3, waiting for transfers between devices, shards(): whole = lax.all_gather(low_a, COL, axis=0, tiled=True)  57.1 us
    ppermute x30, waiting for transfers between devices, turn(): return lax.ppermute(value, axis, [(i, (i + by) % n) for i in range(n)])  52.4 us
    pallas_call x6, Pallas kernels, products(): pl.pallas_call(body, out_shape=[jax.ShapeDtypeStruct(piece, jnp.float32),...  47.2 us
    all_to_all x2, blocking collectives, reduce_rows(): got = lax.all_to_all(send, ROW, 0, 0, tiled=True)  40.9 us
    all_to_all x4, waiting for transfers between devices, reduce_rows(): got = lax.all_to_all(send, ROW, 0, 0, tiled=True)  34.8 us
    all_to_all x4, starting transfers between devices, reduce_rows(): got = lax.all_to_all(send, ROW, 0, 0, tiled=True)  24.7 us
    unnamed x30, local copies, waits for them, and re-layouts  23.7 us
  transfers between devices with their start and end apart: 37, of which 20 were waited for; matrix products, arithmetic and copies ran while one was open for 1% of the time, Pallas kernels for 11%

profile of v2, /device:TPU:1, one launch (start us, length us, event | category | flops | bytes accessed | tf_op | source)
XLA Modules:
  0.0 393.8 jit_solution(11656907968069966736)
XLA Ops:
  9.0 3.9 collective-permute-start
  12.9 3.1 collective-permute-start.1
  16.0 4.4 %collective-permute-start.2 = (bf16[16,32,128]{2,1,0:T(8,128)(2,1)S(1)}, bf16[16,32,128]{2,1,0:T(8,128)(2,1)S(1)}, u32[]{:S(2)}, u32[]{:S(2)}) collective-permute-start(bf16[16,32,128]{2,1,0:T(8,128)(2,1)S(1)} %get-tuple-element.43), channel_id=1, source_target_pairs={{0,4},{2,6},{4,0},{6,2},{1,5},{3,7},{5,1},{7,3},{8,12},{10,14},{12... | collective-permute-start | bytes 393224 | tf_op jit(solution)/shard_map/ppermute | solution.py:129
  20.4 6.1 %collective-permute-done.1 = bf16[16,32,128]{2,1,0:T(8,128)(2,1)S(1)} collective-permute-done((bf16[16,32,128]{2,1,0:T(8,128)(2,1)S(1)}, bf16[16,32,128]{2,1,0:T(8,128)(2,1)S(1)}, u32[]{:S(2)}, u32[]{:S(2)}) %collective-permute-start.1) | collective-permute-done | bytes 131104 | tf_op jit(solution)/shard_map/ppermute | solution.py:129
  34.4 9.4 %collective-permute-done.3.refs_1_ = bf16[64,32,128]{2,1,0:T(8,128)(2,1)S(1)} collective-permute-done((bf16[64,32,128]{2,1,0:T(8,128)(2,1)S(1)}, bf16[64,32,128]{2,1,0:T(8,128)(2,1)S(1)}, u32[]{:S(2)}, u32[]{:S(2)}) %collective-permute-start.3) | collective-permute-done | bytes 524320 | tf_op jit(solution)/shard_map/ppermute | solution.py:129
  45.7 7.8 %collective-permute-start.8 = (bf16[64,32,128]{2,1,0:T(8,128)(2,1)S(1)}, bf16[64,32,128]{2,1,0:T(8,128)(2,1)}, u32[]{:S(2)}, u32[]{:S(2)}) collective-permute-start(bf16[64,32,128]{2,1,0:T(8,128)(2,1)S(1)} %collective-permute-done.4.refs_2_), channel_id=1, source_target_pairs={{0,1},{1,0},{2,3},{3,2},{4,5},{5,4},{6,7},{7,6},{8,9},{9,8},{10,11... | collective-permute-start | bytes 1572872 | tf_op jit(solution)/shard_map/ppermute | solution.py:129
  53.5 3.2 collective-permute-done.5.refs_3_
  56.7 3.8 collective-permute-start.9
  62.1 3.5 copy-done
  65.6 11.0 %products.9 = (f32[16,32,128]{2,1,0:T(8,128)S(1)}, bf16[128,32,128]{2,1,0:T(8,128)(2,1)}) custom-call(s32[256]{0:T(256)S(1)} %bitcast.63, s32[256]{0:T(256)S(1)} %bitcast.69, s32[33]{0:T(128)S(1)} %stack.135.place, bf16[64,32,128]{2,1,0:T(8,128)(2,1)S(1)} %pad_maximum_fusion.refs_0_, bf16[64,32,128]{2,1,0:T(8,128)(2,1)S(1)} %collective-permute-done.3.refs_1_, ...), custom_call_target="tpu_custom_call" | custom-call | flops 268435456 | bytes 13631488 | tf_op jit(solution)/shard_map/products/pallas_call | solution.py:107
  76.6 9.1 %all-to-all-start.3 = ((bf16[128,32,128]{2,1,0:T(8,128)(2,1)}), bf16[128,32,128]{2,1,0:T(8,128)(2,1)S(1)}, u32[]{:S(2)}, u32[]{:S(2)}) async-start(bf16[128,32,128]{2,1,0:T(8,128)(2,1)} %get-tuple-element.21), calls=%async_computation.3 | async-start | bytes 2097152 | tf_op jit(solution)/shard_map/all_to_all | solution.py:146
  85.7 3.4 copy-done.1
  91.3 5.1 %products.6 = (f32[16,32,128]{2,1,0:T(8,128)S(1)}, bf16[128,32,128]{2,1,0:T(8,128)(2,1)}) custom-call(s32[256]{0:T(256)S(1)} %bitcast.64, s32[256]{0:T(256)S(1)} %bitcast.70, s32[33]{0:T(128)S(1)} %stack.135.place, bf16[512,32,128]{2,1,0:T(8,128)(2,1)S(1)} %copy-done.5, bf16[256,128,128]{2,1,0:T(8,128)(2,1)S(1)} %bitcast.58), custom_call_target="tpu_custom_call" | custom-call | flops 268435456 | bytes 13631488 | tf_op jit(solution)/shard_map/products/pallas_call | solution.py:107
  96.3 4.5 %all-to-all-done.3 = bf16[128,32,128]{2,1,0:T(8,128)(2,1)S(1)} async-done(((bf16[128,32,128]{2,1,0:T(8,128)(2,1)}), bf16[128,32,128]{2,1,0:T(8,128)(2,1)S(1)}, u32[]{:S(2)}, u32[]{:S(2)}) %all-to-all-start.3) | async-done | bytes 1048608 | tf_op jit(solution)/shard_map/all_to_all | solution.py:146
  100.8 3.7 all-to-all-start
  104.7 13.7 %all-to-all-done = bf16[128,32,128]{2,1,0:T(8,128)(2,1)S(1)} async-done(((bf16[128,32,128]{2,1,0:T(8,128)(2,1)}), bf16[128,32,128]{2,1,0:T(8,128)(2,1)S(1)}, u32[]{:S(2)}, u32[]{:S(2)}) %all-to-all-start) | async-done | bytes 1048608 | tf_op jit(solution)/shard_map/all_to_all | solution.py:146
  119.5 57.1 %all-gather.6.cloned.1.call-done.x_ref = bf16[512,32,128]{2,1,0:T(8,128)(2,1)} async-done(((bf16[16,32,128]{2,1,0:T(8,128)(2,1)}), bf16[512,32,128]{2,1,0:T(8,128)(2,1)}) %all-gather.6.cloned.1.call-update) | async-done | bytes 4194320 | tf_op jit(solution)/shard_map/all_gather | solution.py:173
  176.6 3.4 copy-done.2
  182.2 4.1 %products.7 = (f32[16,32,128]{2,1,0:T(8,128)S(1)}, bf16[128,32,128]{2,1,0:T(8,128)(2,1)S(1)}) custom-call(s32[256]{0:T(256)S(1)} %bitcast.65, s32[256]{0:T(256)S(1)} %bitcast.71, s32[33]{0:T(128)S(1)} %stack.135.place, bf16[512,32,128]{2,1,0:T(8,128)(2,1)S(1)} %copy-done.7, bf16[256,128,128]{2,1,0:T(8,128)(2,1)S(1)} %bitcast.59), custom_call_target="tpu_custom_call" | custom-call | flops 268435456 | bytes 13631488 | tf_op jit(solution)/shard_map/products/pallas_call | solution.py:107
  186.2 18.7 %all_to_all.30 = bf16[128,32,128]{2,1,0:T(8,128)(2,1)S(1)} all-to-all(bf16[128,32,128]{2,1,0:T(8,128)(2,1)S(1)} %get-tuple-element.17), channel_id=1, replica_groups=mesh['y'=4,'zl'=2,'x'=4,'zh'=4,'core'=2] {'y','zl'}, dimensions={0} | all-to-all | bytes 2097152 | tf_op jit(solution)/shard_map/all_to_all | solution.py:146
  209.6 3.0 collective-permute-start.12
  212.6 2.9 collective-permute-done.11
  215.5 4.4 %collective-permute-done.12 = bf16[16,32,128]{2,1,0:T(8,128)(2,1)S(1)} collective-permute-done((bf16[16,32,128]{2,1,0:T(8,128)(2,1)S(1)}, bf16[16,32,128]{2,1,0:T(8,128)(2,1)S(1)}, u32[]{:S(2)}, u32[]{:S(2)}) %collective-permute-start.12) | collective-permute-done | bytes 131104 | tf_op jit(solution)/shard_map/ppermute | solution.py:129
  223.7 3.2 collective-permute-start.16
  226.8 7.2 %collective-permute-done.13.refs_1_ = bf16[64,32,128]{2,1,0:T(8,128)(2,1)S(1)} collective-permute-done((bf16[64,32,128]{2,1,0:T(8,128)(2,1)S(1)}, bf16[64,32,128]{2,1,0:T(8,128)(2,1)S(1)}, u32[]{:S(2)}, u32[]{:S(2)}) %collective-permute-start.13) | collective-permute-done | bytes 524320 | tf_op jit(solution)/shard_map/ppermute | solution.py:129
  234.1 5.1 %collective-permute-start.17 = (bf16[64,32,128]{2,1,0:T(8,128)(2,1)S(1)}, bf16[64,32,128]{2,1,0:T(8,128)(2,1)S(1)}, u32[]{:S(2)}, u32[]{:S(2)}) collective-permute-start(bf16[64,32,128]{2,1,0:T(8,128)(2,1)S(1)} %collective-permute-done.13.refs_1_), channel_id=1, source_target_pairs={{0,1},{1,0},{2,3},{3,2},{4,5},{5,4},{6,7},{7,6},{8,9},{9,8},{10,11... | collective-permute-start | bytes 1572872 | tf_op jit(solution)/shard_map/ppermute | solution.py:129
  239.2 6.3 %collective-permute-start.18 = (bf16[64,32,128]{2,1,0:T(8,128)(2,1)S(1)}, bf16[64,32,128]{2,1,0:T(8,128)(2,1)S(1)}, u32[]{:S(2)}, u32[]{:S(2)}) collective-permute-start(bf16[64,32,128]{2,1,0:T(8,128)(2,1)S(1)} %collective-permute-done.14.refs_2_), channel_id=1, source_target_pairs={{0,1},{1,0},{2,3},{3,2},{4,5},{5,4},{6,7},{7,6},{8,9},{9,8},{10,11... | collective-permute-start | bytes 1572872 | tf_op jit(solution)/shard_map/ppermute | solution.py:129
  246.6 4.9 %collective-permute-start.19 = (bf16[64,32,128]{2,1,0:T(8,128)(2,1)S(1)}, bf16[64,32,128]{2,1,0:T(8,128)(2,1)S(1)}, u32[]{:S(2)}, u32[]{:S(2)}) collective-permute-start(bf16[64,32,128]{2,1,0:T(8,128)(2,1)S(1)} %collective-permute-done.15.refs_3_), channel_id=1, source_target_pairs={{0,1},{1,0},{2,3},{3,2},{4,5},{5,4},{6,7},{7,6},{8,9},{9,8},{10,11... | collective-permute-start | bytes 1572872 | tf_op jit(solution)/shard_map/ppermute | solution.py:129
  253.1 3.5 copy-done.3
  256.6 10.5 %products.10 = (f32[16,32,128]{2,1,0:T(8,128)S(1)}, bf16[128,32,128]{2,1,0:T(8,128)(2,1)S(1)}) custom-call(s32[256]{0:T(256)S(1)} %bitcast.66, s32[256]{0:T(256)S(1)} %bitcast.72, s32[33]{0:T(128)S(1)} %stack.135.place, bf16[64,32,128]{2,1,0:T(8,128)(2,1)S(1)} %pad_maximum_fusion.1.refs_0_, bf16[64,32,128]{2,1,0:T(8,128)(2,1)S(1)} %collective-permute-done.13.refs_1_, ...), custom_call_target="tpu_custom_call" | custom-call | flops 268435456 | bytes 13631488 | tf_op jit(solution)/shard_map/products/pallas_call | solution.py:107
  267.1 22.2 %all_to_all.31 = bf16[128,32,128]{2,1,0:T(8,128)(2,1)S(1)} all-to-all(bf16[128,32,128]{2,1,0:T(8,128)(2,1)S(1)} %get-tuple-element.23), channel_id=1, replica_groups=mesh['y'=4,'zl'=2,'x'=4,'zh'=4,'core'=2] {'y','zl'}, dimensions={0} | all-to-all | bytes 2097152 | tf_op jit(solution)/shard_map/all_to_all | solution.py:146
  290.5 3.3 collective-permute-start.21
  293.8 3.5 collective-permute-start.22
  299.4 3.2 collective-permute-done.22
  302.6 2.8 collective-permute-start.23
  307.3 3.2 collective-permute-start.26
  310.6 3.4 collective-permute-done.23.refs_1_
  314.0 7.1 %collective-permute-start.27 = (bf16[64,32,128]{2,1,0:T(8,128)(2,1)S(1)}, bf16[64,32,128]{2,1,0:T(8,128)(2,1)S(1)}, u32[]{:S(2)}, u32[]{:S(2)}) collective-permute-start(bf16[64,32,128]{2,1,0:T(8,128)(2,1)S(1)} %collective-permute-done.23.refs_1_), channel_id=1, source_target_pairs={{0,1},{1,0},{2,3},{3,2},{4,5},{5,4},{6,7},{7,6},{8,9},{9,8},{10,11... | collective-permute-start | bytes 1572872 | tf_op jit(solution)/shard_map/ppermute | solution.py:129
  321.0 2.2 collective-permute-start.28
  323.3 3.0 collective-permute-done.25.refs_3_
  326.3 4.1 %collective-permute-start.29 = (bf16[64,32,128]{2,1,0:T(8,128)(2,1)S(1)}, bf16[64,32,128]{2,1,0:T(8,128)(2,1)S(1)}, u32[]{:S(2)}, u32[]{:S(2)}) collective-permute-start(bf16[64,32,128]{2,1,0:T(8,128)(2,1)S(1)} %collective-permute-done.25.refs_3_), channel_id=1, source_target_pairs={{0,1},{1,0},{2,3},{3,2},{4,5},{5,4},{6,7},{7,6},{8,9},{9,8},{10,11... | collective-permute-start | bytes 1572872 | tf_op jit(solution)/shard_map/ppermute | solution.py:129
  331.9 11.5 %products.11 = (f32[16,32,128]{2,1,0:T(8,128)S(1)}, bf16[128,32,128]{2,1,0:T(8,128)(2,1)}) custom-call(s32[256]{0:T(256)S(1)} %bitcast.67, s32[256]{0:T(256)S(1)} %bitcast.73, s32[33]{0:T(128)S(1)} %stack.135.place, bf16[64,32,128]{2,1,0:T(8,128)(2,1)S(1)} %pad_maximum_fusion.2.refs_0_, bf16[64,32,128]{2,1,0:T(8,128)(2,1)S(1)} %collective-permute-done.23.refs_1_, ...), custom_call_target="tpu_custom_call" | custom-call | flops 268435456 | bytes 13631488 | tf_op jit(solution)/shard_map/products/pallas_call | solution.py:107
  343.5 8.3 %all-to-all-start.5 = ((bf16[128,32,128]{2,1,0:T(8,128)(2,1)}), bf16[128,32,128]{2,1,0:T(8,128)(2,1)S(1)}, u32[]{:S(2)}, u32[]{:S(2)}) async-start(bf16[128,32,128]{2,1,0:T(8,128)(2,1)} %get-tuple-element.25), calls=%async_computation.5 | async-start | bytes 2097152 | tf_op jit(solution)/shard_map/all_to_all | solution.py:146
  351.8 3.4 copy-done.4
  357.3 5.1 %products.8 = (f32[16,32,128]{2,1,0:T(8,128)S(1)}, bf16[128,32,128]{2,1,0:T(8,128)(2,1)}) custom-call(s32[256]{0:T(256)S(1)} %bitcast.68, s32[256]{0:T(256)S(1)} %bitcast.74, s32[33]{0:T(128)S(1)} %stack.135.place, bf16[512,32,128]{2,1,0:T(8,128)(2,1)S(1)} %copy-done.6, bf16[256,128,128]{2,1,0:T(8,128)(2,1)S(1)} %bitcast.62), custom_call_target="tpu_custom_call" | custom-call | flops 268435456 | bytes 13631488 | tf_op jit(solution)/shard_map/products/pallas_call | solution.py:107
  362.4 4.5 %all-to-all-done.5 = bf16[128,32,128]{2,1,0:T(8,128)(2,1)S(1)} async-done(((bf16[128,32,128]{2,1,0:T(8,128)(2,1)}), bf16[128,32,128]{2,1,0:T(8,128)(2,1)S(1)}, u32[]{:S(2)}, u32[]{:S(2)}) %all-to-all-start.5) | async-done | bytes 1048608 | tf_op jit(solution)/shard_map/all_to_all | solution.py:146
  366.9 3.7 all-to-all-start.2
  372.3 12.1 %all-to-all-done.2 = bf16[128,32,128]{2,1,0:T(8,128)(2,1)S(1)} async-done(((bf16[128,32,128]{2,1,0:T(8,128)(2,1)}), bf16[128,32,128]{2,1,0:T(8,128)(2,1)S(1)}, u32[]{:S(2)}, u32[]{:S(2)}) %all-to-all-start.2) | async-done | bytes 1048608 | tf_op jit(solution)/shard_map/all_to_all | solution.py:146
  (84 shorter events, 42.3 us)
Async XLA Ops:
  7.2 55.0 %copy-start.8 = (s32[1,1,256]{2,1,0:T(1,128)S(1)}, s32[1,1,256]{2,1,0:T(1,128)}, u32[]{:S(2)}) copy-start(s32[1,1,256]{2,1,0:T(1,128)} %param.8) | copy-start | bytes 3076
  7.2 54.9 %copy-start.9 = (s32[1,1,256]{2,1,0:T(1,128)S(1)}, s32[1,1,256]{2,1,0:T(1,128)}, u32[]{:S(2)}) copy-start(s32[1,1,256]{2,1,0:T(1,128)} %param.9) | copy-start | bytes 3076
  7.2 78.5 %all-gather.4.cloned.1.call-start = ((), (), s32[]{:S(2)}) async-start(), calls=%async_computation.6 | async-start | bytes 4325376 | tf_op jit(solution)/shard_map/all_gather | solution.py:173
  9.0 11.4 %collective-permute-start = (bf16[16,32,128]{2,1,0:T(8,128)(2,1)S(1)}, bf16[16,32,128]{2,1,0:T(8,128)(2,1)S(1)}, u32[]{:S(2)}, u32[]{:S(2)}) collective-permute-start(bf16[16,32,128]{2,1,0:T(8,128)(2,1)S(1)} %get-tuple-element.43), channel_id=1, source_target_pairs={{0,2},{2,4},{4,6},{6,0},{1,3},{3,5},{5,7},{7,1},{8,10},{10,12},{12... | collective-permute-start | bytes 393224 | tf_op jit(solution)/shard_map/ppermute | solution.py:129
  12.9 13.6 %collective-permute-start.1 = (bf16[16,32,128]{2,1,0:T(8,128)(2,1)S(1)}, bf16[16,32,128]{2,1,0:T(8,128)(2,1)S(1)}, u32[]{:S(2)}, u32[]{:S(2)}) collective-permute-start(bf16[16,32,128]{2,1,0:T(8,128)(2,1)S(1)} %get-tuple-element.43), channel_id=1, source_target_pairs={{0,6},{2,0},{4,2},{6,4},{1,7},{3,1},{5,3},{7,5},{8,14},{10,8},{12,... | collective-permute-start | bytes 393224 | tf_op jit(solution)/shard_map/ppermute | solution.py:129
  16.0 12.3 %collective-permute-start.2 = (bf16[16,32,128]{2,1,0:T(8,128)(2,1)S(1)}, bf16[16,32,128]{2,1,0:T(8,128)(2,1)S(1)}, u32[]{:S(2)}, u32[]{:S(2)}) collective-permute-start(bf16[16,32,128]{2,1,0:T(8,128)(2,1)S(1)} %get-tuple-element.43), channel_id=1, source_target_pairs={{0,4},{2,6},{4,0},{6,2},{1,5},{3,7},{5,1},{7,3},{8,12},{10,14},{12... | collective-permute-start | bytes 393224 | tf_op jit(solution)/shard_map/ppermute | solution.py:129
  28.4 15.4 %collective-permute-start.3 = (bf16[64,32,128]{2,1,0:T(8,128)(2,1)S(1)}, bf16[64,32,128]{2,1,0:T(8,128)(2,1)S(1)}, u32[]{:S(2)}, u32[]{:S(2)}) collective-permute-start(bf16[64,32,128]{2,1,0:T(8,128)(2,1)S(1)} %pad_maximum_fusion.refs_0_), channel_id=1, source_target_pairs={{0,8},{8,16},{16,24},{24,0},{1,9},{9,17},{17,25},{25,1},{2,10},{10... | collective-permute-start | bytes 1572872 | tf_op jit(solution)/shard_map/ppermute | solution.py:129
  29.7 16.0 %collective-permute-start.4 = (bf16[64,32,128]{2,1,0:T(8,128)(2,1)S(1)}, bf16[64,32,128]{2,1,0:T(8,128)(2,1)S(1)}, u32[]{:S(2)}, u32[]{:S(2)}) collective-permute-start(bf16[64,32,128]{2,1,0:T(8,128)(2,1)S(1)} %pad_maximum_fusion.refs_0_), channel_id=1, source_target_pairs={{0,24},{8,0},{16,8},{24,16},{1,25},{9,1},{17,9},{25,17},{2,26},{10... | collective-permute-start | bytes 1572872 | tf_op jit(solution)/shard_map/ppermute | solution.py:129
  31.1 25.5 %collective-permute-start.5 = (bf16[64,32,128]{2,1,0:T(8,128)(2,1)S(1)}, bf16[64,32,128]{2,1,0:T(8,128)(2,1)S(1)}, u32[]{:S(2)}, u32[]{:S(2)}) collective-permute-start(bf16[64,32,128]{2,1,0:T(8,128)(2,1)S(1)} %pad_maximum_fusion.refs_0_), channel_id=1, source_target_pairs={{0,16},{8,24},{16,0},{24,8},{1,17},{9,25},{17,1},{25,9},{2,18},{10... | collective-permute-start | bytes 1572872 | tf_op jit(solution)/shard_map/ppermute | solution.py:129
  32.7 27.9 %collective-permute-start.6 = (bf16[64,32,128]{2,1,0:T(8,128)(2,1)S(1)}, bf16[64,32,128]{2,1,0:T(8,128)(2,1)S(1)}, u32[]{:S(2)}, u32[]{:S(2)}) collective-permute-start(bf16[64,32,128]{2,1,0:T(8,128)(2,1)S(1)} %pad_maximum_fusion.refs_0_), channel_id=1, source_target_pairs={{0,1},{1,0},{2,3},{3,2},{4,5},{5,4},{6,7},{7,6},{8,9},{9,8},{10,11... | collective-permute-start | bytes 1572872 | tf_op jit(solution)/shard_map/ppermute | solution.py:129
  43.8 16.8 %collective-permute-start.7 = (bf16[64,32,128]{2,1,0:T(8,128)(2,1)S(1)}, bf16[64,32,128]{2,1,0:T(8,128)(2,1)S(1)}, u32[]{:S(2)}, u32[]{:S(2)}) collective-permute-start(bf16[64,32,128]{2,1,0:T(8,128)(2,1)S(1)} %collective-permute-done.3.refs_1_), channel_id=1, source_target_pairs={{0,1},{1,0},{2,3},{3,2},{4,5},{5,4},{6,7},{7,6},{8,9},{9,8},{10,11... | collective-permute-start | bytes 1572872 | tf_op jit(solution)/shard_map/ppermute | solution.py:129
  45.7 14.9 %collective-permute-start.8 = (bf16[64,32,128]{2,1,0:T(8,128)(2,1)S(1)}, bf16[64,32,128]{2,1,0:T(8,128)(2,1)}, u32[]{:S(2)}, u32[]{:S(2)}) collective-permute-start(bf16[64,32,128]{2,1,0:T(8,128)(2,1)S(1)} %collective-permute-done.4.refs_2_), channel_id=1, source_target_pairs={{0,1},{1,0},{2,3},{3,2},{4,5},{5,4},{6,7},{7,6},{8,9},{9,8},{10,11... | collective-permute-start | bytes 1572872 | tf_op jit(solution)/shard_map/ppermute | solution.py:129
  56.7 5.5 %collective-permute-start.9 = (bf16[64,32,128]{2,1,0:T(8,128)(2,1)S(1)}, bf16[64,32,128]{2,1,0:T(8,128)(2,1)}, u32[]{:S(2)}, u32[]{:S(2)}) collective-permute-start(bf16[64,32,128]{2,1,0:T(8,128)(2,1)S(1)} %collective-permute-done.5.refs_3_), channel_id=1, source_target_pairs={{0,1},{1,0},{2,3},{3,2},{4,5},{5,4},{6,7},{7,6},{8,9},{9,8},{10,11... | collective-permute-start | bytes 1572872 | tf_op jit(solution)/shard_map/ppermute | solution.py:129
  62.1 3.5 copy-start
  76.6 24.2 %all-to-all-start.3 = ((bf16[128,32,128]{2,1,0:T(8,128)(2,1)}), bf16[128,32,128]{2,1,0:T(8,128)(2,1)S(1)}, u32[]{:S(2)}, u32[]{:S(2)}) async-start(bf16[128,32,128]{2,1,0:T(8,128)(2,1)} %get-tuple-element.21), calls=%async_computation.3 | async-start | bytes 2097152 | tf_op jit(solution)/shard_map/all_to_all | solution.py:146
  85.7 3.4 copy-start.1
  100.8 17.8 %copy-start.10 = (f32[16,64,128]{2,1,0:T(8,128)S(1)}, f32[16,64,128]{2,1,0:T(8,128)}, u32[]{:S(2)}) copy-start(f32[16,64,128]{2,1,0:T(8,128)} %param.6) | copy-start | bytes 1572868
  100.8 17.6 %all-to-all-start = ((bf16[128,32,128]{2,1,0:T(8,128)(2,1)}), bf16[128,32,128]{2,1,0:T(8,128)(2,1)S(1)}, u32[]{:S(2)}, u32[]{:S(2)}) async-start(bf16[128,32,128]{2,1,0:T(8,128)(2,1)} %get-tuple-element.15), calls=%async_computation | async-start | bytes 2097152 | tf_op jit(solution)/shard_map/all_to_all | solution.py:146
  104.5 72.1 %all-gather.6.cloned.1.call-start = ((), (), s32[]{:S(2)}) async-start(), calls=%async_computation.7 | async-start | bytes 4325376 | tf_op jit(solution)/shard_map/all_gather | solution.py:173
  119.4 85.7 %copy-start.11 = (f32[16,32,128]{2,1,0:T(8,128)}, f32[16,32,128]{2,1,0:T(8,128)S(1)}, u32[]{:S(2)}) copy-start(f32[16,32,128]{2,1,0:T(8,128)S(1)} %get-tuple-element.33) | copy-start | bytes 786436
  119.4 170.1 %copy-start.13 = (f32[16,32,128]{2,1,0:T(8,128)}, f32[16,32,128]{2,1,0:T(8,128)S(1)}, u32[]{:S(2)}) copy-start(f32[16,32,128]{2,1,0:T(8,128)S(1)} %get-tuple-element.41) | copy-start | bytes 786436
  119.4 232.3 %all-gather.8.cloned.1.call-start = ((), (), s32[]{:S(2)}) async-start(), calls=%async_computation.8 | async-start | bytes 4325376 | tf_op jit(solution)/shard_map/all_gather | solution.py:173
  205.9 6.6 %collective-permute-start.10 = (bf16[16,32,128]{2,1,0:T(8,128)(2,1)S(1)}, bf16[16,32,128]{2,1,0:T(8,128)(2,1)S(1)}, u32[]{:S(2)}, u32[]{:S(2)}) collective-permute-start(bf16[16,32,128]{2,1,0:T(8,128)(2,1)S(1)} %get-tuple-element.40), channel_id=1, source_target_pairs={{0,2},{2,4},{4,6},{6,0},{1,3},{3,5},{5,7},{7,1},{8,10},{10,12},{12... | collective-permute-start | bytes 393224 | tf_op jit(solution)/shard_map/ppermute | solution.py:129
  207.7 7.7 %collective-permute-start.11 = (bf16[16,32,128]{2,1,0:T(8,128)(2,1)S(1)}, bf16[16,32,128]{2,1,0:T(8,128)(2,1)S(1)}, u32[]{:S(2)}, u32[]{:S(2)}) collective-permute-start(bf16[16,32,128]{2,1,0:T(8,128)(2,1)S(1)} %get-tuple-element.40), channel_id=1, source_target_pairs={{0,6},{2,0},{4,2},{6,4},{1,7},{3,1},{5,3},{7,5},{8,14},{10,8},{12,... | collective-permute-start | bytes 393224 | tf_op jit(solution)/shard_map/ppermute | solution.py:129
  209.6 10.3 %collective-permute-start.12 = (bf16[16,32,128]{2,1,0:T(8,128)(2,1)S(1)}, bf16[16,32,128]{2,1,0:T(8,128)(2,1)S(1)}, u32[]{:S(2)}, u32[]{:S(2)}) collective-permute-start(bf16[16,32,128]{2,1,0:T(8,128)(2,1)S(1)} %get-tuple-element.40), channel_id=1, source_target_pairs={{0,4},{2,6},{4,0},{6,2},{1,5},{3,7},{5,1},{7,3},{8,12},{10,14},{12... | collective-permute-start | bytes 393224 | tf_op jit(solution)/shard_map/ppermute | solution.py:129
  220.0 14.1 %collective-permute-start.13 = (bf16[64,32,128]{2,1,0:T(8,128)(2,1)S(1)}, bf16[64,32,128]{2,1,0:T(8,128)(2,1)S(1)}, u32[]{:S(2)}, u32[]{:S(2)}) collective-permute-start(bf16[64,32,128]{2,1,0:T(8,128)(2,1)S(1)} %pad_maximum_fusion.1.refs_0_), channel_id=1, source_target_pairs={{0,8},{8,16},{16,24},{24,0},{1,9},{9,17},{17,25},{25,1},{2,10},{10... | collective-permute-start | bytes 1572872 | tf_op jit(solution)/shard_map/ppermute | solution.py:129
  220.7 18.6 %collective-permute-start.14 = (bf16[64,32,128]{2,1,0:T(8,128)(2,1)S(1)}, bf16[64,32,128]{2,1,0:T(8,128)(2,1)S(1)}, u32[]{:S(2)}, u32[]{:S(2)}) collective-permute-start(bf16[64,32,128]{2,1,0:T(8,128)(2,1)S(1)} %pad_maximum_fusion.1.refs_0_), channel_id=1, source_target_pairs={{0,24},{8,0},{16,8},{24,16},{1,25},{9,1},{17,9},{25,17},{2,26},{10... | collective-permute-start | bytes 1572872 | tf_op jit(solution)/shard_map/ppermute | solution.py:129
  222.7 23.9 %collective-permute-start.15 = (bf16[64,32,128]{2,1,0:T(8,128)(2,1)S(1)}, bf16[64,32,128]{2,1,0:T(8,128)(2,1)S(1)}, u32[]{:S(2)}, u32[]{:S(2)}) collective-permute-start(bf16[64,32,128]{2,1,0:T(8,128)(2,1)S(1)} %pad_maximum_fusion.1.refs_0_), channel_id=1, source_target_pairs={{0,16},{8,24},{16,0},{24,8},{1,17},{9,25},{17,1},{25,9},{2,18},{10... | collective-permute-start | bytes 1572872 | tf_op jit(solution)/shard_map/ppermute | solution.py:129
  223.7 27.9 %collective-permute-start.16 = (bf16[64,32,128]{2,1,0:T(8,128)(2,1)S(1)}, bf16[64,32,128]{2,1,0:T(8,128)(2,1)S(1)}, u32[]{:S(2)}, u32[]{:S(2)}) collective-permute-start(bf16[64,32,128]{2,1,0:T(8,128)(2,1)S(1)} %pad_maximum_fusion.1.refs_0_), channel_id=1, source_target_pairs={{0,1},{1,0},{2,3},{3,2},{4,5},{5,4},{6,7},{7,6},{8,9},{9,8},{10,11... | collective-permute-start | bytes 1572872 | tf_op jit(solution)/shard_map/ppermute | solution.py:129
  234.1 17.5 %collective-permute-start.17 = (bf16[64,32,128]{2,1,0:T(8,128)(2,1)S(1)}, bf16[64,32,128]{2,1,0:T(8,128)(2,1)S(1)}, u32[]{:S(2)}, u32[]{:S(2)}) collective-permute-start(bf16[64,32,128]{2,1,0:T(8,128)(2,1)S(1)} %collective-permute-done.13.refs_1_), channel_id=1, source_target_pairs={{0,1},{1,0},{2,3},{3,2},{4,5},{5,4},{6,7},{7,6},{8,9},{9,8},{10,11... | collective-permute-start | bytes 1572872 | tf_op jit(solution)/shard_map/ppermute | solution.py:129
  239.2 12.4 %collective-permute-start.18 = (bf16[64,32,128]{2,1,0:T(8,128)(2,1)S(1)}, bf16[64,32,128]{2,1,0:T(8,128)(2,1)S(1)}, u32[]{:S(2)}, u32[]{:S(2)}) collective-permute-start(bf16[64,32,128]{2,1,0:T(8,128)(2,1)S(1)} %collective-permute-done.14.refs_2_), channel_id=1, source_target_pairs={{0,1},{1,0},{2,3},{3,2},{4,5},{5,4},{6,7},{7,6},{8,9},{9,8},{10,11... | collective-permute-start | bytes 1572872 | tf_op jit(solution)/shard_map/ppermute | solution.py:129
  246.6 6.5 %collective-permute-start.19 = (bf16[64,32,128]{2,1,0:T(8,128)(2,1)S(1)}, bf16[64,32,128]{2,1,0:T(8,128)(2,1)S(1)}, u32[]{:S(2)}, u32[]{:S(2)}) collective-permute-start(bf16[64,32,128]{2,1,0:T(8,128)(2,1)S(1)} %collective-permute-done.15.refs_3_), channel_id=1, source_target_pairs={{0,1},{1,0},{2,3},{3,2},{4,5},{5,4},{6,7},{7,6},{8,9},{9,8},{10,11... | collective-permute-start | bytes 1572872 | tf_op jit(solution)/shard_map/ppermute | solution.py:129
  253.1 3.5 copy-start.3
  290.2 7.1 %collective-permute-start.20 = (bf16[16,32,128]{2,1,0:T(8,128)(2,1)S(1)}, bf16[16,32,128]{2,1,0:T(8,128)(2,1)S(1)}, u32[]{:S(2)}, u32[]{:S(2)}) collective-permute-start(bf16[16,32,128]{2,1,0:T(8,128)(2,1)S(1)} %get-tuple-element.34), channel_id=1, source_target_pairs={{0,2},{2,4},{4,6},{6,0},{1,3},{3,5},{5,7},{7,1},{8,10},{10,12},{12... | collective-permute-start | bytes 393224 | tf_op jit(solution)/shard_map/ppermute | solution.py:129
  290.5 8.8 %collective-permute-start.21 = (bf16[16,32,128]{2,1,0:T(8,128)(2,1)S(1)}, bf16[16,32,128]{2,1,0:T(8,128)(2,1)S(1)}, u32[]{:S(2)}, u32[]{:S(2)}) collective-permute-start(bf16[16,32,128]{2,1,0:T(8,128)(2,1)S(1)} %get-tuple-element.34), channel_id=1, source_target_pairs={{0,6},{2,0},{4,2},{6,4},{1,7},{3,1},{5,3},{7,5},{8,14},{10,8},{12,... | collective-permute-start | bytes 393224 | tf_op jit(solution)/shard_map/ppermute | solution.py:129
  293.8 8.7 %collective-permute-start.22 = (bf16[16,32,128]{2,1,0:T(8,128)(2,1)S(1)}, bf16[16,32,128]{2,1,0:T(8,128)(2,1)S(1)}, u32[]{:S(2)}, u32[]{:S(2)}) collective-permute-start(bf16[16,32,128]{2,1,0:T(8,128)(2,1)S(1)} %get-tuple-element.34), channel_id=1, source_target_pairs={{0,4},{2,6},{4,0},{6,2},{1,5},{3,7},{5,1},{7,3},{8,12},{10,14},{12... | collective-permute-start | bytes 393224 | tf_op jit(solution)/shard_map/ppermute | solution.py:129
  302.6 11.4 %collective-permute-start.23 = (bf16[64,32,128]{2,1,0:T(8,128)(2,1)S(1)}, bf16[64,32,128]{2,1,0:T(8,128)(2,1)S(1)}, u32[]{:S(2)}, u32[]{:S(2)}) collective-permute-start(bf16[64,32,128]{2,1,0:T(8,128)(2,1)S(1)} %pad_maximum_fusion.2.refs_0_), channel_id=1, source_target_pairs={{0,8},{8,16},{16,24},{24,0},{1,9},{9,17},{17,25},{25,1},{2,10},{10... | collective-permute-start | bytes 1572872 | tf_op jit(solution)/shard_map/ppermute | solution.py:129
  305.4 15.6 %collective-permute-start.24 = (bf16[64,32,128]{2,1,0:T(8,128)(2,1)S(1)}, bf16[64,32,128]{2,1,0:T(8,128)(2,1)S(1)}, u32[]{:S(2)}, u32[]{:S(2)}) collective-permute-start(bf16[64,32,128]{2,1,0:T(8,128)(2,1)S(1)} %pad_maximum_fusion.2.refs_0_), channel_id=1, source_target_pairs={{0,24},{8,0},{16,8},{24,16},{1,25},{9,1},{17,9},{25,17},{2,26},{10... | collective-permute-start | bytes 1572872 | tf_op jit(solution)/shard_map/ppermute | solution.py:129
  305.4 20.8 %collective-permute-start.25 = (bf16[64,32,128]{2,1,0:T(8,128)(2,1)S(1)}, bf16[64,32,128]{2,1,0:T(8,128)(2,1)S(1)}, u32[]{:S(2)}, u32[]{:S(2)}) collective-permute-start(bf16[64,32,128]{2,1,0:T(8,128)(2,1)S(1)} %pad_maximum_fusion.2.refs_0_), channel_id=1, source_target_pairs={{0,16},{8,24},{16,0},{24,8},{1,17},{9,25},{17,1},{25,9},{2,18},{10... | collective-permute-start | bytes 1572872 | tf_op jit(solution)/shard_map/ppermute | solution.py:129
  307.3 23.1 %collective-permute-start.26 = (bf16[64,32,128]{2,1,0:T(8,128)(2,1)S(1)}, bf16[64,32,128]{2,1,0:T(8,128)(2,1)S(1)}, u32[]{:S(2)}, u32[]{:S(2)}) collective-permute-start(bf16[64,32,128]{2,1,0:T(8,128)(2,1)S(1)} %pad_maximum_fusion.2.refs_0_), channel_id=1, source_target_pairs={{0,1},{1,0},{2,3},{3,2},{4,5},{5,4},{6,7},{7,6},{8,9},{9,8},{10,11... | collective-permute-start | bytes 1572872 | tf_op jit(solution)/shard_map/ppermute | solution.py:129
  314.0 16.4 %collective-permute-start.27 = (bf16[64,32,128]{2,1,0:T(8,128)(2,1)S(1)}, bf16[64,32,128]{2,1,0:T(8,128)(2,1)S(1)}, u32[]{:S(2)}, u32[]{:S(2)}) collective-permute-start(bf16[64,32,128]{2,1,0:T(8,128)(2,1)S(1)} %collective-permute-done.23.refs_1_), channel_id=1, source_target_pairs={{0,1},{1,0},{2,3},{3,2},{4,5},{5,4},{6,7},{7,6},{8,9},{9,8},{10,11... | collective-permute-start | bytes 1572872 | tf_op jit(solution)/shard_map/ppermute | solution.py:129
  321.0 9.4 %collective-permute-start.28 = (bf16[64,32,128]{2,1,0:T(8,128)(2,1)S(1)}, bf16[64,32,128]{2,1,0:T(8,128)(2,1)S(1)}, u32[]{:S(2)}, u32[]{:S(2)}) collective-permute-start(bf16[64,32,128]{2,1,0:T(8,128)(2,1)S(1)} %collective-permute-done.24.refs_2_), channel_id=1, source_target_pairs={{0,1},{1,0},{2,3},{3,2},{4,5},{5,4},{6,7},{7,6},{8,9},{9,8},{10,11... | collective-permute-start | bytes 1572872 | tf_op jit(solution)/shard_map/ppermute | solution.py:129
  326.3 5.7 %collective-permute-start.29 = (bf16[64,32,128]{2,1,0:T(8,128)(2,1)S(1)}, bf16[64,32,128]{2,1,0:T(8,128)(2,1)S(1)}, u32[]{:S(2)}, u32[]{:S(2)}) collective-permute-start(bf16[64,32,128]{2,1,0:T(8,128)(2,1)S(1)} %collective-permute-done.25.refs_3_), channel_id=1, source_target_pairs={{0,1},{1,0},{2,3},{3,2},{4,5},{5,4},{6,7},{7,6},{8,9},{9,8},{10,11... | collective-permute-start | bytes 1572872 | tf_op jit(solution)/shard_map/ppermute | solution.py:129
  343.5 23.4 %all-to-all-start.5 = ((bf16[128,32,128]{2,1,0:T(8,128)(2,1)}), bf16[128,32,128]{2,1,0:T(8,128)(2,1)S(1)}, u32[]{:S(2)}, u32[]{:S(2)}) async-start(bf16[128,32,128]{2,1,0:T(8,128)(2,1)} %get-tuple-element.25), calls=%async_computation.5 | async-start | bytes 2097152 | tf_op jit(solution)/shard_map/all_to_all | solution.py:146
  351.8 3.4 copy-start.4
  362.4 9.1 %copy-start.14 = (s32[16,128]{1,0:T(8,128)S(1)}, s32[16,128]{1,0:T(8,128)}, u32[]{:S(2)}) copy-start(s32[16,128]{1,0:T(8,128)} %param.10) | copy-start | bytes 24580
  366.9 17.7 %copy-start.12 = (f32[16,32,128]{2,1,0:T(8,128)S(1)}, f32[16,32,128]{2,1,0:T(8,128)}, u32[]{:S(2)}) copy-start(f32[16,32,128]{2,1,0:T(8,128)} %copy-done.11) | copy-start | bytes 786436
  366.9 17.6 %all-to-all-start.2 = ((bf16[128,32,128]{2,1,0:T(8,128)(2,1)}), bf16[128,32,128]{2,1,0:T(8,128)(2,1)S(1)}, u32[]{:S(2)}, u32[]{:S(2)}) async-start(bf16[128,32,128]{2,1,0:T(8,128)(2,1)} %get-tuple-element.19), calls=%async_computation.2 | async-start | bytes 2097152 | tf_op jit(solution)/shard_map/all_to_all | solution.py:146
  (4 other events, 9.9 us)
Sparse Core Ops, SparseCore 0:
  11.1 64.5 all-gather.3
  119.5 56.9 all-gather.5
  206.0 58.4 all-gather.7

commit v3 on v2

--- a/solution.py
+++ b/solution.py
@@ -114,7 +114,7 @@
             out_specs=[pl.BlockSpec(piece, lambda i, *_: (0, 0, 0)), pl.BlockSpec(send, lambda i, *_: (0, 0, 0))],
             scratch_shapes=scratch,
         ),
-        compiler_params=pltpu.CompilerParams(vmem_limit_bytes=32 << 20),
+        compiler_params=pltpu.CompilerParams(vmem_limit_bytes=60 << 20),
         cost_estimate=pl.CostEstimate(
             flops=2 * n * configs * block_len * block_len,
             bytes_accessed=2 * (sources * configs * block_len + blocks.size + targets * configs * block_len),
@@ -129,16 +129,12 @@
     return lax.ppermute(value, axis, [(i, (i + by) % n) for i in range(n)])
 
 
-def after(value, *others):
-    return lax.optimization_barrier((value, *others))[0]
+def after(values, *others):
+    return lax.optimization_barrier((values, others))[0]
 
 
-def spread_z(mine):
-    return [turn(mine, "zh", by) for by in TURNS[1:]]
-
-
-def spread_x(mine, from_z):
-    column = jnp.concatenate([mine, *from_z], axis=0)
+def spread_x(mine):
+    column = jnp.concatenate([mine] + [turn(mine, "zh", by) for by in TURNS[1:]], axis=0)
     return [column] + [turn(column, "x", by) for by in TURNS[1:]]
 
 
@@ -167,16 +163,21 @@
     state_a, state_b = x_init[:, :half], x_init[:, half:]
     sum_a = weights[0] * reward_f * state_a
     sum_b = weights[0] * reward_f * state_b
+    near = spread_x(state_b.astype(jnp.bfloat16))
+    whole = lax.all_gather(state_a.astype(jnp.bfloat16), COL, axis=0, tiled=True)
     for iteration in range(STEPS):
-        low_a = state_a.astype(jnp.bfloat16)
-        low_b = state_b.astype(jnp.bfloat16)
-        whole = lax.all_gather(low_a, COL, axis=0, tiled=True)
-        near = spread_x(low_b, spread_z(low_b))
         far = [turn(piece, "core", 1) for piece in near]
         state_b = state_b + reduce_rows(*products(src, dst, place, near + far, blocks, span))
+        sum_b = sum_b + weights[iteration + 1] * reward_f * state_b
+        if iteration + 1 < STEPS:
+            near = spread_x(state_b.astype(jnp.bfloat16))
+            whole = after(whole, near[0])
         state_a = state_a + reduce_rows(*products(src, dst, place, [whole], blocks, span))
         sum_a = sum_a + weights[iteration + 1] * reward_f * state_a
-        sum_b = sum_b + weights[iteration + 1] * reward_f * state_b
+        if iteration + 1 < STEPS:
+            low_a = state_a.astype(jnp.bfloat16)
+            low_a, *near = lax.optimization_barrier((low_a, *near))
+            whole = lax.all_gather(low_a, COL, axis=0, tiled=True)
     return (
         jnp.concatenate([state_a, state_b], axis=1),
         jnp.concatenate([sum_a, sum_b], axis=1),

time: 396 us -> 368 us (0.929)
  starting transfers between devices: 114 us -> 69.3 us
  local copies, waits for them, and re-layouts: 25.5 us -> 3.88 us
  waiting for transfers between devices: 144 us -> 162 us
  Pallas kernels: 47.2 us -> 65.1 us
  blocking collectives: 40.9 us -> 45.2 us
    ppermute x30, starting transfers between devices: 89.2 us -> 47 us  [turn(): return lax.ppermute(value, axis, [(i, (i + by) % n) for i in range(n)])]
    ppermute x30, waiting for transfers between devices: 52.4 us -> 78.7 us  [turn(): return lax.ppermute(value, axis, [(i, (i + by) % n) for i in range(n)])]
    unnamed x30 -> x44, local copies, waits for them, and re-layouts: 23.7 us -> 1.52 us
    pallas_call x6, Pallas kernels: 47.2 us -> 65.1 us  [products(): pl.pallas_call(body, out_shape=[jax.ShapeDtypeStruct(piece, jnp.float32),...]
    all_gather x3 -> x2, waiting for transfers between devices: 57.1 us -> 46.1 us  [shards(): whole = lax.all_gather(low_a, COL, axis=0, tiled=True)]
    all_to_all x2, blocking collectives: 40.9 us -> 45.2 us  [reduce_rows(): got = lax.all_to_all(send, ROW, 0, 0, tiled=True)]
  transfers between devices with their start and end apart: 37 -> 37, of which waited for: 20 -> 25; matrix products, arithmetic and copies ran while one was open for 1% -> 1% of each run, Pallas kernels for 11% -> 12%
where the time goes in v3:
time: 368 us; the launch traced here: 367 us
  waiting for transfers between devices  162 us (44%)
  starting transfers between devices  69.3 us (19%)
  Pallas kernels  65.1 us (18%)
  blocking collectives  45.2 us (12%)
  between operations  14.9 us (4%)
  other arithmetic  6.05 us (2%)
  local copies, waits for them, and re-layouts  3.88 us (1%)
    ppermute x30, waiting for transfers between devices, turn(): return lax.ppermute(value, axis, [(i, (i + by) % n) for i in range(n)])  78.7 us
    pallas_call x6, Pallas kernels, products(): pl.pallas_call(body, out_shape=[jax.ShapeDtypeStruct(piece, jnp.float32),...  65.1 us
    ppermute x30, starting transfers between devices, turn(): return lax.ppermute(value, axis, [(i, (i + by) % n) for i in range(n)])  47 us
    all_gather x2, waiting for transfers between devices, shards(): whole = lax.all_gather(low_a, COL, axis=0, tiled=True)  46.1 us
    all_to_all x2, blocking collectives, reduce_rows(): got = lax.all_to_all(send, ROW, 0, 0, tiled=True)  45.2 us
    all_to_all x4, waiting for transfers between devices, reduce_rows(): got = lax.all_to_all(send, ROW, 0, 0, tiled=True)  37.5 us
    all_to_all x4, starting transfers between devices, reduce_rows(): got = lax.all_to_all(send, ROW, 0, 0, tiled=True)  22.2 us
  transfers between devices with their start and end apart: 37, of which 25 were waited for; matrix products, arithmetic and copies ran while one was open for 1% of the time, Pallas kernels for 12%

profile of v3, /device:TPU:1, one launch (start us, length us, event | category | flops | bytes accessed | tf_op | source)
XLA Modules:
  0.0 366.7 jit_solution(609753849304653850)
XLA Ops:
  7.2 1.7 fusion.4
  9.0 3.9 %collective-permute-start = (bf16[16,32,128]{2,1,0:T(8,128)(2,1)S(1)}, bf16[16,32,128]{2,1,0:T(8,128)(2,1)S(1)}, u32[]{:S(2)}, u32[]{:S(2)}) collective-permute-start(bf16[16,32,128]{2,1,0:T(8,128)(2,1)S(1)} %get-tuple-element.65), channel_id=1, source_target_pairs={{0,2},{2,4},{4,6},{6,0},{1,3},{3,5},{5,7},{7,1},{8,10},{10,12},{12... | collective-permute-start | bytes 393224 | tf_op jit(solution)/shard_map/ppermute | solution.py:129
  12.9 3.1 collective-permute-start.1
  16.0 4.4 %collective-permute-start.2 = (bf16[16,32,128]{2,1,0:T(8,128)(2,1)S(1)}, bf16[16,32,128]{2,1,0:T(8,128)(2,1)S(1)}, u32[]{:S(2)}, u32[]{:S(2)}) collective-permute-start(bf16[16,32,128]{2,1,0:T(8,128)(2,1)S(1)} %get-tuple-element.65), channel_id=1, source_target_pairs={{0,4},{2,6},{4,0},{6,2},{1,5},{3,7},{5,1},{7,3},{8,12},{10,14},{12... | collective-permute-start | bytes 393224 | tf_op jit(solution)/shard_map/ppermute | solution.py:129
  20.4 6.1 %collective-permute-done.1 = bf16[16,32,128]{2,1,0:T(8,128)(2,1)S(1)} collective-permute-done((bf16[16,32,128]{2,1,0:T(8,128)(2,1)S(1)}, bf16[16,32,128]{2,1,0:T(8,128)(2,1)S(1)}, u32[]{:S(2)}, u32[]{:S(2)}) %collective-permute-start.1) | collective-permute-done | bytes 131104 | tf_op jit(solution)/shard_map/ppermute | solution.py:129
  26.5 1.8 collective-permute-done.2
  29.7 1.5 collective-permute-start.4
  31.1 1.5 collective-permute-start.5
  32.7 1.7 collective-permute-start.6
  34.4 9.4 %collective-permute-done.3.refs_1_ = bf16[64,32,128]{2,1,0:T(8,128)(2,1)S(1)} collective-permute-done((bf16[64,32,128]{2,1,0:T(8,128)(2,1)S(1)}, bf16[64,32,128]{2,1,0:T(8,128)(2,1)S(1)}, u32[]{:S(2)}, u32[]{:S(2)}) %collective-permute-start.3) | collective-permute-done | bytes 524320 | tf_op jit(solution)/shard_map/ppermute | solution.py:129
  43.7 2.0 collective-permute-start.7
  46.9 9.9 %collective-permute-done.5.refs_3_ = bf16[64,32,128]{2,1,0:T(8,128)(2,1)S(1)} collective-permute-done((bf16[64,32,128]{2,1,0:T(8,128)(2,1)S(1)}, bf16[64,32,128]{2,1,0:T(8,128)(2,1)S(1)}, u32[]{:S(2)}, u32[]{:S(2)}) %collective-permute-start.5) | collective-permute-done | bytes 524320 | tf_op jit(solution)/shard_map/ppermute | solution.py:129
  56.8 3.6 collective-permute-start.9
  62.2 11.8 %products.6 = (f32[16,32,128]{2,1,0:T(8,128)}, bf16[128,32,128]{2,1,0:T(8,128)(2,1)}) custom-call(s32[256]{0:T(256)} %bitcast.69, s32[256]{0:T(256)} %bitcast.75, s32[33]{0:T(128)} %stack.135.place, bf16[64,32,128]{2,1,0:T(8,128)(2,1)} %copy-done.1, bf16[64,32,128]{2,1,0:T(8,128)(2,1)} %copy-done.4, bf16[64,32,128]{2,1,0:T(8,128)(2,1)} %copy-done.5, ...), custom_call_target="tpu_custom_call" | custom-call | flops 268435456 | bytes 13631488 | tf_op jit(solution)/shard_map/products/pallas_call | solution.py:107
  74.0 23.8 %all_to_all.30 = bf16[128,32,128]{2,1,0:T(8,128)(2,1)S(1)} all-to-all(bf16[128,32,128]{2,1,0:T(8,128)(2,1)} %get-tuple-element.27), channel_id=1, replica_groups=mesh['y'=4,'zl'=2,'x'=4,'zh'=4,'core'=2] {'y','zl'}, dimensions={0} | all-to-all | bytes 2097152 | tf_op jit(solution)/shard_map/all_to_all | solution.py:142
  98.1 3.6 collective-permute-start.11
  101.7 1.4 collective-permute-start.12
  103.1 3.7 %collective-permute-done.10 = bf16[16,32,128]{2,1,0:T(8,128)(2,1)S(1)} collective-permute-done((bf16[16,32,128]{2,1,0:T(8,128)(2,1)S(1)}, bf16[16,32,128]{2,1,0:T(8,128)(2,1)S(1)}, u32[]{:S(2)}, u32[]{:S(2)}) %collective-permute-start.10) | collective-permute-done | bytes 131104 | tf_op jit(solution)/shard_map/ppermute | solution.py:129
  106.8 3.4 collective-permute-done.12
  110.3 10.0 %products.7 = (f32[16,32,128]{2,1,0:T(8,128)}, bf16[128,32,128]{2,1,0:T(8,128)(2,1)}) custom-call(s32[256]{0:T(256)} %bitcast.70, s32[256]{0:T(256)} %bitcast.76, s32[33]{0:T(128)} %stack.135.place, bf16[512,32,128]{2,1,0:T(8,128)(2,1)} %all-gather.4.cloned.1.call-done.x_ref, bf16[256,128,128]{2,1,0:T(8,128)(2,1)} %bitcast.58), custom_call_target="tpu_custom_call" | custom-call | flops 268435456 | bytes 13631488 | tf_op jit(solution)/shard_map/products/pallas_call | solution.py:107
  120.3 7.7 %all-to-all-start.1 = ((bf16[128,32,128]{2,1,0:T(8,128)(2,1)}), bf16[128,32,128]{2,1,0:T(8,128)(2,1)S(1)}, u32[]{:S(2)}, u32[]{:S(2)}) async-start(bf16[128,32,128]{2,1,0:T(8,128)(2,1)} %get-tuple-element.30), calls=%async_computation.1 | async-start | bytes 2097152 | tf_op jit(solution)/shard_map/all_to_all | solution.py:142
  129.0 1.8 collective-permute-start.14
  131.1 11.3 %all-to-all-done.1 = bf16[128,32,128]{2,1,0:T(8,128)(2,1)S(1)} async-done(((bf16[128,32,128]{2,1,0:T(8,128)(2,1)}), bf16[128,32,128]{2,1,0:T(8,128)(2,1)S(1)}, u32[]{:S(2)}, u32[]{:S(2)}) %all-to-all-start.1) | async-done | bytes 1048608 | tf_op jit(solution)/shard_map/all_to_all | solution.py:142
  143.2 9.5 %collective-permute-done.15.refs_3_ = bf16[64,32,128]{2,1,0:T(8,128)(2,1)} collective-permute-done((bf16[64,32,128]{2,1,0:T(8,128)(2,1)S(1)}, bf16[64,32,128]{2,1,0:T(8,128)(2,1)}, u32[]{:S(2)}, u32[]{:S(2)}) %collective-permute-start.15) | collective-permute-done | bytes 524320 | tf_op jit(solution)/shard_map/ppermute | solution.py:129
  152.8 2.4 collective-permute-start.16
  156.7 2.2 collective-permute-done.17.refs_5_
  160.0 11.6 %products.8 = (f32[16,32,128]{2,1,0:T(8,128)}, bf16[128,32,128]{2,1,0:T(8,128)(2,1)}) custom-call(s32[256]{0:T(256)} %bitcast.71, s32[256]{0:T(256)} %bitcast.77, s32[33]{0:T(128)} %stack.135.place, bf16[64,32,128]{2,1,0:T(8,128)(2,1)} %copy-done.3, bf16[64,32,128]{2,1,0:T(8,128)(2,1)} %copy-done.10, bf16[64,32,128]{2,1,0:T(8,128)(2,1)} %collective-permute-done.14.refs_2_, ...), custom_call_target="tpu_custom_call" | custom-call | flops 268435456 | bytes 13631488 | tf_op jit(solution)/shard_map/products/pallas_call | solution.py:107
  171.7 21.4 %all_to_all.31 = bf16[128,32,128]{2,1,0:T(8,128)(2,1)S(1)} all-to-all(bf16[128,32,128]{2,1,0:T(8,128)(2,1)} %get-tuple-element.37), channel_id=1, replica_groups=mesh['y'=4,'zl'=2,'x'=4,'zh'=4,'core'=2] {'y','zl'}, dimensions={0} | all-to-all | bytes 2097152 | tf_op jit(solution)/shard_map/all_to_all | solution.py:142
  194.0 3.6 collective-permute-start.21
  197.5 2.8 collective-permute-start.22
  200.4 7.1 %collective-permute-done.20 = bf16[16,32,128]{2,1,0:T(8,128)(2,1)S(1)} collective-permute-done((bf16[16,32,128]{2,1,0:T(8,128)(2,1)S(1)}, bf16[16,32,128]{2,1,0:T(8,128)(2,1)S(1)}, u32[]{:S(2)}, u32[]{:S(2)}) %collective-permute-start.20) | collective-permute-done | bytes 131104 | tf_op jit(solution)/shard_map/ppermute | solution.py:129
  207.5 5.3 %collective-permute-done.21 = bf16[16,32,128]{2,1,0:T(8,128)(2,1)S(1)} collective-permute-done((bf16[16,32,128]{2,1,0:T(8,128)(2,1)S(1)}, bf16[16,32,128]{2,1,0:T(8,128)(2,1)S(1)}, u32[]{:S(2)}, u32[]{:S(2)}) %collective-permute-start.21) | collective-permute-done | bytes 131104 | tf_op jit(solution)/shard_map/ppermute | solution.py:129
  212.7 4.5 %collective-permute-done.22 = bf16[16,32,128]{2,1,0:T(8,128)(2,1)S(1)} collective-permute-done((bf16[16,32,128]{2,1,0:T(8,128)(2,1)S(1)}, bf16[16,32,128]{2,1,0:T(8,128)(2,1)S(1)}, u32[]{:S(2)}, u32[]{:S(2)}) %collective-permute-start.22) | collective-permute-done | bytes 131104 | tf_op jit(solution)/shard_map/ppermute | solution.py:129
  217.3 8.5 %all-gather.6.cloned.1.call-done.x_ref = bf16[512,32,128]{2,1,0:T(8,128)(2,1)} async-done(((bf16[16,32,128]{2,1,0:T(8,128)(2,1)}), bf16[512,32,128]{2,1,0:T(8,128)(2,1)}) %all-gather.6.cloned.1.call-update) | async-done | bytes 4194320 | tf_op jit(solution)/shard_map/all_gather | solution.py:180
  225.8 10.0 %products.9 = (f32[16,32,128]{2,1,0:T(8,128)}, bf16[128,32,128]{2,1,0:T(8,128)(2,1)}) custom-call(s32[256]{0:T(256)} %bitcast.72, s32[256]{0:T(256)} %bitcast.78, s32[33]{0:T(128)} %stack.135.place, bf16[512,32,128]{2,1,0:T(8,128)(2,1)} %all-gather.6.cloned.1.call-done.x_ref, bf16[256,128,128]{2,1,0:T(8,128)(2,1)} %bitcast.60), custom_call_target="tpu_custom_call" | custom-call | flops 268435456 | bytes 13631488 | tf_op jit(solution)/shard_map/products/pallas_call | solution.py:107
  235.9 5.4 %all-to-all-start.3 = ((bf16[128,32,128]{2,1,0:T(8,128)(2,1)}), bf16[128,32,128]{2,1,0:T(8,128)(2,1)S(1)}, u32[]{:S(2)}, u32[]{:S(2)}) async-start(bf16[128,32,128]{2,1,0:T(8,128)(2,1)} %get-tuple-element.40), calls=%async_computation.3 | async-start | bytes 2097152 | tf_op jit(solution)/shard_map/all_to_all | solution.py:142
  241.6 2.5 collective-permute-start.24
  244.7 11.9 %all-to-all-done.3 = bf16[128,32,128]{2,1,0:T(8,128)(2,1)S(1)} async-done(((bf16[128,32,128]{2,1,0:T(8,128)(2,1)}), bf16[128,32,128]{2,1,0:T(8,128)(2,1)S(1)}, u32[]{:S(2)}, u32[]{:S(2)}) %all-to-all-start.3) | async-done | bytes 1048608 | tf_op jit(solution)/shard_map/all_to_all | solution.py:142
  257.6 9.9 %collective-permute-done.25.refs_3_ = bf16[64,32,128]{2,1,0:T(8,128)(2,1)} collective-permute-done((bf16[64,32,128]{2,1,0:T(8,128)(2,1)S(1)}, bf16[64,32,128]{2,1,0:T(8,128)(2,1)}, u32[]{:S(2)}, u32[]{:S(2)}) %collective-permute-start.25) | collective-permute-done | bytes 524320 | tf_op jit(solution)/shard_map/ppermute | solution.py:129
  267.5 1.5 collective-permute-start.26
  270.5 2.2 collective-permute-done.27.refs_5_
  273.8 11.6 %products.11 = (f32[16,32,128]{2,1,0:T(8,128)}, bf16[128,32,128]{2,1,0:T(8,128)(2,1)}) custom-call(s32[256]{0:T(256)} %bitcast.73, s32[256]{0:T(256)} %bitcast.79, s32[33]{0:T(128)} %stack.135.place, bf16[64,32,128]{2,1,0:T(8,128)(2,1)} %copy-done.2, bf16[64,32,128]{2,1,0:T(8,128)(2,1)} %copy-done.9, bf16[64,32,128]{2,1,0:T(8,128)(2,1)} %collective-permute-done.24.refs_2_, ...), custom_call_target="tpu_custom_call" | custom-call | flops 268435456 | bytes 13631488 | tf_op jit(solution)/shard_map/products/pallas_call | solution.py:107
  285.5 5.0 %all-to-all-start.5 = ((bf16[128,32,128]{2,1,0:T(8,128)(2,1)}), bf16[128,32,128]{2,1,0:T(8,128)(2,1)S(1)}, u32[]{:S(2)}, u32[]{:S(2)}) async-start(bf16[128,32,128]{2,1,0:T(8,128)(2,1)} %get-tuple-element.49), calls=%async_computation.5 | async-start | bytes 2097152 | tf_op jit(solution)/shard_map/all_to_all | solution.py:142
  290.5 37.5 %all-gather.8.cloned.1.call-done.x_ref = bf16[512,32,128]{2,1,0:T(8,128)(2,1)} async-done(((bf16[16,32,128]{2,1,0:T(8,128)(2,1)}), bf16[512,32,128]{2,1,0:T(8,128)(2,1)}) %all-gather.8.cloned.1.call-update) | async-done | bytes 4194320 | tf_op jit(solution)/shard_map/all_gather | solution.py:180
  328.0 10.0 %products.10 = (f32[16,32,128]{2,1,0:T(8,128)}, bf16[128,32,128]{2,1,0:T(8,128)(2,1)}) custom-call(s32[256]{0:T(256)} %bitcast.74, s32[256]{0:T(256)} %bitcast.80, s32[33]{0:T(128)} %stack.135.place, bf16[512,32,128]{2,1,0:T(8,128)(2,1)} %all-gather.8.cloned.1.call-done.x_ref, bf16[256,128,128]{2,1,0:T(8,128)(2,1)} %bitcast.62), custom_call_target="tpu_custom_call" | custom-call | flops 268435456 | bytes 13631488 | tf_op jit(solution)/shard_map/products/pallas_call | solution.py:107
  338.0 4.0 %all-to-all-start.4 = ((bf16[128,32,128]{2,1,0:T(8,128)(2,1)}), bf16[128,32,128]{2,1,0:T(8,128)(2,1)S(1)}, u32[]{:S(2)}, u32[]{:S(2)}) async-start(bf16[128,32,128]{2,1,0:T(8,128)(2,1)} %get-tuple-element.43), calls=%async_computation.4 | async-start | bytes 2097152 | tf_op jit(solution)/shard_map/all_to_all | solution.py:142
  343.1 14.3 %all-to-all-done.4 = bf16[128,32,128]{2,1,0:T(8,128)(2,1)S(1)} async-done(((bf16[128,32,128]{2,1,0:T(8,128)(2,1)}), bf16[128,32,128]{2,1,0:T(8,128)(2,1)S(1)}, u32[]{:S(2)}, u32[]{:S(2)}) %all-to-all-start.4) | async-done | bytes 1048608 | tf_op jit(solution)/shard_map/all_to_all | solution.py:142
  357.5 1.5 multiply_add_fusion.1
  (99 shorter events, 16.4 us)
Async XLA Ops:
  7.2 103.1 %all-gather.4.cloned.1.call-start = ((), (), s32[]{:S(2)}) async-start(), calls=%async_computation.6 | async-start | bytes 4325376 | tf_op jit(solution)/shard_map/all_gather | solution.py:167
  9.0 11.4 %collective-permute-start = (bf16[16,32,128]{2,1,0:T(8,128)(2,1)S(1)}, bf16[16,32,128]{2,1,0:T(8,128)(2,1)S(1)}, u32[]{:S(2)}, u32[]{:S(2)}) collective-permute-start(bf16[16,32,128]{2,1,0:T(8,128)(2,1)S(1)} %get-tuple-element.65), channel_id=1, source_target_pairs={{0,2},{2,4},{4,6},{6,0},{1,3},{3,5},{5,7},{7,1},{8,10},{10,12},{12... | collective-permute-start | bytes 393224 | tf_op jit(solution)/shard_map/ppermute | solution.py:129
  12.9 13.6 %collective-permute-start.1 = (bf16[16,32,128]{2,1,0:T(8,128)(2,1)S(1)}, bf16[16,32,128]{2,1,0:T(8,128)(2,1)S(1)}, u32[]{:S(2)}, u32[]{:S(2)}) collective-permute-start(bf16[16,32,128]{2,1,0:T(8,128)(2,1)S(1)} %get-tuple-element.65), channel_id=1, source_target_pairs={{0,6},{2,0},{4,2},{6,4},{1,7},{3,1},{5,3},{7,5},{8,14},{10,8},{12,... | collective-permute-start | bytes 393224 | tf_op jit(solution)/shard_map/ppermute | solution.py:129
  16.0 12.3 %collective-permute-start.2 = (bf16[16,32,128]{2,1,0:T(8,128)(2,1)S(1)}, bf16[16,32,128]{2,1,0:T(8,128)(2,1)S(1)}, u32[]{:S(2)}, u32[]{:S(2)}) collective-permute-start(bf16[16,32,128]{2,1,0:T(8,128)(2,1)S(1)} %get-tuple-element.65), channel_id=1, source_target_pairs={{0,4},{2,6},{4,0},{6,2},{1,5},{3,7},{5,1},{7,3},{8,12},{10,14},{12... | collective-permute-start | bytes 393224 | tf_op jit(solution)/shard_map/ppermute | solution.py:129
  28.4 33.8 %copy-start.1 = (bf16[64,32,128]{2,1,0:T(8,128)(2,1)}, bf16[64,32,128]{2,1,0:T(8,128)(2,1)S(1)}, u32[]{:S(2)}) copy-start(bf16[64,32,128]{2,1,0:T(8,128)(2,1)S(1)} %pad_maximum_fusion.refs_0_) | copy-start | bytes 1572868
  28.4 15.4 %collective-permute-start.3 = (bf16[64,32,128]{2,1,0:T(8,128)(2,1)S(1)}, bf16[64,32,128]{2,1,0:T(8,128)(2,1)S(1)}, u32[]{:S(2)}, u32[]{:S(2)}) collective-permute-start(bf16[64,32,128]{2,1,0:T(8,128)(2,1)S(1)} %pad_maximum_fusion.refs_0_), channel_id=1, source_target_pairs={{0,8},{8,16},{16,24},{24,0},{1,9},{9,17},{17,25},{25,1},{2,10},{10... | collective-permute-start | bytes 1572872 | tf_op jit(solution)/shard_map/ppermute | solution.py:129
  29.7 16.1 %collective-permute-start.4 = (bf16[64,32,128]{2,1,0:T(8,128)(2,1)S(1)}, bf16[64,32,128]{2,1,0:T(8,128)(2,1)S(1)}, u32[]{:S(2)}, u32[]{:S(2)}) collective-permute-start(bf16[64,32,128]{2,1,0:T(8,128)(2,1)S(1)} %pad_maximum_fusion.refs_0_), channel_id=1, source_target_pairs={{0,24},{8,0},{16,8},{24,16},{1,25},{9,1},{17,9},{25,17},{2,26},{10... | collective-permute-start | bytes 1572872 | tf_op jit(solution)/shard_map/ppermute | solution.py:129
  31.1 25.6 %collective-permute-start.5 = (bf16[64,32,128]{2,1,0:T(8,128)(2,1)S(1)}, bf16[64,32,128]{2,1,0:T(8,128)(2,1)S(1)}, u32[]{:S(2)}, u32[]{:S(2)}) collective-permute-start(bf16[64,32,128]{2,1,0:T(8,128)(2,1)S(1)} %pad_maximum_fusion.refs_0_), channel_id=1, source_target_pairs={{0,16},{8,24},{16,0},{24,8},{1,17},{9,25},{17,1},{25,9},{2,18},{10... | collective-permute-start | bytes 1572872 | tf_op jit(solution)/shard_map/ppermute | solution.py:129
  32.7 28.3 %collective-permute-start.6 = (bf16[64,32,128]{2,1,0:T(8,128)(2,1)S(1)}, bf16[64,32,128]{2,1,0:T(8,128)(2,1)S(1)}, u32[]{:S(2)}, u32[]{:S(2)}) collective-permute-start(bf16[64,32,128]{2,1,0:T(8,128)(2,1)S(1)} %pad_maximum_fusion.refs_0_), channel_id=1, source_target_pairs={{0,1},{1,0},{2,3},{3,2},{4,5},{5,4},{6,7},{7,6},{8,9},{9,8},{10,11... | collective-permute-start | bytes 1572872 | tf_op jit(solution)/shard_map/ppermute | solution.py:129
  43.7 18.4 %copy-start.4 = (bf16[64,32,128]{2,1,0:T(8,128)(2,1)}, bf16[64,32,128]{2,1,0:T(8,128)(2,1)S(1)}, u32[]{:S(2)}) copy-start(bf16[64,32,128]{2,1,0:T(8,128)(2,1)S(1)} %collective-permute-done.3.refs_1_) | copy-start | bytes 1572868
  43.7 17.2 %collective-permute-start.7 = (bf16[64,32,128]{2,1,0:T(8,128)(2,1)S(1)}, bf16[64,32,128]{2,1,0:T(8,128)(2,1)S(1)}, u32[]{:S(2)}, u32[]{:S(2)}) collective-permute-start(bf16[64,32,128]{2,1,0:T(8,128)(2,1)S(1)} %collective-permute-done.3.refs_1_), channel_id=1, source_target_pairs={{0,1},{1,0},{2,3},{3,2},{4,5},{5,4},{6,7},{7,6},{8,9},{9,8},{10,11... | collective-permute-start | bytes 1572872 | tf_op jit(solution)/shard_map/ppermute | solution.py:129
  45.8 16.4 %copy-start.5 = (bf16[64,32,128]{2,1,0:T(8,128)(2,1)}, bf16[64,32,128]{2,1,0:T(8,128)(2,1)S(1)}, u32[]{:S(2)}) copy-start(bf16[64,32,128]{2,1,0:T(8,128)(2,1)S(1)} %collective-permute-done.4.refs_2_) | copy-start | bytes 1572868
  45.8 15.2 %collective-permute-start.8 = (bf16[64,32,128]{2,1,0:T(8,128)(2,1)S(1)}, bf16[64,32,128]{2,1,0:T(8,128)(2,1)}, u32[]{:S(2)}, u32[]{:S(2)}) collective-permute-start(bf16[64,32,128]{2,1,0:T(8,128)(2,1)S(1)} %collective-permute-done.4.refs_2_), channel_id=1, source_target_pairs={{0,1},{1,0},{2,3},{3,2},{4,5},{5,4},{6,7},{7,6},{8,9},{9,8},{10,11... | collective-permute-start | bytes 1572872 | tf_op jit(solution)/shard_map/ppermute | solution.py:129
  56.8 5.4 %collective-permute-start.9 = (bf16[64,32,128]{2,1,0:T(8,128)(2,1)S(1)}, bf16[64,32,128]{2,1,0:T(8,128)(2,1)}, u32[]{:S(2)}, u32[]{:S(2)}) collective-permute-start(bf16[64,32,128]{2,1,0:T(8,128)(2,1)S(1)} %collective-permute-done.5.refs_3_), channel_id=1, source_target_pairs={{0,1},{1,0},{2,3},{3,2},{4,5},{5,4},{6,7},{7,6},{8,9},{9,8},{10,11... | collective-permute-start | bytes 1572872 | tf_op jit(solution)/shard_map/ppermute | solution.py:129
  74.0 23.9 %copy-start = (f32[16,64,128]{2,1,0:T(8,128)S(1)}, f32[16,64,128]{2,1,0:T(8,128)}, u32[]{:S(2)}) copy-start(f32[16,64,128]{2,1,0:T(8,128)} %param.6) | copy-start | bytes 1572868
  74.0 23.9 %copy-start.20 = (f32[16,32,128]{2,1,0:T(8,128)S(1)}, f32[16,32,128]{2,1,0:T(8,128)}, u32[]{:S(2)}) copy-start(f32[16,32,128]{2,1,0:T(8,128)} %get-tuple-element.26) | copy-start | bytes 786436
  98.0 8.7 %collective-permute-start.10 = (bf16[16,32,128]{2,1,0:T(8,128)(2,1)S(1)}, bf16[16,32,128]{2,1,0:T(8,128)(2,1)S(1)}, u32[]{:S(2)}, u32[]{:S(2)}) collective-permute-start(bf16[16,32,128]{2,1,0:T(8,128)(2,1)S(1)} %get-tuple-element.60), channel_id=1, source_target_pairs={{0,2},{2,4},{4,6},{6,0},{1,3},{3,5},{5,7},{7,1},{8,10},{10,12},{12... | collective-permute-start | bytes 393224 | tf_op jit(solution)/shard_map/ppermute | solution.py:129
  98.1 8.6 %collective-permute-start.11 = (bf16[16,32,128]{2,1,0:T(8,128)(2,1)S(1)}, bf16[16,32,128]{2,1,0:T(8,128)(2,1)S(1)}, u32[]{:S(2)}, u32[]{:S(2)}) collective-permute-start(bf16[16,32,128]{2,1,0:T(8,128)(2,1)S(1)} %get-tuple-element.60), channel_id=1, source_target_pairs={{0,6},{2,0},{4,2},{6,4},{1,7},{3,1},{5,3},{7,5},{8,14},{10,8},{12,... | collective-permute-start | bytes 393224 | tf_op jit(solution)/shard_map/ppermute | solution.py:129
  101.7 8.5 %collective-permute-start.12 = (bf16[16,32,128]{2,1,0:T(8,128)(2,1)S(1)}, bf16[16,32,128]{2,1,0:T(8,128)(2,1)S(1)}, u32[]{:S(2)}, u32[]{:S(2)}) collective-permute-start(bf16[16,32,128]{2,1,0:T(8,128)(2,1)S(1)} %get-tuple-element.60), channel_id=1, source_target_pairs={{0,4},{2,6},{4,0},{6,2},{1,5},{3,7},{5,1},{7,3},{8,12},{10,14},{12... | collective-permute-start | bytes 393224 | tf_op jit(solution)/shard_map/ppermute | solution.py:129
  110.3 42.5 %copy-start.3 = (bf16[64,32,128]{2,1,0:T(8,128)(2,1)}, bf16[64,32,128]{2,1,0:T(8,128)(2,1)S(1)}, u32[]{:S(2)}) copy-start(bf16[64,32,128]{2,1,0:T(8,128)(2,1)S(1)} %pad_maximum_fusion.1.refs_0_) | copy-start | bytes 1572868
  120.3 22.2 %copy-start.18 = (f32[16,32,128]{2,1,0:T(8,128)S(1)}, f32[16,32,128]{2,1,0:T(8,128)}, u32[]{:S(2)}) copy-start(f32[16,32,128]{2,1,0:T(8,128)} %get-tuple-element.29) | copy-start | bytes 786436
  120.3 22.0 %all-to-all-start.1 = ((bf16[128,32,128]{2,1,0:T(8,128)(2,1)}), bf16[128,32,128]{2,1,0:T(8,128)(2,1)S(1)}, u32[]{:S(2)}, u32[]{:S(2)}) async-start(bf16[128,32,128]{2,1,0:T(8,128)(2,1)} %get-tuple-element.30), calls=%async_computation.1 | async-start | bytes 2097152 | tf_op jit(solution)/shard_map/all_to_all | solution.py:142
  128.0 97.8 %all-gather.6.cloned.1.call-start = ((), (), s32[]{:S(2)}) async-start(), calls=%async_computation.7 | async-start | bytes 4325376 | tf_op jit(solution)/shard_map/all_gather | solution.py:180
  128.1 15.2 %collective-permute-start.13 = (bf16[64,32,128]{2,1,0:T(8,128)(2,1)S(1)}, bf16[64,32,128]{2,1,0:T(8,128)(2,1)S(1)}, u32[]{:S(2)}, u32[]{:S(2)}) collective-permute-start(bf16[64,32,128]{2,1,0:T(8,128)(2,1)S(1)} %pad_maximum_fusion.1.refs_0_), channel_id=1, source_target_pairs={{0,8},{8,16},{16,24},{24,0},{1,9},{9,17},{17,25},{25,1},{2,10},{10... | collective-permute-start | bytes 1572872 | tf_op jit(solution)/shard_map/ppermute | solution.py:129
  129.0 14.2 %collective-permute-start.14 = (bf16[64,32,128]{2,1,0:T(8,128)(2,1)S(1)}, bf16[64,32,128]{2,1,0:T(8,128)(2,1)}, u32[]{:S(2)}, u32[]{:S(2)}) collective-permute-start(bf16[64,32,128]{2,1,0:T(8,128)(2,1)S(1)} %pad_maximum_fusion.1.refs_0_), channel_id=1, source_target_pairs={{0,24},{8,0},{16,8},{24,16},{1,25},{9,1},{17,9},{25,17},{2,26},{10... | collective-permute-start | bytes 1572872 | tf_op jit(solution)/shard_map/ppermute | solution.py:129
  130.8 21.9 %collective-permute-start.15 = (bf16[64,32,128]{2,1,0:T(8,128)(2,1)S(1)}, bf16[64,32,128]{2,1,0:T(8,128)(2,1)}, u32[]{:S(2)}, u32[]{:S(2)}) collective-permute-start(bf16[64,32,128]{2,1,0:T(8,128)(2,1)S(1)} %pad_maximum_fusion.1.refs_0_), channel_id=1, source_target_pairs={{0,16},{8,24},{16,0},{24,8},{1,17},{9,25},{17,1},{25,9},{2,18},{10... | collective-permute-start | bytes 1572872 | tf_op jit(solution)/shard_map/ppermute | solution.py:129
  143.2 16.0 %copy-start.10 = (bf16[64,32,128]{2,1,0:T(8,128)(2,1)}, bf16[64,32,128]{2,1,0:T(8,128)(2,1)S(1)}, u32[]{:S(2)}) copy-start(bf16[64,32,128]{2,1,0:T(8,128)(2,1)S(1)} %collective-permute-done.13.refs_1_) | copy-start | bytes 1572868
  152.8 3.9 %collective-permute-start.16 = (bf16[64,32,128]{2,1,0:T(8,128)(2,1)S(1)}, bf16[64,32,128]{2,1,0:T(8,128)(2,1)S(1)}, u32[]{:S(2)}, u32[]{:S(2)}) collective-permute-start(bf16[64,32,128]{2,1,0:T(8,128)(2,1)S(1)} %pad_maximum_fusion.1.refs_0_), channel_id=1, source_target_pairs={{0,1},{1,0},{2,3},{3,2},{4,5},{5,4},{6,7},{7,6},{8,9},{9,8},{10,11... | collective-permute-start | bytes 1572872 | tf_op jit(solution)/shard_map/ppermute | solution.py:129
  155.1 3.8 %collective-permute-start.17 = (bf16[64,32,128]{2,1,0:T(8,128)(2,1)S(1)}, bf16[64,32,128]{2,1,0:T(8,128)(2,1)S(1)}, u32[]{:S(2)}, u32[]{:S(2)}) collective-permute-start(bf16[64,32,128]{2,1,0:T(8,128)(2,1)S(1)} %collective-permute-done.13.refs_1_), channel_id=1, source_target_pairs={{0,1},{1,0},{2,3},{3,2},{4,5},{5,4},{6,7},{7,6},{8,9},{9,8},{10,11... | collective-permute-start | bytes 1572872 | tf_op jit(solution)/shard_map/ppermute | solution.py:129
  155.2 3.9 %collective-permute-start.18 = (bf16[64,32,128]{2,1,0:T(8,128)(2,1)}, bf16[64,32,128]{2,1,0:T(8,128)(2,1)S(1)}, u32[]{:S(2)}, u32[]{:S(2)}) collective-permute-start(bf16[64,32,128]{2,1,0:T(8,128)(2,1)} %collective-permute-done.14.refs_2_), channel_id=1, source_target_pairs={{0,1},{1,0},{2,3},{3,2},{4,5},{5,4},{6,7},{7,6},{8,9},{9,8},{10,11... | collective-permute-start | bytes 1572872 | tf_op jit(solution)/shard_map/ppermute | solution.py:129
  155.7 3.6 collective-permute-start.19
  171.7 21.5 %copy-start.19 = (f32[16,32,128]{2,1,0:T(8,128)S(1)}, f32[16,32,128]{2,1,0:T(8,128)}, u32[]{:S(2)}) copy-start(f32[16,32,128]{2,1,0:T(8,128)} %get-tuple-element.36) | copy-start | bytes 786436
  194.0 13.5 %collective-permute-start.20 = (bf16[16,32,128]{2,1,0:T(8,128)(2,1)S(1)}, bf16[16,32,128]{2,1,0:T(8,128)(2,1)S(1)}, u32[]{:S(2)}, u32[]{:S(2)}) collective-permute-start(bf16[16,32,128]{2,1,0:T(8,128)(2,1)S(1)} %get-tuple-element.56), channel_id=1, source_target_pairs={{0,2},{2,4},{4,6},{6,0},{1,3},{3,5},{5,7},{7,1},{8,10},{10,12},{12... | collective-permute-start | bytes 393224 | tf_op jit(solution)/shard_map/ppermute | solution.py:129
  194.0 18.8 %collective-permute-start.21 = (bf16[16,32,128]{2,1,0:T(8,128)(2,1)S(1)}, bf16[16,32,128]{2,1,0:T(8,128)(2,1)S(1)}, u32[]{:S(2)}, u32[]{:S(2)}) collective-permute-start(bf16[16,32,128]{2,1,0:T(8,128)(2,1)S(1)} %get-tuple-element.56), channel_id=1, source_target_pairs={{0,6},{2,0},{4,2},{6,4},{1,7},{3,1},{5,3},{7,5},{8,14},{10,8},{12,... | collective-permute-start | bytes 393224 | tf_op jit(solution)/shard_map/ppermute | solution.py:129
  197.5 19.7 %collective-permute-start.22 = (bf16[16,32,128]{2,1,0:T(8,128)(2,1)S(1)}, bf16[16,32,128]{2,1,0:T(8,128)(2,1)S(1)}, u32[]{:S(2)}, u32[]{:S(2)}) collective-permute-start(bf16[16,32,128]{2,1,0:T(8,128)(2,1)S(1)} %get-tuple-element.56), channel_id=1, source_target_pairs={{0,4},{2,6},{4,0},{6,2},{1,5},{3,7},{5,1},{7,3},{8,12},{10,14},{12... | collective-permute-start | bytes 393224 | tf_op jit(solution)/shard_map/ppermute | solution.py:129
  217.3 50.2 %copy-start.2 = (bf16[64,32,128]{2,1,0:T(8,128)(2,1)}, bf16[64,32,128]{2,1,0:T(8,128)(2,1)S(1)}, u32[]{:S(2)}) copy-start(bf16[64,32,128]{2,1,0:T(8,128)(2,1)S(1)} %pad_maximum_fusion.2.refs_0_) | copy-start | bytes 1572868
  235.9 20.9 %copy-start.17 = (f32[16,32,128]{2,1,0:T(8,128)S(1)}, f32[16,32,128]{2,1,0:T(8,128)}, u32[]{:S(2)}) copy-start(f32[16,32,128]{2,1,0:T(8,128)} %get-tuple-element.39) | copy-start | bytes 786436
  235.9 20.7 %all-to-all-start.3 = ((bf16[128,32,128]{2,1,0:T(8,128)(2,1)}), bf16[128,32,128]{2,1,0:T(8,128)(2,1)S(1)}, u32[]{:S(2)}, u32[]{:S(2)}) async-start(bf16[128,32,128]{2,1,0:T(8,128)(2,1)} %get-tuple-element.40), calls=%async_computation.3 | async-start | bytes 2097152 | tf_op jit(solution)/shard_map/all_to_all | solution.py:142
  241.3 86.7 %all-gather.8.cloned.1.call-start = ((), (), s32[]{:S(2)}) async-start(), calls=%async_computation.8 | async-start | bytes 4325376 | tf_op jit(solution)/shard_map/all_gather | solution.py:180
  241.3 16.2 %collective-permute-start.23 = (bf16[64,32,128]{2,1,0:T(8,128)(2,1)S(1)}, bf16[64,32,128]{2,1,0:T(8,128)(2,1)S(1)}, u32[]{:S(2)}, u32[]{:S(2)}) collective-permute-start(bf16[64,32,128]{2,1,0:T(8,128)(2,1)S(1)} %pad_maximum_fusion.2.refs_0_), channel_id=1, source_target_pairs={{0,8},{8,16},{16,24},{24,0},{1,9},{9,17},{17,25},{25,1},{2,10},{10... | collective-permute-start | bytes 1572872 | tf_op jit(solution)/shard_map/ppermute | solution.py:129
  241.6 16.0 %collective-permute-start.24 = (bf16[64,32,128]{2,1,0:T(8,128)(2,1)S(1)}, bf16[64,32,128]{2,1,0:T(8,128)(2,1)}, u32[]{:S(2)}, u32[]{:S(2)}) collective-permute-start(bf16[64,32,128]{2,1,0:T(8,128)(2,1)S(1)} %pad_maximum_fusion.2.refs_0_), channel_id=1, source_target_pairs={{0,24},{8,0},{16,8},{24,16},{1,25},{9,1},{17,9},{25,17},{2,26},{10... | collective-permute-start | bytes 1572872 | tf_op jit(solution)/shard_map/ppermute | solution.py:129
  244.1 23.4 %collective-permute-start.25 = (bf16[64,32,128]{2,1,0:T(8,128)(2,1)S(1)}, bf16[64,32,128]{2,1,0:T(8,128)(2,1)}, u32[]{:S(2)}, u32[]{:S(2)}) collective-permute-start(bf16[64,32,128]{2,1,0:T(8,128)(2,1)S(1)} %pad_maximum_fusion.2.refs_0_), channel_id=1, source_target_pairs={{0,16},{8,24},{16,0},{24,8},{1,17},{9,25},{17,1},{25,9},{2,18},{10... | collective-permute-start | bytes 1572872 | tf_op jit(solution)/shard_map/ppermute | solution.py:129
  267.5 3.0 collective-permute-start.26
  269.0 3.8 %collective-permute-start.27 = (bf16[64,32,128]{2,1,0:T(8,128)(2,1)S(1)}, bf16[64,32,128]{2,1,0:T(8,128)(2,1)S(1)}, u32[]{:S(2)}, u32[]{:S(2)}) collective-permute-start(bf16[64,32,128]{2,1,0:T(8,128)(2,1)S(1)} %collective-permute-done.23.refs_1_), channel_id=1, source_target_pairs={{0,1},{1,0},{2,3},{3,2},{4,5},{5,4},{6,7},{7,6},{8,9},{9,8},{10,11... | collective-permute-start | bytes 1572872 | tf_op jit(solution)/shard_map/ppermute | solution.py:129
  269.1 3.9 %collective-permute-start.28 = (bf16[64,32,128]{2,1,0:T(8,128)(2,1)}, bf16[64,32,128]{2,1,0:T(8,128)(2,1)S(1)}, u32[]{:S(2)}, u32[]{:S(2)}) collective-permute-start(bf16[64,32,128]{2,1,0:T(8,128)(2,1)} %collective-permute-done.24.refs_2_), channel_id=1, source_target_pairs={{0,1},{1,0},{2,3},{3,2},{4,5},{5,4},{6,7},{7,6},{8,9},{9,8},{10,11... | collective-permute-start | bytes 1572872 | tf_op jit(solution)/shard_map/ppermute | solution.py:129
  269.5 3.6 collective-permute-start.29
  285.5 52.6 %all-to-all-start.5 = ((bf16[128,32,128]{2,1,0:T(8,128)(2,1)}), bf16[128,32,128]{2,1,0:T(8,128)(2,1)S(1)}, u32[]{:S(2)}, u32[]{:S(2)}) async-start(bf16[128,32,128]{2,1,0:T(8,128)(2,1)} %get-tuple-element.49), calls=%async_computation.5 | async-start | bytes 2097152 | tf_op jit(solution)/shard_map/all_to_all | solution.py:142
  338.0 19.4 %all-to-all-start.4 = ((bf16[128,32,128]{2,1,0:T(8,128)(2,1)}), bf16[128,32,128]{2,1,0:T(8,128)(2,1)S(1)}, u32[]{:S(2)}, u32[]{:S(2)}) async-start(bf16[128,32,128]{2,1,0:T(8,128)(2,1)} %get-tuple-element.43), calls=%async_computation.4 | async-start | bytes 2097152 | tf_op jit(solution)/shard_map/all_to_all | solution.py:142
  (11 other events, 36.8 us)
Sparse Core Ops, SparseCore 0:
  10.6 64.9 all-gather.3
  152.9 72.9 all-gather.5
  267.6 60.3 all-gather.7

commit v4 on v3

--- a/solution.py
+++ b/solution.py
@@ -11,6 +11,7 @@
 ROW = ("y", "zl")
 COL = ("x", "zh", "core")
 GROUPS = 8
+STREAMS = 4
 TURNS = (0, 1, 3, 2)
 
 
@@ -26,13 +27,14 @@
     return weights
 
 
-def add_products(step, base, src, dst, x_ref, blk_ref, acc):
-    slots = blk_ref.shape[0]
-    for slot in range(slots):
-        at = step * slots + slot
+def add_products(step, base, src, dst, x_ref, streams, acc):
+    slots = streams[0].shape[0]
+    for slot in range(len(streams) * slots):
+        at = step * len(streams) * slots + slot
         vectors = x_ref[src[at] - base]
         into = dst[at]
-        acc[into] += jnp.dot(vectors, blk_ref[slot], preferred_element_type=jnp.float32)
+        block = streams[slot // slots][slot % slots]
+        acc[into] += jnp.dot(vectors, block, preferred_element_type=jnp.float32)
 
 
 def hand_out(place, own_ref, send_ref, acc):
@@ -43,14 +45,15 @@
     send_ref[mine] = jnp.zeros(own_ref.shape, send_ref.dtype)
 
 
-def whole_body(src, dst, place, x_ref, blk_ref, own_ref, send_ref, acc):
+def whole_body(src, dst, place, x_ref, *refs):
+    streams, (own_ref, send_ref, acc) = refs[:STREAMS], refs[STREAMS:]
     step = pl.program_id(0)
 
     @pl.when(step == 0)
     def _():
         acc[...] = jnp.zeros_like(acc)
 
-    add_products(step, step * x_ref.shape[0], src, dst, x_ref, blk_ref, acc)
+    add_products(step, step * x_ref.shape[0], src, dst, x_ref, streams, acc)
 
     @pl.when(step == pl.num_programs(0) - 1)
     def _():
@@ -58,7 +61,8 @@
 
 
 def pieces_body(src, dst, place, *refs):
-    pieces, (blk_ref, own_ref, send_ref, acc, whole, sems) = refs[:8], refs[8:]
+    pieces, streams = refs[:8], refs[8 : 8 + STREAMS]
+    own_ref, send_ref, acc, whole, sems = refs[8 + STREAMS :]
     span = own_ref.shape[0]
     step = pl.program_id(0)
 
@@ -82,11 +86,16 @@
         for copy in copies:
             copy.wait()
 
-    add_products(step, 0, src, dst, whole, blk_ref, acc)
+    add_products(step, 0, src, dst, whole, streams, acc)
 
     @pl.when(step == pl.num_programs(0) - 1)
     def _():
         hand_out(place, own_ref, send_ref, acc)
+
+
+def stream(n, block_len, q):
+    shape = (n // GROUPS // STREAMS, block_len, block_len)
+    return pl.BlockSpec(shape, lambda i, *_: (i * STREAMS + q, 0, 0))
 
 
 def products(src, dst, place, given, blocks, span):
@@ -110,7 +119,7 @@
         grid_spec=pltpu.PrefetchScalarGridSpec(
             num_scalar_prefetch=3,
             grid=(GROUPS,),
-            in_specs=specs + [pl.BlockSpec((n // GROUPS, block_len, block_len), lambda i, *_: (i, 0, 0))],
+            in_specs=specs + [stream(n, block_len, q) for q in range(STREAMS)],
             out_specs=[pl.BlockSpec(piece, lambda i, *_: (0, 0, 0)), pl.BlockSpec(send, lambda i, *_: (0, 0, 0))],
             scratch_shapes=scratch,
         ),
@@ -121,7 +130,7 @@
             transcendentals=0,
         ),
         name="products",
-    )(src, dst, place, *given, blocks)
+    )(src, dst, place, *given, *[blocks] * STREAMS)
 
 
 def turn(value, axis, by):
@@ -166,18 +175,21 @@
     near = spread_x(state_b.astype(jnp.bfloat16))
     whole = lax.all_gather(state_a.astype(jnp.bfloat16), COL, axis=0, tiled=True)
     for iteration in range(STEPS):
+        last = iteration + 1 == STEPS
+        own_a, send_a = products(src, dst, place, [after(whole, *near)], blocks, span)
+        near = after(near, send_a)
         far = [turn(piece, "core", 1) for piece in near]
-        state_b = state_b + reduce_rows(*products(src, dst, place, near + far, blocks, span))
+        own_b, send_b = products(src, dst, place, near + far, blocks, span)
+        state_a = state_a + reduce_rows(own_a, send_a)
+        sum_a = sum_a + weights[iteration + 1] * reward_f * state_a
+        if not last:
+            low_a = state_a.astype(jnp.bfloat16)
+            low_a, send_b = lax.optimization_barrier((low_a, send_b))
+            whole = lax.all_gather(low_a, COL, axis=0, tiled=True)
+        state_b = state_b + reduce_rows(own_b, send_b)
         sum_b = sum_b + weights[iteration + 1] * reward_f * state_b
-        if iteration + 1 < STEPS:
+        if not last:
             near = spread_x(state_b.astype(jnp.bfloat16))
-            whole = after(whole, near[0])
-        state_a = state_a + reduce_rows(*products(src, dst, place, [whole], blocks, span))
-        sum_a = sum_a + weights[iteration + 1] * reward_f * state_a
-        if iteration + 1 < STEPS:
-            low_a = state_a.astype(jnp.bfloat16)
-            low_a, *near = lax.optimization_barrier((low_a, *near))
-            whole = lax.all_gather(low_a, COL, axis=0, tiled=True)
     return (
         jnp.concatenate([state_a, state_b], axis=1),
         jnp.concatenate([sum_a, sum_b], axis=1),

time: 368 us -> 347 us (0.943)
  waiting for transfers between devices: 162 us -> 145 us
  starting transfers between devices: 69.3 us -> 63.7 us
    all_gather x2, waiting for transfers between devices: 46.1 us -> 0.01 us  [shards(): whole = lax.all_gather(low_a, COL, axis=0, tiled=True)]
    ppermute x30, waiting for transfers between devices: 78.7 us -> 112 us  [turn(): return lax.ppermute(value, axis, [(i, (i + by) % n) for i in range(n)])]
    all_to_all x4, waiting for transfers between devices: 37.5 us -> 14.2 us  [reduce_rows(): got = lax.all_to_all(send, ROW, 0, 0, tiled=True)]
    all_gather x1, waiting for transfers between devices: 0.02 us -> 18.8 us  [shards(): lax.all_gather(state_a.astype(jnp.bfloat16), COL, axis=0, tiled=True)]
    ppermute x30, starting transfers between devices: 47 us -> 41.8 us  [turn(): return lax.ppermute(value, axis, [(i, (i + by) % n) for i in range(n)])]
  transfers between devices with their start and end apart: 37 -> 37, of which waited for: 25 -> 24; matrix products, arithmetic and copies ran while one was open for 1% -> 1% of each run, Pallas kernels for 12% -> 10%
where the time goes in v4:
time: 347 us; the launch traced here: 346 us
  waiting for transfers between devices  145 us (42%)
  Pallas kernels  64 us (18%)
  starting transfers between devices  63.7 us (18%)
  blocking collectives  45.2 us (13%)
  between operations  14.9 us (4%)
  local copies, waits for them, and re-layouts  6.88 us (2%)
  other arithmetic  6.03 us (2%)
    ppermute x30, waiting for transfers between devices, turn(): return lax.ppermute(value, axis, [(i, (i + by) % n) for i in range(n)])  112 us
    pallas_call x6, Pallas kernels, products(): pl.pallas_call(body, out_shape=[jax.ShapeDtypeStruct(piece, jnp.float32),...  64 us
    all_to_all x2, blocking collectives, reduce_rows(): got = lax.all_to_all(send, ROW, 0, 0, tiled=True)  45.2 us
    ppermute x30, starting transfers between devices, turn(): return lax.ppermute(value, axis, [(i, (i + by) % n) for i in range(n)])  41.8 us
    all_to_all x4, starting transfers between devices, reduce_rows(): got = lax.all_to_all(send, ROW, 0, 0, tiled=True)  21.7 us
    all_gather x1, waiting for transfers between devices, shards(): lax.all_gather(state_a.astype(jnp.bfloat16), COL, axis=0, tiled=True)  18.8 us
    all_to_all x4, waiting for transfers between devices, reduce_rows(): got = lax.all_to_all(send, ROW, 0, 0, tiled=True)  14.2 us
  transfers between devices with their start and end apart: 37, of which 24 were waited for; matrix products, arithmetic and copies ran while one was open for 1% of the time, Pallas kernels for 10%

profile of v4, /device:TPU:1, one launch (start us, length us, event | category | flops | bytes accessed | tf_op | source)
XLA Modules:
  0.0 345.7 jit_solution(12212402886817706030)
XLA Ops:
  7.2 1.7 fusion.4
  9.0 3.9 %collective-permute-start = (bf16[16,32,128]{2,1,0:T(8,128)(2,1)S(1)}, bf16[16,32,128]{2,1,0:T(8,128)(2,1)S(1)}, u32[]{:S(2)}, u32[]{:S(2)}) collective-permute-start(bf16[16,32,128]{2,1,0:T(8,128)(2,1)S(1)} %get-tuple-element.79), channel_id=1, source_target_pairs={{0,2},{2,4},{4,6},{6,0},{1,3},{3,5},{5,7},{7,1},{8,10},{10,12},{12... | collective-permute-start | bytes 393224 | tf_op jit(solution)/shard_map/ppermute | solution.py:138
  12.9 3.1 collective-permute-start.1
  16.0 4.4 %collective-permute-start.2 = (bf16[16,32,128]{2,1,0:T(8,128)(2,1)S(1)}, bf16[16,32,128]{2,1,0:T(8,128)(2,1)S(1)}, u32[]{:S(2)}, u32[]{:S(2)}) collective-permute-start(bf16[16,32,128]{2,1,0:T(8,128)(2,1)S(1)} %get-tuple-element.79), channel_id=1, source_target_pairs={{0,4},{2,6},{4,0},{6,2},{1,5},{3,7},{5,1},{7,3},{8,12},{10,14},{12... | collective-permute-start | bytes 393224 | tf_op jit(solution)/shard_map/ppermute | solution.py:138
  20.4 6.1 %collective-permute-done.1 = bf16[16,32,128]{2,1,0:T(8,128)(2,1)S(1)} collective-permute-done((bf16[16,32,128]{2,1,0:T(8,128)(2,1)S(1)}, bf16[16,32,128]{2,1,0:T(8,128)(2,1)S(1)}, u32[]{:S(2)}, u32[]{:S(2)}) %collective-permute-start.1) | collective-permute-done | bytes 131104 | tf_op jit(solution)/shard_map/ppermute | solution.py:138
  26.5 1.8 collective-permute-done.2
  28.4 1.3 collective-permute-start.3
  29.7 1.5 collective-permute-start.4
  31.1 1.5 collective-permute-start.5
  33.3 10.4 %collective-permute-done.3.refs_1_ = bf16[64,32,128]{2,1,0:T(8,128)(2,1)S(1)} collective-permute-done((bf16[64,32,128]{2,1,0:T(8,128)(2,1)S(1)}, bf16[64,32,128]{2,1,0:T(8,128)(2,1)S(1)}, u32[]{:S(2)}, u32[]{:S(2)}) %collective-permute-start.3) | collective-permute-done | bytes 524320 | tf_op jit(solution)/shard_map/ppermute | solution.py:138
  43.8 13.0 %collective-permute-done.5.refs_3_ = bf16[64,32,128]{2,1,0:T(8,128)(2,1)S(1)} collective-permute-done((bf16[64,32,128]{2,1,0:T(8,128)(2,1)S(1)}, bf16[64,32,128]{2,1,0:T(8,128)(2,1)S(1)}, u32[]{:S(2)}, u32[]{:S(2)}) %collective-permute-start.5) | collective-permute-done | bytes 524320 | tf_op jit(solution)/shard_map/ppermute | solution.py:138
  56.8 18.8 %all-gather.4.cloned.1.call-done.x_ref = bf16[512,32,128]{2,1,0:T(8,128)(2,1)} async-done(((bf16[16,32,128]{2,1,0:T(8,128)(2,1)}), bf16[512,32,128]{2,1,0:T(8,128)(2,1)}) %all-gather.4.cloned.1.call-update) | async-done | bytes 4194320 | tf_op jit(solution)/shard_map/all_gather | solution.py:176
  75.6 9.9 %products.6 = (f32[16,32,128]{2,1,0:T(8,128)}, bf16[128,32,128]{2,1,0:T(8,128)(2,1)}) custom-call(s32[256]{0:T(256)} %bitcast.87, s32[256]{0:T(256)} %bitcast.93, s32[33]{0:T(128)} %stack.135.place, bf16[512,32,128]{2,1,0:T(8,128)(2,1)} %all-gather.4.cloned.1.call-done.x_ref, bf16[256,128,128]{2,1,0:T(8,128)(2,1)} %bitcast.57, ...), custom_call_target="tpu_custom_call" | custom-call | flops 268435456 | bytes 13631488 | tf_op jit(solution)/shard_map/products/pallas_call | solution.py:116
  85.4 3.9 %all-to-all-start = ((bf16[128,32,128]{2,1,0:T(8,128)(2,1)}), bf16[128,32,128]{2,1,0:T(8,128)(2,1)S(1)}, u32[]{:S(2)}, u32[]{:S(2)}) async-start(bf16[128,32,128]{2,1,0:T(8,128)(2,1)} %get-tuple-element.35), calls=%async_computation | async-start | bytes 2097152 | tf_op jit(solution)/shard_map/all_to_all | solution.py:151
  91.6 1.5 collective-permute-done.7.refs_5_
  94.7 11.4 %products.7 = (f32[16,32,128]{2,1,0:T(8,128)}, bf16[128,32,128]{2,1,0:T(8,128)(2,1)}) custom-call(s32[256]{0:T(256)} %bitcast.88, s32[256]{0:T(256)} %bitcast.94, s32[33]{0:T(128)} %stack.135.place, bf16[64,32,128]{2,1,0:T(8,128)(2,1)} %copy-done.1, bf16[64,32,128]{2,1,0:T(8,128)(2,1)} %copy-done.5, bf16[64,32,128]{2,1,0:T(8,128)(2,1)} %copy-done.6, ...), custom_call_target="tpu_custom_call" | custom-call | flops 268435456 | bytes 13631488 | tf_op jit(solution)/shard_map/products/pallas_call | solution.py:116
  107.4 22.3 %all_to_all.30 = bf16[128,32,128]{2,1,0:T(8,128)(2,1)S(1)} all-to-all(bf16[128,32,128]{2,1,0:T(8,128)(2,1)S(1)} %copy-done.4), channel_id=1, replica_groups=mesh['y'=4,'zl'=2,'x'=4,'zh'=4,'core'=2] {'y','zl'}, dimensions={0} | all-to-all | bytes 2097152 | tf_op jit(solution)/shard_map/all_to_all | solution.py:151
  130.7 2.9 collective-permute-start.11
  133.6 2.5 collective-permute-start.12
  136.1 2.8 collective-permute-done.10
  139.1 3.6 %collective-permute-done.12 = bf16[16,32,128]{2,1,0:T(8,128)(2,1)S(1)} collective-permute-done((bf16[16,32,128]{2,1,0:T(8,128)(2,1)S(1)}, bf16[16,32,128]{2,1,0:T(8,128)(2,1)S(1)}, u32[]{:S(2)}, u32[]{:S(2)}) %collective-permute-start.12) | collective-permute-done | bytes 131104 | tf_op jit(solution)/shard_map/ppermute | solution.py:138
  143.8 2.8 collective-permute-start.14
  146.6 1.1 collective-permute-start.15
  147.7 18.4 %collective-permute-done.13.refs_1_ = bf16[64,32,128]{2,1,0:T(8,128)(2,1)S(1)} collective-permute-done((bf16[64,32,128]{2,1,0:T(8,128)(2,1)S(1)}, bf16[64,32,128]{2,1,0:T(8,128)(2,1)S(1)}, u32[]{:S(2)}, u32[]{:S(2)}) %collective-permute-start.13) | collective-permute-done | bytes 524320 | tf_op jit(solution)/shard_map/ppermute | solution.py:138
  166.1 10.2 %collective-permute-done.15.refs_3_ = bf16[64,32,128]{2,1,0:T(8,128)(2,1)S(1)} collective-permute-done((bf16[64,32,128]{2,1,0:T(8,128)(2,1)S(1)}, bf16[64,32,128]{2,1,0:T(8,128)(2,1)S(1)}, u32[]{:S(2)}, u32[]{:S(2)}) %collective-permute-start.15) | collective-permute-done | bytes 524320 | tf_op jit(solution)/shard_map/ppermute | solution.py:138
  176.4 9.9 %products.8 = (f32[16,32,128]{2,1,0:T(8,128)}, bf16[128,32,128]{2,1,0:T(8,128)(2,1)}) custom-call(s32[256]{0:T(256)} %bitcast.89, s32[256]{0:T(256)} %bitcast.95, s32[33]{0:T(128)} %stack.135.place, bf16[512,32,128]{2,1,0:T(8,128)(2,1)} %all-gather.6.cloned.1.call-done.x_ref, bf16[256,128,128]{2,1,0:T(8,128)(2,1)} %bitcast.68, ...), custom_call_target="tpu_custom_call" | custom-call | flops 268435456 | bytes 13631488 | tf_op jit(solution)/shard_map/products/pallas_call | solution.py:116
  186.3 5.4 %all-to-all-start.2 = ((bf16[128,32,128]{2,1,0:T(8,128)(2,1)}), bf16[128,32,128]{2,1,0:T(8,128)(2,1)S(1)}, u32[]{:S(2)}, u32[]{:S(2)}) async-start(bf16[128,32,128]{2,1,0:T(8,128)(2,1)} %get-tuple-element.46), calls=%async_computation.2 | async-start | bytes 2097152 | tf_op jit(solution)/shard_map/all_to_all | solution.py:151
  191.8 2.3 collective-permute-start.16
  195.6 2.2 collective-permute-done.17.refs_5_
  199.4 11.4 %products.9 = (f32[16,32,128]{2,1,0:T(8,128)}, bf16[128,32,128]{2,1,0:T(8,128)(2,1)}) custom-call(s32[256]{0:T(256)} %bitcast.90, s32[256]{0:T(256)} %bitcast.96, s32[33]{0:T(128)} %stack.135.place, bf16[64,32,128]{2,1,0:T(8,128)(2,1)} %copy-done.2, bf16[64,32,128]{2,1,0:T(8,128)(2,1)} %copy-done.8, bf16[64,32,128]{2,1,0:T(8,128)(2,1)} %copy-done.10, ...), custom_call_target="tpu_custom_call" | custom-call | flops 268435456 | bytes 13631488 | tf_op jit(solution)/shard_map/products/pallas_call | solution.py:116
  211.9 22.8 %all_to_all.31 = bf16[128,32,128]{2,1,0:T(8,128)(2,1)S(1)} all-to-all(bf16[128,32,128]{2,1,0:T(8,128)(2,1)} %get-tuple-element.54), channel_id=1, replica_groups=mesh['y'=4,'zl'=2,'x'=4,'zh'=4,'core'=2] {'y','zl'}, dimensions={0} | all-to-all | bytes 2097152 | tf_op jit(solution)/shard_map/all_to_all | solution.py:151
  235.6 3.6 %collective-permute-start.21 = (bf16[16,32,128]{2,1,0:T(8,128)(2,1)S(1)}, bf16[16,32,128]{2,1,0:T(8,128)(2,1)S(1)}, u32[]{:S(2)}, u32[]{:S(2)}) collective-permute-start(bf16[16,32,128]{2,1,0:T(8,128)(2,1)S(1)} %get-tuple-element.68), channel_id=1, source_target_pairs={{0,6},{2,0},{4,2},{6,4},{1,7},{3,1},{5,3},{7,5},{8,14},{10,8},{12,... | collective-permute-start | bytes 393224 | tf_op jit(solution)/shard_map/ppermute | solution.py:138
  239.2 2.0 collective-permute-start.22
  242.5 5.4 %collective-permute-done.22 = bf16[16,32,128]{2,1,0:T(8,128)(2,1)S(1)} collective-permute-done((bf16[16,32,128]{2,1,0:T(8,128)(2,1)S(1)}, bf16[16,32,128]{2,1,0:T(8,128)(2,1)S(1)}, u32[]{:S(2)}, u32[]{:S(2)}) %collective-permute-start.22) | collective-permute-done | bytes 131104 | tf_op jit(solution)/shard_map/ppermute | solution.py:138
  248.0 1.1 collective-permute-start.23
  249.1 1.7 collective-permute-start.24
  251.1 17.6 %collective-permute-done.23.refs_1_ = bf16[64,32,128]{2,1,0:T(8,128)(2,1)S(1)} collective-permute-done((bf16[64,32,128]{2,1,0:T(8,128)(2,1)S(1)}, bf16[64,32,128]{2,1,0:T(8,128)(2,1)S(1)}, u32[]{:S(2)}, u32[]{:S(2)}) %collective-permute-start.23) | collective-permute-done | bytes 524320 | tf_op jit(solution)/shard_map/ppermute | solution.py:138
  268.8 1.3 collective-permute-done.24.refs_2_
  270.1 11.2 %collective-permute-done.25.refs_3_ = bf16[64,32,128]{2,1,0:T(8,128)(2,1)S(1)} collective-permute-done((bf16[64,32,128]{2,1,0:T(8,128)(2,1)S(1)}, bf16[64,32,128]{2,1,0:T(8,128)(2,1)S(1)}, u32[]{:S(2)}, u32[]{:S(2)}) %collective-permute-start.25) | collective-permute-done | bytes 524320 | tf_op jit(solution)/shard_map/ppermute | solution.py:138
  281.3 9.9 %products.10 = (f32[16,32,128]{2,1,0:T(8,128)}, bf16[128,32,128]{2,1,0:T(8,128)(2,1)}) custom-call(s32[256]{0:T(256)} %bitcast.91, s32[256]{0:T(256)} %bitcast.97, s32[33]{0:T(128)} %stack.135.place, bf16[512,32,128]{2,1,0:T(8,128)(2,1)} %all-gather.8.cloned.1.call-done.x_ref, bf16[256,128,128]{2,1,0:T(8,128)(2,1)} %bitcast.73, ...), custom_call_target="tpu_custom_call" | custom-call | flops 268435456 | bytes 13631488 | tf_op jit(solution)/shard_map/products/pallas_call | solution.py:116
  291.2 7.1 %all-to-all-start.4 = ((bf16[128,32,128]{2,1,0:T(8,128)(2,1)}), bf16[128,32,128]{2,1,0:T(8,128)(2,1)S(1)}, u32[]{:S(2)}, u32[]{:S(2)}) async-start(bf16[128,32,128]{2,1,0:T(8,128)(2,1)} %get-tuple-element.57), calls=%async_computation.4 | async-start | bytes 2097152 | tf_op jit(solution)/shard_map/all_to_all | solution.py:151
  298.3 1.4 collective-permute-start.26
  301.2 1.5 collective-permute-done.27.refs_5_
  304.3 11.5 %products.11 = (f32[16,32,128]{2,1,0:T(8,128)}, bf16[128,32,128]{2,1,0:T(8,128)(2,1)}) custom-call(s32[256]{0:T(256)} %bitcast.92, s32[256]{0:T(256)} %bitcast.98, s32[33]{0:T(128)} %stack.135.place, bf16[64,32,128]{2,1,0:T(8,128)(2,1)} %copy-done.3, bf16[64,32,128]{2,1,0:T(8,128)(2,1)} %copy-done.9, bf16[64,32,128]{2,1,0:T(8,128)(2,1)} %copy-done.11, ...), custom_call_target="tpu_custom_call" | custom-call | flops 268435456 | bytes 13631488 | tf_op jit(solution)/shard_map/products/pallas_call | solution.py:116
  315.9 5.3 %all-to-all-start.5 = ((bf16[128,32,128]{2,1,0:T(8,128)(2,1)}), bf16[128,32,128]{2,1,0:T(8,128)(2,1)S(1)}, u32[]{:S(2)}, u32[]{:S(2)}) async-start(bf16[128,32,128]{2,1,0:T(8,128)(2,1)} %get-tuple-element.63), calls=%async_computation.5 | async-start | bytes 2097152 | tf_op jit(solution)/shard_map/all_to_all | solution.py:151
  322.3 14.2 %all-to-all-done.5 = bf16[128,32,128]{2,1,0:T(8,128)(2,1)S(1)} async-done(((bf16[128,32,128]{2,1,0:T(8,128)(2,1)}), bf16[128,32,128]{2,1,0:T(8,128)(2,1)S(1)}, u32[]{:S(2)}, u32[]{:S(2)}) %all-to-all-start.5) | async-done | bytes 1048608 | tf_op jit(solution)/shard_map/all_to_all | solution.py:151
  336.6 1.5 multiply_add_fusion.1
  338.1 1.1 pad_maximum_fusion.3
  (111 shorter events, 18.4 us)
Async XLA Ops:
  7.2 68.4 %all-gather.4.cloned.1.call-start = ((), (), s32[]{:S(2)}) async-start(), calls=%async_computation.6 | async-start | bytes 4325376 | tf_op jit(solution)/shard_map/all_gather | solution.py:176
  9.0 11.4 %collective-permute-start = (bf16[16,32,128]{2,1,0:T(8,128)(2,1)S(1)}, bf16[16,32,128]{2,1,0:T(8,128)(2,1)S(1)}, u32[]{:S(2)}, u32[]{:S(2)}) collective-permute-start(bf16[16,32,128]{2,1,0:T(8,128)(2,1)S(1)} %get-tuple-element.79), channel_id=1, source_target_pairs={{0,2},{2,4},{4,6},{6,0},{1,3},{3,5},{5,7},{7,1},{8,10},{10,12},{12... | collective-permute-start | bytes 393224 | tf_op jit(solution)/shard_map/ppermute | solution.py:138
  12.9 13.6 %collective-permute-start.1 = (bf16[16,32,128]{2,1,0:T(8,128)(2,1)S(1)}, bf16[16,32,128]{2,1,0:T(8,128)(2,1)S(1)}, u32[]{:S(2)}, u32[]{:S(2)}) collective-permute-start(bf16[16,32,128]{2,1,0:T(8,128)(2,1)S(1)} %get-tuple-element.79), channel_id=1, source_target_pairs={{0,6},{2,0},{4,2},{6,4},{1,7},{3,1},{5,3},{7,5},{8,14},{10,8},{12,... | collective-permute-start | bytes 393224 | tf_op jit(solution)/shard_map/ppermute | solution.py:138
  16.0 12.3 %collective-permute-start.2 = (bf16[16,32,128]{2,1,0:T(8,128)(2,1)S(1)}, bf16[16,32,128]{2,1,0:T(8,128)(2,1)S(1)}, u32[]{:S(2)}, u32[]{:S(2)}) collective-permute-start(bf16[16,32,128]{2,1,0:T(8,128)(2,1)S(1)} %get-tuple-element.79), channel_id=1, source_target_pairs={{0,4},{2,6},{4,0},{6,2},{1,5},{3,7},{5,1},{7,3},{8,12},{10,14},{12... | collective-permute-start | bytes 393224 | tf_op jit(solution)/shard_map/ppermute | solution.py:138
  28.4 61.0 %copy-start.1 = (bf16[64,32,128]{2,1,0:T(8,128)(2,1)}, bf16[64,32,128]{2,1,0:T(8,128)(2,1)S(1)}, u32[]{:S(2)}) copy-start(bf16[64,32,128]{2,1,0:T(8,128)(2,1)S(1)} %pad_maximum_fusion.refs_0_) | copy-start | bytes 1572868
  28.4 15.4 %collective-permute-start.3 = (bf16[64,32,128]{2,1,0:T(8,128)(2,1)S(1)}, bf16[64,32,128]{2,1,0:T(8,128)(2,1)S(1)}, u32[]{:S(2)}, u32[]{:S(2)}) collective-permute-start(bf16[64,32,128]{2,1,0:T(8,128)(2,1)S(1)} %pad_maximum_fusion.refs_0_), channel_id=1, source_target_pairs={{0,8},{8,16},{16,24},{24,0},{1,9},{9,17},{17,25},{25,1},{2,10},{10... | collective-permute-start | bytes 1572872 | tf_op jit(solution)/shard_map/ppermute | solution.py:138
  29.7 14.1 %collective-permute-start.4 = (bf16[64,32,128]{2,1,0:T(8,128)(2,1)S(1)}, bf16[64,32,128]{2,1,0:T(8,128)(2,1)S(1)}, u32[]{:S(2)}, u32[]{:S(2)}) collective-permute-start(bf16[64,32,128]{2,1,0:T(8,128)(2,1)S(1)} %pad_maximum_fusion.refs_0_), channel_id=1, source_target_pairs={{0,24},{8,0},{16,8},{24,16},{1,25},{9,1},{17,9},{25,17},{2,26},{10... | collective-permute-start | bytes 1572872 | tf_op jit(solution)/shard_map/ppermute | solution.py:138
  31.1 25.6 %collective-permute-start.5 = (bf16[64,32,128]{2,1,0:T(8,128)(2,1)S(1)}, bf16[64,32,128]{2,1,0:T(8,128)(2,1)S(1)}, u32[]{:S(2)}, u32[]{:S(2)}) collective-permute-start(bf16[64,32,128]{2,1,0:T(8,128)(2,1)S(1)} %pad_maximum_fusion.refs_0_), channel_id=1, source_target_pairs={{0,16},{8,24},{16,0},{24,8},{1,17},{9,25},{17,1},{25,9},{2,18},{10... | collective-permute-start | bytes 1572872 | tf_op jit(solution)/shard_map/ppermute | solution.py:138
  43.7 46.3 %copy-start.5 = (bf16[64,32,128]{2,1,0:T(8,128)(2,1)}, bf16[64,32,128]{2,1,0:T(8,128)(2,1)S(1)}, u32[]{:S(2)}) copy-start(bf16[64,32,128]{2,1,0:T(8,128)(2,1)S(1)} %collective-permute-done.3.refs_1_) | copy-start | bytes 1572868
  43.8 46.4 %copy-start.6 = (bf16[64,32,128]{2,1,0:T(8,128)(2,1)}, bf16[64,32,128]{2,1,0:T(8,128)(2,1)S(1)}, u32[]{:S(2)}) copy-start(bf16[64,32,128]{2,1,0:T(8,128)(2,1)S(1)} %collective-permute-done.4.refs_2_) | copy-start | bytes 1572868
  56.8 28.7 %copy-start.7 = (bf16[64,32,128]{2,1,0:T(8,128)(2,1)}, bf16[64,32,128]{2,1,0:T(8,128)(2,1)S(1)}, u32[]{:S(2)}) copy-start(bf16[64,32,128]{2,1,0:T(8,128)(2,1)S(1)} %collective-permute-done.5.refs_3_) | copy-start | bytes 1572868
  85.4 20.7 %all-to-all-start = ((bf16[128,32,128]{2,1,0:T(8,128)(2,1)}), bf16[128,32,128]{2,1,0:T(8,128)(2,1)S(1)}, u32[]{:S(2)}, u32[]{:S(2)}) async-start(bf16[128,32,128]{2,1,0:T(8,128)(2,1)} %get-tuple-element.35), calls=%async_computation | async-start | bytes 2097152 | tf_op jit(solution)/shard_map/all_to_all | solution.py:151
  89.4 87.0 %all-gather.6.cloned.1.call-start = ((), (), s32[]{:S(2)}) async-start(), calls=%async_computation.7 | async-start | bytes 4325376 | tf_op jit(solution)/shard_map/all_gather | solution.py:188
  89.4 2.2 collective-permute-start.6
  90.0 3.0 collective-permute-start.7
  90.1 3.7 %collective-permute-start.8 = (bf16[64,32,128]{2,1,0:T(8,128)(2,1)S(1)}, bf16[64,32,128]{2,1,0:T(8,128)(2,1)S(1)}, u32[]{:S(2)}, u32[]{:S(2)}) collective-permute-start(bf16[64,32,128]{2,1,0:T(8,128)(2,1)S(1)} %collective-permute-done.4.refs_2_), channel_id=1, source_target_pairs={{0,1},{1,0},{2,3},{3,2},{4,5},{5,4},{6,7},{7,6},{8,9},{9,8},{10,11... | collective-permute-start | bytes 1572872 | tf_op jit(solution)/shard_map/ppermute | solution.py:138
  90.5 4.1 %collective-permute-start.9 = (bf16[64,32,128]{2,1,0:T(8,128)(2,1)}, bf16[64,32,128]{2,1,0:T(8,128)(2,1)}, u32[]{:S(2)}, u32[]{:S(2)}) collective-permute-start(bf16[64,32,128]{2,1,0:T(8,128)(2,1)} %copy-done.7), channel_id=1, source_target_pairs={{0,1},{1,0},{2,3},{3,2},{4,5},{5,4},{6,7},{7,6},{8,9},{9,8},{10,11... | collective-permute-start | bytes 1572872 | tf_op jit(solution)/shard_map/ppermute | solution.py:138
  106.3 23.6 %copy-start.26 = (f32[16,32,128]{2,1,0:T(8,128)S(1)}, f32[16,32,128]{2,1,0:T(8,128)}, u32[]{:S(2)}) copy-start(f32[16,32,128]{2,1,0:T(8,128)} %get-tuple-element.42) | copy-start | bytes 786436
  130.0 8.9 %collective-permute-start.10 = (bf16[16,32,128]{2,1,0:T(8,128)(2,1)S(1)}, bf16[16,32,128]{2,1,0:T(8,128)(2,1)S(1)}, u32[]{:S(2)}, u32[]{:S(2)}) collective-permute-start(bf16[16,32,128]{2,1,0:T(8,128)(2,1)S(1)} %get-tuple-element.72), channel_id=1, source_target_pairs={{0,2},{2,4},{4,6},{6,0},{1,3},{3,5},{5,7},{7,1},{8,10},{10,12},{12... | collective-permute-start | bytes 393224 | tf_op jit(solution)/shard_map/ppermute | solution.py:138
  130.7 8.4 %collective-permute-start.11 = (bf16[16,32,128]{2,1,0:T(8,128)(2,1)S(1)}, bf16[16,32,128]{2,1,0:T(8,128)(2,1)S(1)}, u32[]{:S(2)}, u32[]{:S(2)}) collective-permute-start(bf16[16,32,128]{2,1,0:T(8,128)(2,1)S(1)} %get-tuple-element.72), channel_id=1, source_target_pairs={{0,6},{2,0},{4,2},{6,4},{1,7},{3,1},{5,3},{7,5},{8,14},{10,8},{12,... | collective-permute-start | bytes 393224 | tf_op jit(solution)/shard_map/ppermute | solution.py:138
  133.6 9.1 %collective-permute-start.12 = (bf16[16,32,128]{2,1,0:T(8,128)(2,1)S(1)}, bf16[16,32,128]{2,1,0:T(8,128)(2,1)S(1)}, u32[]{:S(2)}, u32[]{:S(2)}) collective-permute-start(bf16[16,32,128]{2,1,0:T(8,128)(2,1)S(1)} %get-tuple-element.72), channel_id=1, source_target_pairs={{0,4},{2,6},{4,0},{6,2},{1,5},{3,7},{5,1},{7,3},{8,12},{10,14},{12... | collective-permute-start | bytes 393224 | tf_op jit(solution)/shard_map/ppermute | solution.py:138
  142.8 48.9 %copy-start.2 = (bf16[64,32,128]{2,1,0:T(8,128)(2,1)}, bf16[64,32,128]{2,1,0:T(8,128)(2,1)S(1)}, u32[]{:S(2)}) copy-start(bf16[64,32,128]{2,1,0:T(8,128)(2,1)S(1)} %pad_maximum_fusion.1.refs_0_) | copy-start | bytes 1572868
  142.8 23.3 %collective-permute-start.13 = (bf16[64,32,128]{2,1,0:T(8,128)(2,1)S(1)}, bf16[64,32,128]{2,1,0:T(8,128)(2,1)S(1)}, u32[]{:S(2)}, u32[]{:S(2)}) collective-permute-start(bf16[64,32,128]{2,1,0:T(8,128)(2,1)S(1)} %pad_maximum_fusion.1.refs_0_), channel_id=1, source_target_pairs={{0,8},{8,16},{16,24},{24,0},{1,9},{9,17},{17,25},{25,1},{2,10},{10... | collective-permute-start | bytes 1572872 | tf_op jit(solution)/shard_map/ppermute | solution.py:138
  143.8 22.3 %collective-permute-start.14 = (bf16[64,32,128]{2,1,0:T(8,128)(2,1)S(1)}, bf16[64,32,128]{2,1,0:T(8,128)(2,1)S(1)}, u32[]{:S(2)}, u32[]{:S(2)}) collective-permute-start(bf16[64,32,128]{2,1,0:T(8,128)(2,1)S(1)} %pad_maximum_fusion.1.refs_0_), channel_id=1, source_target_pairs={{0,24},{8,0},{16,8},{24,16},{1,25},{9,1},{17,9},{25,17},{2,26},{10... | collective-permute-start | bytes 1572872 | tf_op jit(solution)/shard_map/ppermute | solution.py:138
  146.6 29.7 %collective-permute-start.15 = (bf16[64,32,128]{2,1,0:T(8,128)(2,1)S(1)}, bf16[64,32,128]{2,1,0:T(8,128)(2,1)S(1)}, u32[]{:S(2)}, u32[]{:S(2)}) collective-permute-start(bf16[64,32,128]{2,1,0:T(8,128)(2,1)S(1)} %pad_maximum_fusion.1.refs_0_), channel_id=1, source_target_pairs={{0,16},{8,24},{16,0},{24,8},{1,17},{9,25},{17,1},{25,9},{2,18},{10... | collective-permute-start | bytes 1572872 | tf_op jit(solution)/shard_map/ppermute | solution.py:138
  166.1 27.9 %copy-start.8 = (bf16[64,32,128]{2,1,0:T(8,128)(2,1)}, bf16[64,32,128]{2,1,0:T(8,128)(2,1)S(1)}, u32[]{:S(2)}) copy-start(bf16[64,32,128]{2,1,0:T(8,128)(2,1)S(1)} %collective-permute-done.13.refs_1_) | copy-start | bytes 1572868
  186.3 24.6 %all-to-all-start.2 = ((bf16[128,32,128]{2,1,0:T(8,128)(2,1)}), bf16[128,32,128]{2,1,0:T(8,128)(2,1)S(1)}, u32[]{:S(2)}, u32[]{:S(2)}) async-start(bf16[128,32,128]{2,1,0:T(8,128)(2,1)} %get-tuple-element.46), calls=%async_computation.2 | async-start | bytes 2097152 | tf_op jit(solution)/shard_map/all_to_all | solution.py:151
  191.7 89.6 %all-gather.8.cloned.1.call-start = ((), (), s32[]{:S(2)}) async-start(), calls=%async_computation.8 | async-start | bytes 4325376 | tf_op jit(solution)/shard_map/all_gather | solution.py:188
  191.8 3.8 %collective-permute-start.16 = (bf16[64,32,128]{2,1,0:T(8,128)(2,1)S(1)}, bf16[64,32,128]{2,1,0:T(8,128)(2,1)S(1)}, u32[]{:S(2)}, u32[]{:S(2)}) collective-permute-start(bf16[64,32,128]{2,1,0:T(8,128)(2,1)S(1)} %pad_maximum_fusion.1.refs_0_), channel_id=1, source_target_pairs={{0,1},{1,0},{2,3},{3,2},{4,5},{5,4},{6,7},{7,6},{8,9},{9,8},{10,11... | collective-permute-start | bytes 1572872 | tf_op jit(solution)/shard_map/ppermute | solution.py:138
  194.0 3.8 %collective-permute-start.17 = (bf16[64,32,128]{2,1,0:T(8,128)(2,1)S(1)}, bf16[64,32,128]{2,1,0:T(8,128)(2,1)S(1)}, u32[]{:S(2)}, u32[]{:S(2)}) collective-permute-start(bf16[64,32,128]{2,1,0:T(8,128)(2,1)S(1)} %collective-permute-done.13.refs_1_), channel_id=1, source_target_pairs={{0,1},{1,0},{2,3},{3,2},{4,5},{5,4},{6,7},{7,6},{8,9},{9,8},{10,11... | collective-permute-start | bytes 1572872 | tf_op jit(solution)/shard_map/ppermute | solution.py:138
  194.1 4.5 %collective-permute-start.18 = (bf16[64,32,128]{2,1,0:T(8,128)(2,1)}, bf16[64,32,128]{2,1,0:T(8,128)(2,1)S(1)}, u32[]{:S(2)}, u32[]{:S(2)}) collective-permute-start(bf16[64,32,128]{2,1,0:T(8,128)(2,1)} %copy-done.10), channel_id=1, source_target_pairs={{0,1},{1,0},{2,3},{3,2},{4,5},{5,4},{6,7},{7,6},{8,9},{9,8},{10,11... | collective-permute-start | bytes 1572872 | tf_op jit(solution)/shard_map/ppermute | solution.py:138
  194.5 4.9 %collective-permute-start.19 = (bf16[64,32,128]{2,1,0:T(8,128)(2,1)}, bf16[64,32,128]{2,1,0:T(8,128)(2,1)}, u32[]{:S(2)}, u32[]{:S(2)}) collective-permute-start(bf16[64,32,128]{2,1,0:T(8,128)(2,1)} %copy-done.12), channel_id=1, source_target_pairs={{0,1},{1,0},{2,3},{3,2},{4,5},{5,4},{6,7},{7,6},{8,9},{9,8},{10,11... | collective-permute-start | bytes 1572872 | tf_op jit(solution)/shard_map/ppermute | solution.py:138
  211.0 23.8 %copy-start.25 = (f32[16,32,128]{2,1,0:T(8,128)S(1)}, f32[16,32,128]{2,1,0:T(8,128)}, u32[]{:S(2)}) copy-start(f32[16,32,128]{2,1,0:T(8,128)} %get-tuple-element.53) | copy-start | bytes 786436
  235.6 5.9 %collective-permute-start.20 = (bf16[16,32,128]{2,1,0:T(8,128)(2,1)S(1)}, bf16[16,32,128]{2,1,0:T(8,128)(2,1)S(1)}, u32[]{:S(2)}, u32[]{:S(2)}) collective-permute-start(bf16[16,32,128]{2,1,0:T(8,128)(2,1)S(1)} %get-tuple-element.68), channel_id=1, source_target_pairs={{0,2},{2,4},{4,6},{6,0},{1,3},{3,5},{5,7},{7,1},{8,10},{10,12},{12... | collective-permute-start | bytes 393224 | tf_op jit(solution)/shard_map/ppermute | solution.py:138
  235.6 6.9 %collective-permute-start.21 = (bf16[16,32,128]{2,1,0:T(8,128)(2,1)S(1)}, bf16[16,32,128]{2,1,0:T(8,128)(2,1)S(1)}, u32[]{:S(2)}, u32[]{:S(2)}) collective-permute-start(bf16[16,32,128]{2,1,0:T(8,128)(2,1)S(1)} %get-tuple-element.68), channel_id=1, source_target_pairs={{0,6},{2,0},{4,2},{6,4},{1,7},{3,1},{5,3},{7,5},{8,14},{10,8},{12,... | collective-permute-start | bytes 393224 | tf_op jit(solution)/shard_map/ppermute | solution.py:138
  239.2 8.7 %collective-permute-start.22 = (bf16[16,32,128]{2,1,0:T(8,128)(2,1)S(1)}, bf16[16,32,128]{2,1,0:T(8,128)(2,1)S(1)}, u32[]{:S(2)}, u32[]{:S(2)}) collective-permute-start(bf16[16,32,128]{2,1,0:T(8,128)(2,1)S(1)} %get-tuple-element.68), channel_id=1, source_target_pairs={{0,4},{2,6},{4,0},{6,2},{1,5},{3,7},{5,1},{7,3},{8,12},{10,14},{12... | collective-permute-start | bytes 393224 | tf_op jit(solution)/shard_map/ppermute | solution.py:138
  248.0 50.2 %copy-start.3 = (bf16[64,32,128]{2,1,0:T(8,128)(2,1)}, bf16[64,32,128]{2,1,0:T(8,128)(2,1)S(1)}, u32[]{:S(2)}) copy-start(bf16[64,32,128]{2,1,0:T(8,128)(2,1)S(1)} %pad_maximum_fusion.2.refs_0_) | copy-start | bytes 1572868
  248.0 20.8 %collective-permute-start.23 = (bf16[64,32,128]{2,1,0:T(8,128)(2,1)S(1)}, bf16[64,32,128]{2,1,0:T(8,128)(2,1)S(1)}, u32[]{:S(2)}, u32[]{:S(2)}) collective-permute-start(bf16[64,32,128]{2,1,0:T(8,128)(2,1)S(1)} %pad_maximum_fusion.2.refs_0_), channel_id=1, source_target_pairs={{0,8},{8,16},{16,24},{24,0},{1,9},{9,17},{17,25},{25,1},{2,10},{10... | collective-permute-start | bytes 1572872 | tf_op jit(solution)/shard_map/ppermute | solution.py:138
  249.1 21.0 %collective-permute-start.24 = (bf16[64,32,128]{2,1,0:T(8,128)(2,1)S(1)}, bf16[64,32,128]{2,1,0:T(8,128)(2,1)S(1)}, u32[]{:S(2)}, u32[]{:S(2)}) collective-permute-start(bf16[64,32,128]{2,1,0:T(8,128)(2,1)S(1)} %pad_maximum_fusion.2.refs_0_), channel_id=1, source_target_pairs={{0,24},{8,0},{16,8},{24,16},{1,25},{9,1},{17,9},{25,17},{2,26},{10... | collective-permute-start | bytes 1572872 | tf_op jit(solution)/shard_map/ppermute | solution.py:138
  250.8 30.5 %collective-permute-start.25 = (bf16[64,32,128]{2,1,0:T(8,128)(2,1)S(1)}, bf16[64,32,128]{2,1,0:T(8,128)(2,1)S(1)}, u32[]{:S(2)}, u32[]{:S(2)}) collective-permute-start(bf16[64,32,128]{2,1,0:T(8,128)(2,1)S(1)} %pad_maximum_fusion.2.refs_0_), channel_id=1, source_target_pairs={{0,16},{8,24},{16,0},{24,8},{1,17},{9,25},{17,1},{25,9},{2,18},{10... | collective-permute-start | bytes 1572872 | tf_op jit(solution)/shard_map/ppermute | solution.py:138
  268.8 30.9 %copy-start.9 = (bf16[64,32,128]{2,1,0:T(8,128)(2,1)}, bf16[64,32,128]{2,1,0:T(8,128)(2,1)S(1)}, u32[]{:S(2)}) copy-start(bf16[64,32,128]{2,1,0:T(8,128)(2,1)S(1)} %collective-permute-done.23.refs_1_) | copy-start | bytes 1572868
  270.1 21.1 %copy-start.11 = (bf16[64,32,128]{2,1,0:T(8,128)(2,1)}, bf16[64,32,128]{2,1,0:T(8,128)(2,1)S(1)}, u32[]{:S(2)}) copy-start(bf16[64,32,128]{2,1,0:T(8,128)(2,1)S(1)} %collective-permute-done.24.refs_2_) | copy-start | bytes 1572868
  291.2 24.7 %all-to-all-start.4 = ((bf16[128,32,128]{2,1,0:T(8,128)(2,1)}), bf16[128,32,128]{2,1,0:T(8,128)(2,1)S(1)}, u32[]{:S(2)}, u32[]{:S(2)}) async-start(bf16[128,32,128]{2,1,0:T(8,128)(2,1)} %get-tuple-element.57), calls=%async_computation.4 | async-start | bytes 2097152 | tf_op jit(solution)/shard_map/all_to_all | solution.py:151
  298.3 3.0 collective-permute-start.26
  299.7 3.0 collective-permute-start.27
  300.0 3.5 %collective-permute-start.28 = (bf16[64,32,128]{2,1,0:T(8,128)(2,1)}, bf16[64,32,128]{2,1,0:T(8,128)(2,1)S(1)}, u32[]{:S(2)}, u32[]{:S(2)}) collective-permute-start(bf16[64,32,128]{2,1,0:T(8,128)(2,1)} %copy-done.11), channel_id=1, source_target_pairs={{0,1},{1,0},{2,3},{3,2},{4,5},{5,4},{6,7},{7,6},{8,9},{9,8},{10,11... | collective-permute-start | bytes 1572872 | tf_op jit(solution)/shard_map/ppermute | solution.py:138
  300.2 4.1 %collective-permute-start.29 = (bf16[64,32,128]{2,1,0:T(8,128)(2,1)}, bf16[64,32,128]{2,1,0:T(8,128)(2,1)}, u32[]{:S(2)}, u32[]{:S(2)}) collective-permute-start(bf16[64,32,128]{2,1,0:T(8,128)(2,1)} %copy-done.13), channel_id=1, source_target_pairs={{0,1},{1,0},{2,3},{3,2},{4,5},{5,4},{6,7},{7,6},{8,9},{9,8},{10,11... | collective-permute-start | bytes 1572872 | tf_op jit(solution)/shard_map/ppermute | solution.py:138
  315.9 20.5 %all-to-all-start.5 = ((bf16[128,32,128]{2,1,0:T(8,128)(2,1)}), bf16[128,32,128]{2,1,0:T(8,128)(2,1)S(1)}, u32[]{:S(2)}, u32[]{:S(2)}) async-start(bf16[128,32,128]{2,1,0:T(8,128)(2,1)} %get-tuple-element.63), calls=%async_computation.5 | async-start | bytes 2097152 | tf_op jit(solution)/shard_map/all_to_all | solution.py:151
  (17 other events, 115.6 us)
Sparse Core Ops, SparseCore 0:
  10.6 64.9 all-gather.3
  107.2 61.5 all-gather.5
  212.0 61.4 all-gather.7

commit v5 on v3

v5 whole, which is shorter than its diff:
```python
import jax
import jax.numpy as jnp
from jax import lax
from jax.experimental import pallas as pl
from jax.experimental.pallas import tpu as pltpu
from jax.sharding import Mesh, PartitionSpec as P

STEPS = 3
AXES = ("y", "zl", "x", "zh", "core")
SHAPE = (4, 2, 4, 4, 2)
ROW = ("y", "zl")
COL = ("x", "zh", "core")
GROUPS = 8
AHEAD = 3
TURNS = (0, 1, 3, 2)


def poisson_weights(horizon):
    rate_time = horizon[0]
    poisson_term = jnp.exp(-rate_time)
    cumulated = poisson_term
    weights = [(1.0 - cumulated) / rate_time]
    for iteration in range(STEPS):
        poisson_term = poisson_term * rate_time / (iteration + 1.0)
        cumulated = cumulated + poisson_term
        weights.append((1.0 - cumulated) / rate_time)
    return weights


def hand_out(place, own_ref, send_ref, acc):
    span = own_ref.shape[0]
    mine = pl.ds(place[0] * span, span)
    own_ref[...] = acc[mine]
    send_ref[...] = acc[...].astype(send_ref.dtype)
    send_ref[mine] = jnp.zeros(own_ref.shape, send_ref.dtype)


def whole_body(src, dst, place, given, blk, own_ref, send_ref, acc, held, sems, whole, more_sems):
    slots = held.shape[0] // GROUPS
    rows = whole.shape[0] // GROUPS

    def fetch(group):
        part = pl.ds(pl.multiple_of(group * rows, rows), rows)
        block = pl.ds(pl.multiple_of(group * slots, slots), slots)
        return (
            pltpu.make_async_copy(given.at[part], whole.at[part], more_sems.at[group]),
            pltpu.make_async_copy(blk.at[block], held.at[block], sems.at[group]),
        )

    for group in range(AHEAD):
        for copy in fetch(group):
            copy.start()
    acc[...] = jnp.zeros_like(acc)

    @pl.loop(0, GROUPS)
    def _(group):
        for copy in fetch(group):
            copy.wait()

        @pl.when(group + AHEAD < GROUPS)
        def _():
            for copy in fetch(group + AHEAD):
                copy.start()

        for slot in range(slots):
            at = group * slots + slot
            acc[dst[at]] += jnp.dot(whole[src[at]], held[at], preferred_element_type=jnp.float32)

    hand_out(place, own_ref, send_ref, acc)


def pieces_body(src, dst, place, *refs):
    pieces, (blk, own_ref, send_ref, acc, held, sems) = refs[:-6], refs[-6:]
    span = own_ref.shape[0]
    counts = [piece.shape[0] // span for piece in pieces]
    firsts = [sum(counts[:number]) for number in range(len(counts))]
    slots = held.shape[0] // sum(counts)

    def fetch(shard):
        there = pl.ds(pl.multiple_of(shard * slots, slots), slots)
        part = pl.ds(pl.multiple_of(place[1 + shard] * slots, slots), slots)
        return pltpu.make_async_copy(blk.at[part], held.at[there], sems.at[shard])

    ahead = 4 * AHEAD
    for shard in range(ahead):
        fetch(shard).start()
    acc[...] = jnp.zeros_like(acc)
    for first, count, piece in zip(firsts, counts, pieces):

        @pl.loop(0, count // 2)
        def _(pair):
            for one in range(2):
                at_z = pair * 2 + one
                fetch(first + at_z).wait()

                @pl.when(first + at_z + ahead < sum(counts))
                def _():
                    fetch(first + at_z + ahead).start()

                shard = place[1 + first + at_z]
                for slot in range(slots):
                    at = shard * slots + slot
                    row = src[at] + (at_z - shard) * span
                    block = held[(first + at_z) * slots + slot]
                    acc[dst[at]] += jnp.dot(piece[row], block, preferred_element_type=jnp.float32)

    hand_out(place, own_ref, send_ref, acc)


def products(src, dst, place, given, blocks, span):
    n, block_len, _ = blocks.shape
    configs = given[0].shape[1]
    targets = SHAPE[0] * SHAPE[1] * span
    sources = SHAPE[2] * SHAPE[3] * SHAPE[4] * span
    piece = (span, configs, block_len)
    send = (targets, configs, block_len)
    scratch = [pltpu.VMEM(send, jnp.float32), pltpu.VMEM(blocks.shape, blocks.dtype)]
    if len(given) == 1:
        body, where = whole_body, pltpu.HBM
        scratch += [pltpu.SemaphoreType.DMA((GROUPS,)), pltpu.VMEM((sources, configs, block_len), jnp.bfloat16)]
        scratch += [pltpu.SemaphoreType.DMA((GROUPS,))]
    else:
        body, where = pieces_body, pltpu.VMEM
        scratch += [pltpu.SemaphoreType.DMA((sources // span,))]
    given = [pltpu.with_memory_space_constraint(value, where) for value in given]
    blocks = pltpu.with_memory_space_constraint(blocks, pltpu.HBM)
    return pl.pallas_call(
        body,
        out_shape=[jax.ShapeDtypeStruct(piece, jnp.float32), jax.ShapeDtypeStruct(send, jnp.bfloat16)],
        grid_spec=pltpu.PrefetchScalarGridSpec(
            num_scalar_prefetch=3,
            grid=(1,),
            in_specs=[pl.BlockSpec(memory_space=where)] * len(given) + [pl.BlockSpec(memory_space=pltpu.HBM)],
            out_specs=[pl.BlockSpec(piece, lambda i, *_: (0, 0, 0)), pl.BlockSpec(send, lambda i, *_: (0, 0, 0))],
            scratch_shapes=scratch,
        ),
        compiler_params=pltpu.CompilerParams(vmem_limit_bytes=24 << 20),
        cost_estimate=pl.CostEstimate(
            flops=2 * n * configs * block_len * block_len,
            bytes_accessed=2 * (sources * configs * block_len + n * block_len * block_len),
            transcendentals=0,
        ),
        name="products",
    )(src, dst, place, *given, blocks)


def turn(value, axis, by):
    n = lax.axis_size(axis)
    return lax.ppermute(value, axis, [(i, (i + by) % n) for i in range(n)])


def after(values, *others):
    return lax.optimization_barrier((values, others))[0]


def spread_z(mine):
    return [mine] + [turn(mine, "zh", by) for by in TURNS[1:]]


def spread_x(column):
    return [column, turn(column, "x", 1), turn(column, "x", 3)]


def pass_on(near):
    half = near[0].shape[0] // 2
    near = near + [turn(near[1][:half], "x", 1), turn(near[2][half:], "x", 3)]
    return jnp.concatenate(near, axis=0)


def exchange_rows(send):
    return lax.all_to_all(send, ROW, 0, 0, tiled=True)


def add_rows(own, got):
    total = own
    for part in jnp.split(got, SHAPE[0] * SHAPE[1], axis=0):
        total = total + part.astype(jnp.float32)
    return total


def shards(x_init, gen_blocks, blk_src, blk_dst, reward, horizon):
    blocks = gen_blocks[0, 0]
    src = blk_src[0, 0]
    dst = blk_dst[0, 0]
    span = x_init.shape[0]
    half = x_init.shape[1] // 2
    weights = poisson_weights(horizon)
    reward_f = reward.astype(jnp.float32)[:, None, :]
    x, zh, core = (lax.axis_index(a) for a in COL)
    row = lax.axis_index("y") * SHAPE[1] + lax.axis_index("zl")
    place = [row]
    for other in range(2):
        for by_x in TURNS:
            for by_z in TURNS:
                place.append((((x - by_x) % 4) * 4 + (zh - by_z) % 4) * 2 + (core + other) % 2)
    place = jnp.stack(place).astype(jnp.int32)
    state_a, state_b = x_init[:, :half], x_init[:, half:]
    sum_a = weights[0] * reward_f * state_a
    sum_b = weights[0] * reward_f * state_b
    whole = lax.all_gather(state_a.astype(jnp.bfloat16), COL, axis=0, tiled=True)
    column = jnp.concatenate(spread_z(state_b.astype(jnp.bfloat16)), axis=0)
    near = spread_x(column)
    for iteration in range(STEPS):
        last = iteration + 1 == STEPS
        near = pass_on(near)
        own_b, send_b = products(src, dst, place, [near, turn(near, "core", 1)], blocks, span)
        state_b = state_b + add_rows(own_b, exchange_rows(send_b))
        sum_b = sum_b + weights[iteration + 1] * reward_f * state_b
        low_b = state_b.astype(jnp.bfloat16)
        whole = after(whole, low_b if iteration == 1 else send_b)
        own_a, send_a = products(src, dst, place, [whole], blocks, span)
        got_a = exchange_rows(send_a)
        if not last:
            column = jnp.concatenate(after(spread_z(low_b), send_a), axis=0)
            got_a = after(got_a, column)
        state_a = state_a + add_rows(own_a, got_a)
        sum_a = sum_a + weights[iteration + 1] * reward_f * state_a
        if not last:
            low_a = state_a.astype(jnp.bfloat16)
            whole = lax.all_gather(low_a, COL, axis=0, tiled=True)
            near = after(spread_x(column), low_a)
    return (
        jnp.concatenate([state_a, state_b], axis=1),
        jnp.concatenate([sum_a, sum_b], axis=1),
    )


def solution(mesh):
    fine = Mesh(mesh.devices.reshape(SHAPE), AXES)
    rc = P((*ROW, *COL), None, None)
    in_specs = (
        rc,
        P(ROW, COL, None, None, None),
        P(ROW, COL, None),
        P(ROW, COL, None),
        P((*ROW, *COL), None),
        P(),
    )
    return jax.shard_map(shards, mesh=fine, in_specs=in_specs, out_specs=(rc, rc), check_vma=False)
```

time: 368 us -> 334 us (0.908)
  waiting for transfers between devices: 162 us -> 142 us
  starting transfers between devices: 69.3 us -> 84.9 us
  Pallas kernels: 65.1 us -> 49.5 us
  blocking collectives: 45.2 us -> 31.6 us
    all_gather x2, waiting for transfers between devices: 46.1 us -> 21.1 us  [shards(): whole = lax.all_gather(low_a, COL, axis=0, tiled=True)]
    ppermute x30 -> x24, waiting for transfers between devices: 78.7 us -> 100 us  [turn(): return lax.ppermute(value, axis, [(i, (i + by) % n) for i in range(n)])]
    all_to_all x4 -> x5, waiting for transfers between devices: 37.5 us -> 20.4 us  [exchange_rows(): return lax.all_to_all(send, ROW, 0, 0, tiled=True)]
    pallas_call x6, Pallas kernels: 65.1 us -> 49.5 us  [products(): pl.pallas_call(body, out_shape=[jax.ShapeDtypeStruct(piece, jnp.float32),...]
    all_to_all x2 -> x1, blocking collectives: 45.2 us -> 31.6 us  [exchange_rows(): return lax.all_to_all(send, ROW, 0, 0, tiled=True)]
    ppermute x30 -> x24, starting transfers between devices: 47 us -> 58.7 us  [turn(): return lax.ppermute(value, axis, [(i, (i + by) % n) for i in range(n)])]
    all_to_all x4 -> x5, starting transfers between devices: 22.2 us -> 26 us  [exchange_rows(): return lax.all_to_all(send, ROW, 0, 0, tiled=True)]
  transfers between devices with their start and end apart: 37 -> 32, of which waited for: 25 -> 19; matrix products, arithmetic and copies ran while one was open for 1% -> 1% of each run, Pallas kernels for 12% -> 13%
where the time goes in v5:
time: 334 us; the launch traced here: 333 us
  waiting for transfers between devices  142 us (43%)
  starting transfers between devices  84.9 us (25%)
  Pallas kernels  49.5 us (15%)
  blocking collectives  31.6 us (9%)
  between operations  15.1 us (5%)
  other arithmetic  7.23 us (2%)
    ppermute x24, waiting for transfers between devices, turn(): return lax.ppermute(value, axis, [(i, (i + by) % n) for i in range(n)])  100 us
    ppermute x24, starting transfers between devices, turn(): return lax.ppermute(value, axis, [(i, (i + by) % n) for i in range(n)])  58.7 us
    pallas_call x6, Pallas kernels, products(): pl.pallas_call(body, out_shape=[jax.ShapeDtypeStruct(piece, jnp.float32),...  49.5 us
    all_to_all x1, blocking collectives, exchange_rows(): return lax.all_to_all(send, ROW, 0, 0, tiled=True)  31.6 us
    all_to_all x5, starting transfers between devices, exchange_rows(): return lax.all_to_all(send, ROW, 0, 0, tiled=True)  26 us
    all_gather x2, waiting for transfers between devices, shards(): whole = lax.all_gather(low_a, COL, axis=0, tiled=True)  21.1 us
    all_to_all x5, waiting for transfers between devices, exchange_rows(): return lax.all_to_all(send, ROW, 0, 0, tiled=True)  20.4 us
  transfers between devices with their start and end apart: 32, of which 19 were waited for; matrix products, arithmetic and copies ran while one was open for 1% of the time, Pallas kernels for 13%

profile of v5, /device:TPU:1, one launch (start us, length us, event | category | flops | bytes accessed | tf_op | source)
XLA Modules:
  0.0 333.1 jit_solution(2220008828678437854)
XLA Ops:
  7.2 1.8 constant_dynamic-update-slice_fusion.7
  9.0 3.9 %collective-permute-start = (bf16[16,32,128]{2,1,0:T(8,128)(2,1)S(1)}, bf16[16,32,128]{2,1,0:T(8,128)(2,1)S(1)}, u32[]{:S(2)}, u32[]{:S(2)}) collective-permute-start(bf16[16,32,128]{2,1,0:T(8,128)(2,1)S(1)} %get-tuple-element.77), channel_id=1, source_target_pairs={{0,2},{2,4},{4,6},{6,0},{1,3},{3,5},{5,7},{7,1},{8,10},{10,12},{12... | collective-permute-start | bytes 393224 | tf_op jit(solution)/shard_map/ppermute | solution.py:149
  12.9 3.1 collective-permute-start.1
  16.0 4.4 %collective-permute-start.2 = (bf16[16,32,128]{2,1,0:T(8,128)(2,1)S(1)}, bf16[16,32,128]{2,1,0:T(8,128)(2,1)S(1)}, u32[]{:S(2)}, u32[]{:S(2)}) collective-permute-start(bf16[16,32,128]{2,1,0:T(8,128)(2,1)S(1)} %get-tuple-element.77), channel_id=1, source_target_pairs={{0,4},{2,6},{4,0},{6,2},{1,5},{3,7},{5,1},{7,3},{8,12},{10,14},{12... | collective-permute-start | bytes 393224 | tf_op jit(solution)/shard_map/ppermute | solution.py:149
  20.4 6.1 %collective-permute-done.1 = bf16[16,32,128]{2,1,0:T(8,128)(2,1)S(1)} collective-permute-done((bf16[16,32,128]{2,1,0:T(8,128)(2,1)S(1)}, bf16[16,32,128]{2,1,0:T(8,128)(2,1)S(1)}, u32[]{:S(2)}, u32[]{:S(2)}) %collective-permute-start.1) | collective-permute-done | bytes 131104 | tf_op jit(solution)/shard_map/ppermute | solution.py:149
  26.5 1.8 collective-permute-done.2
  31.2 12.5 %collective-permute-done.3 = bf16[64,32,128]{2,1,0:T(8,128)(2,1)S(1)} collective-permute-done((bf16[64,32,128]{2,1,0:T(8,128)(2,1)S(1)}, bf16[64,32,128]{2,1,0:T(8,128)(2,1)S(1)}, u32[]{:S(2)}, u32[]{:S(2)}) %collective-permute-start.3) | collective-permute-done | bytes 524320 | tf_op jit(solution)/shard_map/ppermute | solution.py:149
  43.9 2.7 collective-permute-start.6
  46.8 4.3 %collective-permute-done.5 = bf16[32,32,128]{2,1,0:T(8,128)(2,1)S(1)} collective-permute-done((bf16[32,32,128]{2,1,0:T(8,128)(2,1)S(1)}, bf16[32,32,128]{2,1,0:T(8,128)(2,1)S(1)}, u32[]{:S(2)}, u32[]{:S(2)}) %collective-permute-start.5) | collective-permute-done | bytes 262176 | tf_op jit(solution)/shard_map/ppermute | solution.py:149
  51.2 4.1 %collective-permute-start.7 = (bf16[256,32,128]{2,1,0:T(8,128)(2,1)S(1)}, bf16[256,32,128]{2,1,0:T(8,128)(2,1)}, u32[]{:S(2)}, u32[]{:S(2)}) collective-permute-start(bf16[256,32,128]{2,1,0:T(8,128)(2,1)S(1)} %constant_dynamic-update-slice_fusion.refs_0_), channel_id=1, source_target_pairs={{0,1},{1,0},{2,3},{3,2},{4,5},{5,4},{6,7},{7,6},{8,9},{9,8},{10,11... | collective-permute-start | bytes 6291464 | tf_op jit(solution)/shard_map/ppermute | solution.py:149
  55.5 3.8 %collective-permute-done.7.refs_1_ = bf16[256,32,128]{2,1,0:T(8,128)(2,1)} collective-permute-done((bf16[256,32,128]{2,1,0:T(8,128)(2,1)S(1)}, bf16[256,32,128]{2,1,0:T(8,128)(2,1)}, u32[]{:S(2)}, u32[]{:S(2)}) %collective-permute-start.7) | collective-permute-done | bytes 2097184 | tf_op jit(solution)/shard_map/ppermute | solution.py:149
  59.3 10.7 %products.6 = (f32[16,32,128]{2,1,0:T(8,128)S(1)}, bf16[128,32,128]{2,1,0:T(8,128)(2,1)}) custom-call(s32[256]{0:T(256)S(1)} %bitcast.45, s32[256]{0:T(256)S(1)} %bitcast.51, s32[33]{0:T(128)S(1)} %stack.135.place, bf16[256,32,128]{2,1,0:T(8,128)(2,1)S(1)} %constant_dynamic-update-slice_fusion.refs_0_, bf16[256,32,128]{2,1,0:T(8,128)(2,1)} %collective-permute-done.7.refs_1_, ...), custom_call_target="tpu_custom_call" | custom-call | flops 268435456 | bytes 12582912 | tf_op jit(solution)/shard_map/products/pallas_call | solution.py:127
  70.0 8.4 %all-to-all-start.1 = ((bf16[128,32,128]{2,1,0:T(8,128)(2,1)}), bf16[128,32,128]{2,1,0:T(8,128)(2,1)S(1)}, u32[]{:S(2)}, u32[]{:S(2)}) async-start(bf16[128,32,128]{2,1,0:T(8,128)(2,1)} %get-tuple-element.33), calls=%async_computation.1 | async-start | bytes 2097152 | tf_op jit(solution)/shard_map/all_to_all | solution.py:171
  78.4 7.2 %products.7 = (f32[16,32,128]{2,1,0:T(8,128)S(1)}, bf16[128,32,128]{2,1,0:T(8,128)(2,1)}) custom-call(s32[256]{0:T(256)S(1)} %bitcast.46, s32[256]{0:T(256)S(1)} %bitcast.52, s32[33]{0:T(128)S(1)} %stack.135.place, bf16[512,32,128]{2,1,0:T(8,128)(2,1)} %all-gather.4.cloned.1.call-done.given, bf16[256,128,128]{2,1,0:T(8,128)(2,1)} %bitcast.58), custom_call_target="tpu_custom_call" | custom-call | flops 268435456 | bytes 12582912 | tf_op jit(solution)/shard_map/products/pallas_call | solution.py:127
  85.7 7.9 %all-to-all-done.1 = bf16[128,32,128]{2,1,0:T(8,128)(2,1)S(1)} async-done(((bf16[128,32,128]{2,1,0:T(8,128)(2,1)}), bf16[128,32,128]{2,1,0:T(8,128)(2,1)S(1)}, u32[]{:S(2)}, u32[]{:S(2)}) %all-to-all-start.1) | async-done | bytes 1048608 | tf_op jit(solution)/shard_map/all_to_all | solution.py:171
  93.6 3.6 %all-to-all-start = ((bf16[128,32,128]{2,1,0:T(8,128)(2,1)}), bf16[128,32,128]{2,1,0:T(8,128)(2,1)S(1)}, u32[]{:S(2)}, u32[]{:S(2)}) async-start(bf16[128,32,128]{2,1,0:T(8,128)(2,1)} %get-tuple-element.36), calls=%async_computation | async-start | bytes 2097152 | tf_op jit(solution)/shard_map/all_to_all | solution.py:171
  97.5 3.6 %collective-permute-start.9 = (bf16[16,32,128]{2,1,0:T(8,128)(2,1)S(1)}, bf16[16,32,128]{2,1,0:T(8,128)(2,1)S(1)}, u32[]{:S(2)}, u32[]{:S(2)}) collective-permute-start(bf16[16,32,128]{2,1,0:T(8,128)(2,1)S(1)} %get-tuple-element.38), channel_id=1, source_target_pairs={{0,6},{2,0},{4,2},{6,4},{1,7},{3,1},{5,3},{7,5},{8,14},{10,8},{12,... | collective-permute-start | bytes 393224 | tf_op jit(solution)/shard_map/ppermute | solution.py:149
  101.1 4.1 %collective-permute-start.10 = (bf16[16,32,128]{2,1,0:T(8,128)(2,1)S(1)}, bf16[16,32,128]{2,1,0:T(8,128)(2,1)S(1)}, u32[]{:S(2)}, u32[]{:S(2)}) collective-permute-start(bf16[16,32,128]{2,1,0:T(8,128)(2,1)S(1)} %get-tuple-element.38), channel_id=1, source_target_pairs={{0,4},{2,6},{4,0},{6,2},{1,5},{3,7},{5,1},{7,3},{8,12},{10,14},{12... | collective-permute-start | bytes 393224 | tf_op jit(solution)/shard_map/ppermute | solution.py:149
  105.2 8.2 %collective-permute-done.8 = bf16[16,32,128]{2,1,0:T(8,128)(2,1)S(1)} collective-permute-done((bf16[16,32,128]{2,1,0:T(8,128)(2,1)S(1)}, bf16[16,32,128]{2,1,0:T(8,128)(2,1)S(1)}, u32[]{:S(2)}, u32[]{:S(2)}) %collective-permute-start.8) | collective-permute-done | bytes 131104 | tf_op jit(solution)/shard_map/ppermute | solution.py:149
  113.4 10.4 %collective-permute-done.10 = bf16[16,32,128]{2,1,0:T(8,128)(2,1)S(1)} collective-permute-done((bf16[16,32,128]{2,1,0:T(8,128)(2,1)S(1)}, bf16[16,32,128]{2,1,0:T(8,128)(2,1)S(1)}, u32[]{:S(2)}, u32[]{:S(2)}) %collective-permute-start.10) | collective-permute-done | bytes 131104 | tf_op jit(solution)/shard_map/ppermute | solution.py:149
  124.8 2.7 collective-permute-start.12
  127.5 10.0 %collective-permute-done.11 = bf16[64,32,128]{2,1,0:T(8,128)(2,1)S(1)} collective-permute-done((bf16[64,32,128]{2,1,0:T(8,128)(2,1)S(1)}, bf16[64,32,128]{2,1,0:T(8,128)(2,1)S(1)}, u32[]{:S(2)}, u32[]{:S(2)}) %collective-permute-start.11) | collective-permute-done | bytes 524320 | tf_op jit(solution)/shard_map/ppermute | solution.py:149
  137.8 2.6 collective-permute-start.14
  140.6 3.6 %collective-permute-done.13 = bf16[32,32,128]{2,1,0:T(8,128)(2,1)S(1)} collective-permute-done((bf16[32,32,128]{2,1,0:T(8,128)(2,1)S(1)}, bf16[32,32,128]{2,1,0:T(8,128)(2,1)S(1)}, u32[]{:S(2)}, u32[]{:S(2)}) %collective-permute-start.13) | collective-permute-done | bytes 262176 | tf_op jit(solution)/shard_map/ppermute | solution.py:149
  144.6 4.8 %collective-permute-start.15 = (bf16[256,32,128]{2,1,0:T(8,128)(2,1)S(1)}, bf16[256,32,128]{2,1,0:T(8,128)(2,1)S(1)}, u32[]{:S(2)}, u32[]{:S(2)}) collective-permute-start(bf16[256,32,128]{2,1,0:T(8,128)(2,1)S(1)} %constant_dynamic-update-slice_fusion.12.refs_0_), channel_id=1, source_target_pairs={{0,1},{1,0},{2,3},{3,2},{4,5},{5,4},{6,7},{7,6},{8,9},{9,8},{10,11... | collective-permute-start | bytes 6291464 | tf_op jit(solution)/shard_map/ppermute | solution.py:149
  149.4 3.8 %collective-permute-done.15.refs_1_ = bf16[256,32,128]{2,1,0:T(8,128)(2,1)S(1)} collective-permute-done((bf16[256,32,128]{2,1,0:T(8,128)(2,1)S(1)}, bf16[256,32,128]{2,1,0:T(8,128)(2,1)S(1)}, u32[]{:S(2)}, u32[]{:S(2)}) %collective-permute-start.15) | collective-permute-done | bytes 2097184 | tf_op jit(solution)/shard_map/ppermute | solution.py:149
  153.2 8.1 %products.8 = (f32[16,32,128]{2,1,0:T(8,128)S(1)}, bf16[128,32,128]{2,1,0:T(8,128)(2,1)S(1)}) custom-call(s32[256]{0:T(256)S(1)} %bitcast.47, s32[256]{0:T(256)S(1)} %bitcast.53, s32[33]{0:T(128)S(1)} %stack.135.place, bf16[256,32,128]{2,1,0:T(8,128)(2,1)S(1)} %constant_dynamic-update-slice_fusion.12.refs_0_, ...), custom_call_target="tpu_custom_call" | custom-call | flops 268435456 | bytes 12582912 | tf_op jit(solution)/shard_map/products/pallas_call | solution.py:127
  161.2 31.6 %all_to_all.30 = bf16[128,32,128]{2,1,0:T(8,128)(2,1)S(1)} all-to-all(bf16[128,32,128]{2,1,0:T(8,128)(2,1)S(1)} %get-tuple-element.47), channel_id=1, replica_groups=mesh['y'=4,'zl'=2,'x'=4,'zh'=4,'core'=2] {'y','zl'}, dimensions={0} | all-to-all | bytes 2097152 | tf_op jit(solution)/shard_map/all_to_all | solution.py:171
  193.7 7.2 %products.9 = (f32[16,32,128]{2,1,0:T(8,128)S(1)}, bf16[128,32,128]{2,1,0:T(8,128)(2,1)}) custom-call(s32[256]{0:T(256)S(1)} %bitcast.48, s32[256]{0:T(256)S(1)} %bitcast.54, s32[33]{0:T(128)S(1)} %stack.135.place, bf16[512,32,128]{2,1,0:T(8,128)(2,1)} %all-gather.6.cloned.1.call-done.given, bf16[256,128,128]{2,1,0:T(8,128)(2,1)} %bitcast.60), custom_call_target="tpu_custom_call" | custom-call | flops 268435456 | bytes 12582912 | tf_op jit(solution)/shard_map/products/pallas_call | solution.py:127
  201.0 3.6 %all-to-all-start.3 = ((bf16[128,32,128]{2,1,0:T(8,128)(2,1)}), bf16[128,32,128]{2,1,0:T(8,128)(2,1)S(1)}, u32[]{:S(2)}, u32[]{:S(2)}) async-start(bf16[128,32,128]{2,1,0:T(8,128)(2,1)} %get-tuple-element.50), calls=%async_computation.3 | async-start | bytes 2097152 | tf_op jit(solution)/shard_map/all_to_all | solution.py:171
  204.6 1.9 collective-permute-start.16
  206.5 1.8 collective-permute-start.17
  208.2 4.7 %collective-permute-start.18 = (bf16[16,32,128]{2,1,0:T(8,128)(2,1)S(1)}, bf16[16,32,128]{2,1,0:T(8,128)(2,1)S(1)}, u32[]{:S(2)}, u32[]{:S(2)}) collective-permute-start(bf16[16,32,128]{2,1,0:T(8,128)(2,1)S(1)} %get-tuple-element.51), channel_id=1, source_target_pairs={{0,4},{2,6},{4,0},{6,2},{1,5},{3,7},{5,1},{7,3},{8,12},{10,14},{12... | collective-permute-start | bytes 393224 | tf_op jit(solution)/shard_map/ppermute | solution.py:149
  212.9 11.9 %collective-permute-done.16 = bf16[16,32,128]{2,1,0:T(8,128)(2,1)S(1)} collective-permute-done((bf16[16,32,128]{2,1,0:T(8,128)(2,1)S(1)}, bf16[16,32,128]{2,1,0:T(8,128)(2,1)S(1)}, u32[]{:S(2)}, u32[]{:S(2)}) %collective-permute-start.16) | collective-permute-done | bytes 131104 | tf_op jit(solution)/shard_map/ppermute | solution.py:149
  224.8 6.0 %collective-permute-done.18 = bf16[16,32,128]{2,1,0:T(8,128)(2,1)S(1)} collective-permute-done((bf16[16,32,128]{2,1,0:T(8,128)(2,1)S(1)}, bf16[16,32,128]{2,1,0:T(8,128)(2,1)S(1)}, u32[]{:S(2)}, u32[]{:S(2)}) %collective-permute-start.18) | collective-permute-done | bytes 131104 | tf_op jit(solution)/shard_map/ppermute | solution.py:149
  233.2 1.5 collective-permute-start.20
  234.7 9.3 %collective-permute-done.19 = bf16[64,32,128]{2,1,0:T(8,128)(2,1)S(1)} collective-permute-done((bf16[64,32,128]{2,1,0:T(8,128)(2,1)S(1)}, bf16[64,32,128]{2,1,0:T(8,128)(2,1)S(1)}, u32[]{:S(2)}, u32[]{:S(2)}) %collective-permute-start.19) | collective-permute-done | bytes 524320 | tf_op jit(solution)/shard_map/ppermute | solution.py:149
  245.1 1.7 collective-permute-start.22
  247.0 4.4 %collective-permute-done.21 = bf16[32,32,128]{2,1,0:T(8,128)(2,1)S(1)} collective-permute-done((bf16[32,32,128]{2,1,0:T(8,128)(2,1)S(1)}, bf16[32,32,128]{2,1,0:T(8,128)(2,1)S(1)}, u32[]{:S(2)}, u32[]{:S(2)}) %collective-permute-start.21) | collective-permute-done | bytes 262176 | tf_op jit(solution)/shard_map/ppermute | solution.py:149
  251.6 5.6 %collective-permute-start.23 = (bf16[256,32,128]{2,1,0:T(8,128)(2,1)S(1)}, bf16[256,32,128]{2,1,0:T(8,128)(2,1)S(1)}, u32[]{:S(2)}, u32[]{:S(2)}) collective-permute-start(bf16[256,32,128]{2,1,0:T(8,128)(2,1)S(1)} %constant_dynamic-update-slice_fusion.21.refs_0_), channel_id=1, source_target_pairs={{0,1},{1,0},{2,3},{3,2},{4,5},{5,4},{6,7},{7,6},{8,9},{9,8},{10,11... | collective-permute-start | bytes 6291464 | tf_op jit(solution)/shard_map/ppermute | solution.py:149
  257.2 3.8 %collective-permute-done.23.refs_1_ = bf16[256,32,128]{2,1,0:T(8,128)(2,1)S(1)} collective-permute-done((bf16[256,32,128]{2,1,0:T(8,128)(2,1)S(1)}, bf16[256,32,128]{2,1,0:T(8,128)(2,1)S(1)}, u32[]{:S(2)}, u32[]{:S(2)}) %collective-permute-start.23) | collective-permute-done | bytes 2097184 | tf_op jit(solution)/shard_map/ppermute | solution.py:149
  261.0 9.1 %products.10 = (f32[16,32,128]{2,1,0:T(8,128)S(1)}, bf16[128,32,128]{2,1,0:T(8,128)(2,1)}) custom-call(s32[256]{0:T(256)S(1)} %bitcast.49, s32[256]{0:T(256)S(1)} %bitcast.55, s32[33]{0:T(128)S(1)} %stack.135.place, bf16[256,32,128]{2,1,0:T(8,128)(2,1)S(1)} %constant_dynamic-update-slice_fusion.21.refs_0_, ...), custom_call_target="tpu_custom_call" | custom-call | flops 268435456 | bytes 12582912 | tf_op jit(solution)/shard_map/products/pallas_call | solution.py:127
  270.0 6.7 %all-to-all-start.5 = ((bf16[128,32,128]{2,1,0:T(8,128)(2,1)}), bf16[128,32,128]{2,1,0:T(8,128)(2,1)S(1)}, u32[]{:S(2)}, u32[]{:S(2)}) async-start(bf16[128,32,128]{2,1,0:T(8,128)(2,1)} %get-tuple-element.59), calls=%async_computation.5 | async-start | bytes 2097152 | tf_op jit(solution)/shard_map/all_to_all | solution.py:171
  276.7 21.1 %all-gather.8.cloned.1.call-done.given = bf16[512,32,128]{2,1,0:T(8,128)(2,1)} async-done(((bf16[16,32,128]{2,1,0:T(8,128)(2,1)}), bf16[512,32,128]{2,1,0:T(8,128)(2,1)}) %all-gather.8.cloned.1.call-update) | async-done | bytes 4194320 | tf_op jit(solution)/shard_map/all_gather | solution.py:220
  297.8 7.2 %products.11 = (f32[16,32,128]{2,1,0:T(8,128)S(1)}, bf16[128,32,128]{2,1,0:T(8,128)(2,1)}) custom-call(s32[256]{0:T(256)S(1)} %bitcast.50, s32[256]{0:T(256)S(1)} %bitcast.56, s32[33]{0:T(128)S(1)} %stack.135.place, bf16[512,32,128]{2,1,0:T(8,128)(2,1)} %all-gather.8.cloned.1.call-done.given, bf16[256,128,128]{2,1,0:T(8,128)(2,1)} %bitcast.62), custom_call_target="tpu_custom_call" | custom-call | flops 268435456 | bytes 12582912 | tf_op jit(solution)/shard_map/products/pallas_call | solution.py:127
  305.0 3.8 %all-to-all-start.4 = ((bf16[128,32,128]{2,1,0:T(8,128)(2,1)}), bf16[128,32,128]{2,1,0:T(8,128)(2,1)S(1)}, u32[]{:S(2)}, u32[]{:S(2)}) async-start(bf16[128,32,128]{2,1,0:T(8,128)(2,1)} %get-tuple-element.62), calls=%async_computation.4 | async-start | bytes 2097152 | tf_op jit(solution)/shard_map/all_to_all | solution.py:171
  309.8 2.0 multiply_add_fusion
  311.8 12.4 %all-to-all-done.4 = bf16[128,32,128]{2,1,0:T(8,128)(2,1)S(1)} async-done(((bf16[128,32,128]{2,1,0:T(8,128)(2,1)}), bf16[128,32,128]{2,1,0:T(8,128)(2,1)S(1)}, u32[]{:S(2)}, u32[]{:S(2)}) %all-to-all-start.4) | async-done | bytes 1048608 | tf_op jit(solution)/shard_map/all_to_all | solution.py:171
  (88 shorter events, 12.4 us)
Async XLA Ops:
  7.2 71.3 %all-gather.4.cloned.1.call-start = ((), (), s32[]{:S(2)}) async-start(), calls=%async_computation.6 | async-start | bytes 4325376 | tf_op jit(solution)/shard_map/all_gather | solution.py:200
  9.0 11.4 %collective-permute-start = (bf16[16,32,128]{2,1,0:T(8,128)(2,1)S(1)}, bf16[16,32,128]{2,1,0:T(8,128)(2,1)S(1)}, u32[]{:S(2)}, u32[]{:S(2)}) collective-permute-start(bf16[16,32,128]{2,1,0:T(8,128)(2,1)S(1)} %get-tuple-element.77), channel_id=1, source_target_pairs={{0,2},{2,4},{4,6},{6,0},{1,3},{3,5},{5,7},{7,1},{8,10},{10,12},{12... | collective-permute-start | bytes 393224 | tf_op jit(solution)/shard_map/ppermute | solution.py:149
  12.9 13.6 %collective-permute-start.1 = (bf16[16,32,128]{2,1,0:T(8,128)(2,1)S(1)}, bf16[16,32,128]{2,1,0:T(8,128)(2,1)S(1)}, u32[]{:S(2)}, u32[]{:S(2)}) collective-permute-start(bf16[16,32,128]{2,1,0:T(8,128)(2,1)S(1)} %get-tuple-element.77), channel_id=1, source_target_pairs={{0,6},{2,0},{4,2},{6,4},{1,7},{3,1},{5,3},{7,5},{8,14},{10,8},{12,... | collective-permute-start | bytes 393224 | tf_op jit(solution)/shard_map/ppermute | solution.py:149
  16.0 12.3 %collective-permute-start.2 = (bf16[16,32,128]{2,1,0:T(8,128)(2,1)S(1)}, bf16[16,32,128]{2,1,0:T(8,128)(2,1)S(1)}, u32[]{:S(2)}, u32[]{:S(2)}) collective-permute-start(bf16[16,32,128]{2,1,0:T(8,128)(2,1)S(1)} %get-tuple-element.77), channel_id=1, source_target_pairs={{0,4},{2,6},{4,0},{6,2},{1,5},{3,7},{5,1},{7,3},{8,12},{10,14},{12... | collective-permute-start | bytes 393224 | tf_op jit(solution)/shard_map/ppermute | solution.py:149
  28.4 15.3 %collective-permute-start.3 = (bf16[64,32,128]{2,1,0:T(8,128)(2,1)S(1)}, bf16[64,32,128]{2,1,0:T(8,128)(2,1)S(1)}, u32[]{:S(2)}, u32[]{:S(2)}) collective-permute-start(bf16[64,32,128]{2,1,0:T(8,128)(2,1)S(1)} %pad_maximum_fusion), channel_id=1, source_target_pairs={{0,8},{8,16},{16,24},{24,0},{1,9},{9,17},{17,25},{25,1},{2,10},{10... | collective-permute-start | bytes 1572872 | tf_op jit(solution)/shard_map/ppermute | solution.py:149
  29.7 14.2 %collective-permute-start.4 = (bf16[64,32,128]{2,1,0:T(8,128)(2,1)S(1)}, bf16[64,32,128]{2,1,0:T(8,128)(2,1)S(1)}, u32[]{:S(2)}, u32[]{:S(2)}) collective-permute-start(bf16[64,32,128]{2,1,0:T(8,128)(2,1)S(1)} %pad_maximum_fusion), channel_id=1, source_target_pairs={{0,24},{8,0},{16,8},{24,16},{1,25},{9,1},{17,9},{25,17},{2,26},{10... | collective-permute-start | bytes 1572872 | tf_op jit(solution)/shard_map/ppermute | solution.py:149
  43.7 7.4 %collective-permute-start.5 = (bf16[32,32,128]{2,1,0:T(8,128)(2,1)S(1)}, bf16[32,32,128]{2,1,0:T(8,128)(2,1)S(1)}, u32[]{:S(2)}, u32[]{:S(2)}) collective-permute-start(bf16[32,32,128]{2,1,0:T(8,128)(2,1)S(1)} %slice.32), channel_id=1, source_target_pairs={{0,8},{8,16},{16,24},{24,0},{1,9},{9,17},{17,25},{25,1},{2,10},{10... | collective-permute-start | bytes 786440 | tf_op jit(solution)/shard_map/ppermute | solution.py:149
  43.9 15.4 %copy-start = (s32[1,1,256]{2,1,0:T(1,128)S(1)}, s32[1,1,256]{2,1,0:T(1,128)}, u32[]{:S(2)}) copy-start(s32[1,1,256]{2,1,0:T(1,128)} %param.8) | copy-start | bytes 3076
  43.9 15.4 %copy-start.1 = (s32[1,1,256]{2,1,0:T(1,128)S(1)}, s32[1,1,256]{2,1,0:T(1,128)}, u32[]{:S(2)}) copy-start(s32[1,1,256]{2,1,0:T(1,128)} %param.9) | copy-start | bytes 3076
  43.9 7.2 %collective-permute-start.6 = (bf16[32,32,128]{2,1,0:T(8,128)(2,1)S(1)}, bf16[32,32,128]{2,1,0:T(8,128)(2,1)S(1)}, u32[]{:S(2)}, u32[]{:S(2)}) collective-permute-start(bf16[32,32,128]{2,1,0:T(8,128)(2,1)S(1)} %slice.33), channel_id=1, source_target_pairs={{0,24},{8,0},{16,8},{24,16},{1,25},{9,1},{17,9},{25,17},{2,26},{10... | collective-permute-start | bytes 786440 | tf_op jit(solution)/shard_map/ppermute | solution.py:149
  51.2 8.0 %collective-permute-start.7 = (bf16[256,32,128]{2,1,0:T(8,128)(2,1)S(1)}, bf16[256,32,128]{2,1,0:T(8,128)(2,1)}, u32[]{:S(2)}, u32[]{:S(2)}) collective-permute-start(bf16[256,32,128]{2,1,0:T(8,128)(2,1)S(1)} %constant_dynamic-update-slice_fusion.refs_0_), channel_id=1, source_target_pairs={{0,1},{1,0},{2,3},{3,2},{4,5},{5,4},{6,7},{7,6},{8,9},{9,8},{10,11... | collective-permute-start | bytes 6291464 | tf_op jit(solution)/shard_map/ppermute | solution.py:149
  70.0 23.6 %all-to-all-start.1 = ((bf16[128,32,128]{2,1,0:T(8,128)(2,1)}), bf16[128,32,128]{2,1,0:T(8,128)(2,1)S(1)}, u32[]{:S(2)}, u32[]{:S(2)}) async-start(bf16[128,32,128]{2,1,0:T(8,128)(2,1)} %get-tuple-element.33), calls=%async_computation.1 | async-start | bytes 2097152 | tf_op jit(solution)/shard_map/all_to_all | solution.py:171
  85.7 11.6 %copy-start.2 = (f32[16,64,128]{2,1,0:T(8,128)S(1)}, f32[16,64,128]{2,1,0:T(8,128)}, u32[]{:S(2)}) copy-start(f32[16,64,128]{2,1,0:T(8,128)} %param.6) | copy-start | bytes 1572868
  93.6 30.3 %all-to-all-start = ((bf16[128,32,128]{2,1,0:T(8,128)(2,1)}), bf16[128,32,128]{2,1,0:T(8,128)(2,1)S(1)}, u32[]{:S(2)}, u32[]{:S(2)}) async-start(bf16[128,32,128]{2,1,0:T(8,128)(2,1)} %get-tuple-element.36), calls=%async_computation | async-start | bytes 2097152 | tf_op jit(solution)/shard_map/all_to_all | solution.py:171
  97.2 96.6 %all-gather.6.cloned.1.call-start = ((), (), s32[]{:S(2)}) async-start(), calls=%async_computation.7 | async-start | bytes 4325376 | tf_op jit(solution)/shard_map/all_gather | solution.py:220
  97.4 95.4 %copy-start.4 = (f32[16,32,128]{2,1,0:T(8,128)}, f32[16,32,128]{2,1,0:T(8,128)S(1)}, u32[]{:S(2)}) copy-start(f32[16,32,128]{2,1,0:T(8,128)S(1)} %get-tuple-element.75) | copy-start | bytes 786436
  97.4 15.9 %collective-permute-start.8 = (bf16[16,32,128]{2,1,0:T(8,128)(2,1)S(1)}, bf16[16,32,128]{2,1,0:T(8,128)(2,1)S(1)}, u32[]{:S(2)}, u32[]{:S(2)}) collective-permute-start(bf16[16,32,128]{2,1,0:T(8,128)(2,1)S(1)} %get-tuple-element.38), channel_id=1, source_target_pairs={{0,2},{2,4},{4,6},{6,0},{1,3},{3,5},{5,7},{7,1},{8,10},{10,12},{12... | collective-permute-start | bytes 393224 | tf_op jit(solution)/shard_map/ppermute | solution.py:149
  97.5 15.9 %collective-permute-start.9 = (bf16[16,32,128]{2,1,0:T(8,128)(2,1)S(1)}, bf16[16,32,128]{2,1,0:T(8,128)(2,1)S(1)}, u32[]{:S(2)}, u32[]{:S(2)}) collective-permute-start(bf16[16,32,128]{2,1,0:T(8,128)(2,1)S(1)} %get-tuple-element.38), channel_id=1, source_target_pairs={{0,6},{2,0},{4,2},{6,4},{1,7},{3,1},{5,3},{7,5},{8,14},{10,8},{12,... | collective-permute-start | bytes 393224 | tf_op jit(solution)/shard_map/ppermute | solution.py:149
  101.1 22.7 %collective-permute-start.10 = (bf16[16,32,128]{2,1,0:T(8,128)(2,1)S(1)}, bf16[16,32,128]{2,1,0:T(8,128)(2,1)S(1)}, u32[]{:S(2)}, u32[]{:S(2)}) collective-permute-start(bf16[16,32,128]{2,1,0:T(8,128)(2,1)S(1)} %get-tuple-element.38), channel_id=1, source_target_pairs={{0,4},{2,6},{4,0},{6,2},{1,5},{3,7},{5,1},{7,3},{8,12},{10,14},{12... | collective-permute-start | bytes 393224 | tf_op jit(solution)/shard_map/ppermute | solution.py:149
  124.7 106.3 %copy-start.6 = (f32[16,32,128]{2,1,0:T(8,128)}, f32[16,32,128]{2,1,0:T(8,128)S(1)}, u32[]{:S(2)}) copy-start(f32[16,32,128]{2,1,0:T(8,128)S(1)} %get-tuple-element.73) | copy-start | bytes 786436
  124.7 12.8 %collective-permute-start.11 = (bf16[64,32,128]{2,1,0:T(8,128)(2,1)S(1)}, bf16[64,32,128]{2,1,0:T(8,128)(2,1)S(1)}, u32[]{:S(2)}, u32[]{:S(2)}) collective-permute-start(bf16[64,32,128]{2,1,0:T(8,128)(2,1)S(1)} %constant_dynamic-update-slice_fusion.8), channel_id=1, source_target_pairs={{0,8},{8,16},{16,24},{24,0},{1,9},{9,17},{17,25},{25,1},{2,10},{10... | collective-permute-start | bytes 1572872 | tf_op jit(solution)/shard_map/ppermute | solution.py:149
  124.8 12.7 %collective-permute-start.12 = (bf16[64,32,128]{2,1,0:T(8,128)(2,1)S(1)}, bf16[64,32,128]{2,1,0:T(8,128)(2,1)S(1)}, u32[]{:S(2)}, u32[]{:S(2)}) collective-permute-start(bf16[64,32,128]{2,1,0:T(8,128)(2,1)S(1)} %constant_dynamic-update-slice_fusion.8), channel_id=1, source_target_pairs={{0,24},{8,0},{16,8},{24,16},{1,25},{9,1},{17,9},{25,17},{2,26},{10... | collective-permute-start | bytes 1572872 | tf_op jit(solution)/shard_map/ppermute | solution.py:149
  137.5 6.7 %collective-permute-start.13 = (bf16[32,32,128]{2,1,0:T(8,128)(2,1)S(1)}, bf16[32,32,128]{2,1,0:T(8,128)(2,1)S(1)}, u32[]{:S(2)}, u32[]{:S(2)}) collective-permute-start(bf16[32,32,128]{2,1,0:T(8,128)(2,1)S(1)} %slice.28), channel_id=1, source_target_pairs={{0,8},{8,16},{16,24},{24,0},{1,9},{9,17},{17,25},{25,1},{2,10},{10... | collective-permute-start | bytes 786440 | tf_op jit(solution)/shard_map/ppermute | solution.py:149
  137.8 6.8 %collective-permute-start.14 = (bf16[32,32,128]{2,1,0:T(8,128)(2,1)S(1)}, bf16[32,32,128]{2,1,0:T(8,128)(2,1)S(1)}, u32[]{:S(2)}, u32[]{:S(2)}) collective-permute-start(bf16[32,32,128]{2,1,0:T(8,128)(2,1)S(1)} %slice.29), channel_id=1, source_target_pairs={{0,24},{8,0},{16,8},{24,16},{1,25},{9,1},{17,9},{25,17},{2,26},{10... | collective-permute-start | bytes 786440 | tf_op jit(solution)/shard_map/ppermute | solution.py:149
  144.6 8.6 %collective-permute-start.15 = (bf16[256,32,128]{2,1,0:T(8,128)(2,1)S(1)}, bf16[256,32,128]{2,1,0:T(8,128)(2,1)S(1)}, u32[]{:S(2)}, u32[]{:S(2)}) collective-permute-start(bf16[256,32,128]{2,1,0:T(8,128)(2,1)S(1)} %constant_dynamic-update-slice_fusion.12.refs_0_), channel_id=1, source_target_pairs={{0,1},{1,0},{2,3},{3,2},{4,5},{5,4},{6,7},{7,6},{8,9},{9,8},{10,11... | collective-permute-start | bytes 6291464 | tf_op jit(solution)/shard_map/ppermute | solution.py:149
  201.0 30.0 %all-to-all-start.3 = ((bf16[128,32,128]{2,1,0:T(8,128)(2,1)}), bf16[128,32,128]{2,1,0:T(8,128)(2,1)S(1)}, u32[]{:S(2)}, u32[]{:S(2)}) async-start(bf16[128,32,128]{2,1,0:T(8,128)(2,1)} %get-tuple-element.50), calls=%async_computation.3 | async-start | bytes 2097152 | tf_op jit(solution)/shard_map/all_to_all | solution.py:171
  204.5 93.2 %all-gather.8.cloned.1.call-start = ((), (), s32[]{:S(2)}) async-start(), calls=%async_computation.8 | async-start | bytes 4325376 | tf_op jit(solution)/shard_map/all_gather | solution.py:220
  204.6 20.2 %collective-permute-start.16 = (bf16[16,32,128]{2,1,0:T(8,128)(2,1)S(1)}, bf16[16,32,128]{2,1,0:T(8,128)(2,1)S(1)}, u32[]{:S(2)}, u32[]{:S(2)}) collective-permute-start(bf16[16,32,128]{2,1,0:T(8,128)(2,1)S(1)} %get-tuple-element.51), channel_id=1, source_target_pairs={{0,2},{2,4},{4,6},{6,0},{1,3},{3,5},{5,7},{7,1},{8,10},{10,12},{12... | collective-permute-start | bytes 393224 | tf_op jit(solution)/shard_map/ppermute | solution.py:149
  206.5 18.4 %collective-permute-start.17 = (bf16[16,32,128]{2,1,0:T(8,128)(2,1)S(1)}, bf16[16,32,128]{2,1,0:T(8,128)(2,1)S(1)}, u32[]{:S(2)}, u32[]{:S(2)}) collective-permute-start(bf16[16,32,128]{2,1,0:T(8,128)(2,1)S(1)} %get-tuple-element.51), channel_id=1, source_target_pairs={{0,6},{2,0},{4,2},{6,4},{1,7},{3,1},{5,3},{7,5},{8,14},{10,8},{12,... | collective-permute-start | bytes 393224 | tf_op jit(solution)/shard_map/ppermute | solution.py:149
  208.2 22.6 %collective-permute-start.18 = (bf16[16,32,128]{2,1,0:T(8,128)(2,1)S(1)}, bf16[16,32,128]{2,1,0:T(8,128)(2,1)S(1)}, u32[]{:S(2)}, u32[]{:S(2)}) collective-permute-start(bf16[16,32,128]{2,1,0:T(8,128)(2,1)S(1)} %get-tuple-element.51), channel_id=1, source_target_pairs={{0,4},{2,6},{4,0},{6,2},{1,5},{3,7},{5,1},{7,3},{8,12},{10,14},{12... | collective-permute-start | bytes 393224 | tf_op jit(solution)/shard_map/ppermute | solution.py:149
  231.9 12.0 %collective-permute-start.19 = (bf16[64,32,128]{2,1,0:T(8,128)(2,1)S(1)}, bf16[64,32,128]{2,1,0:T(8,128)(2,1)S(1)}, u32[]{:S(2)}, u32[]{:S(2)}) collective-permute-start(bf16[64,32,128]{2,1,0:T(8,128)(2,1)S(1)} %constant_dynamic-update-slice_fusion.17), channel_id=1, source_target_pairs={{0,8},{8,16},{16,24},{24,0},{1,9},{9,17},{17,25},{25,1},{2,10},{10... | collective-permute-start | bytes 1572872 | tf_op jit(solution)/shard_map/ppermute | solution.py:149
  233.2 10.8 %collective-permute-start.20 = (bf16[64,32,128]{2,1,0:T(8,128)(2,1)S(1)}, bf16[64,32,128]{2,1,0:T(8,128)(2,1)S(1)}, u32[]{:S(2)}, u32[]{:S(2)}) collective-permute-start(bf16[64,32,128]{2,1,0:T(8,128)(2,1)S(1)} %constant_dynamic-update-slice_fusion.17), channel_id=1, source_target_pairs={{0,24},{8,0},{16,8},{24,16},{1,25},{9,1},{17,9},{25,17},{2,26},{10... | collective-permute-start | bytes 1572872 | tf_op jit(solution)/shard_map/ppermute | solution.py:149
  244.0 7.5 %collective-permute-start.21 = (bf16[32,32,128]{2,1,0:T(8,128)(2,1)S(1)}, bf16[32,32,128]{2,1,0:T(8,128)(2,1)S(1)}, u32[]{:S(2)}, u32[]{:S(2)}) collective-permute-start(bf16[32,32,128]{2,1,0:T(8,128)(2,1)S(1)} %slice.30), channel_id=1, source_target_pairs={{0,8},{8,16},{16,24},{24,0},{1,9},{9,17},{17,25},{25,1},{2,10},{10... | collective-permute-start | bytes 786440 | tf_op jit(solution)/shard_map/ppermute | solution.py:149
  245.1 6.4 %collective-permute-start.22 = (bf16[32,32,128]{2,1,0:T(8,128)(2,1)S(1)}, bf16[32,32,128]{2,1,0:T(8,128)(2,1)S(1)}, u32[]{:S(2)}, u32[]{:S(2)}) collective-permute-start(bf16[32,32,128]{2,1,0:T(8,128)(2,1)S(1)} %slice.31), channel_id=1, source_target_pairs={{0,24},{8,0},{16,8},{24,16},{1,25},{9,1},{17,9},{25,17},{2,26},{10... | collective-permute-start | bytes 786440 | tf_op jit(solution)/shard_map/ppermute | solution.py:149
  251.6 9.4 %collective-permute-start.23 = (bf16[256,32,128]{2,1,0:T(8,128)(2,1)S(1)}, bf16[256,32,128]{2,1,0:T(8,128)(2,1)S(1)}, u32[]{:S(2)}, u32[]{:S(2)}) collective-permute-start(bf16[256,32,128]{2,1,0:T(8,128)(2,1)S(1)} %constant_dynamic-update-slice_fusion.21.refs_0_), channel_id=1, source_target_pairs={{0,1},{1,0},{2,3},{3,2},{4,5},{5,4},{6,7},{7,6},{8,9},{9,8},{10,11... | collective-permute-start | bytes 6291464 | tf_op jit(solution)/shard_map/ppermute | solution.py:149
  270.0 35.0 %all-to-all-start.5 = ((bf16[128,32,128]{2,1,0:T(8,128)(2,1)}), bf16[128,32,128]{2,1,0:T(8,128)(2,1)S(1)}, u32[]{:S(2)}, u32[]{:S(2)}) async-start(bf16[128,32,128]{2,1,0:T(8,128)(2,1)} %get-tuple-element.59), calls=%async_computation.5 | async-start | bytes 2097152 | tf_op jit(solution)/shard_map/all_to_all | solution.py:171
  305.0 4.7 %copy-start.9 = (s32[16,128]{1,0:T(8,128)S(1)}, s32[16,128]{1,0:T(8,128)}, u32[]{:S(2)}) copy-start(s32[16,128]{1,0:T(8,128)} %param.10) | copy-start | bytes 24580
  305.0 4.8 %copy-start.3 = (f32[16,64,128]{2,1,0:T(8,128)S(1)}, f32[16,64,128]{2,1,0:T(8,128)}, u32[]{:S(2)}) copy-start(f32[16,64,128]{2,1,0:T(8,128)} %param.6) | copy-start | bytes 1572868
  305.0 4.8 %copy-start.5 = (f32[16,32,128]{2,1,0:T(8,128)S(1)}, f32[16,32,128]{2,1,0:T(8,128)}, u32[]{:S(2)}) copy-start(f32[16,32,128]{2,1,0:T(8,128)} %copy-done.4) | copy-start | bytes 786436
  305.0 19.2 %all-to-all-start.4 = ((bf16[128,32,128]{2,1,0:T(8,128)(2,1)}), bf16[128,32,128]{2,1,0:T(8,128)(2,1)S(1)}, u32[]{:S(2)}, u32[]{:S(2)}) async-start(bf16[128,32,128]{2,1,0:T(8,128)(2,1)} %get-tuple-element.62), calls=%async_computation.4 | async-start | bytes 2097152 | tf_op jit(solution)/shard_map/all_to_all | solution.py:171
  311.8 13.7 %copy-start.7 = (f32[16,32,128]{2,1,0:T(8,128)S(1)}, f32[16,32,128]{2,1,0:T(8,128)}, u32[]{:S(2)}) copy-start(f32[16,32,128]{2,1,0:T(8,128)} %get-tuple-element.66) | copy-start | bytes 786436
  311.8 13.7 %copy-start.8 = (f32[16,32,128]{2,1,0:T(8,128)S(1)}, f32[16,32,128]{2,1,0:T(8,128)}, u32[]{:S(2)}) copy-start(f32[16,32,128]{2,1,0:T(8,128)} %get-tuple-element.67) | copy-start | bytes 786436
Sparse Core Ops, SparseCore 0:
  11.1 64.6 all-gather.3
  124.8 67.6 all-gather.5
  232.1 65.6 all-gather.7

commit v6 on v5

--- a/solution.py
+++ b/solution.py
@@ -204,21 +204,18 @@
         last = iteration + 1 == STEPS
         near = pass_on(near)
         own_b, send_b = products(src, dst, place, [near, turn(near, "core", 1)], blocks, span)
-        state_b = state_b + add_rows(own_b, exchange_rows(send_b))
+        own_a, send_a = products(src, dst, place, [after(whole, send_b)], blocks, span)
+        got_b = after(exchange_rows(send_b), send_a)
+        got_a = exchange_rows(after(send_a, got_b))
+        state_b = state_b + add_rows(own_b, got_b)
         sum_b = sum_b + weights[iteration + 1] * reward_f * state_b
-        low_b = state_b.astype(jnp.bfloat16)
-        whole = after(whole, low_b if iteration == 1 else send_b)
-        own_a, send_a = products(src, dst, place, [whole], blocks, span)
-        got_a = exchange_rows(send_a)
-        if not last:
-            column = jnp.concatenate(after(spread_z(low_b), send_a), axis=0)
-            got_a = after(got_a, column)
         state_a = state_a + add_rows(own_a, got_a)
         sum_a = sum_a + weights[iteration + 1] * reward_f * state_a
         if not last:
             low_a = state_a.astype(jnp.bfloat16)
             whole = lax.all_gather(low_a, COL, axis=0, tiled=True)
-            near = after(spread_x(column), low_a)
+            low_b = after(state_b.astype(jnp.bfloat16), low_a)
+            near = spread_x(jnp.concatenate(spread_z(low_b), axis=0))
     return (
         jnp.concatenate([state_a, state_b], axis=1),
         jnp.concatenate([sum_a, sum_b], axis=1),

time: 334 us -> 317 us (0.949)
  waiting for transfers between devices: 142 us -> 112 us
  starting transfers between devices: 84.9 us -> 92.3 us
  blocking collectives: 31.6 us -> 36.1 us
    ppermute x24, waiting for transfers between devices: 100 us -> 75.5 us  [turn(): return lax.ppermute(value, axis, [(i, (i + by) % n) for i in range(n)])]
    all_gather x2, waiting for transfers between devices: 21.1 us -> 0.03 us  [shards(): whole = lax.all_gather(low_a, COL, axis=0, tiled=True)]
    all_to_all x5 -> x4, waiting for transfers between devices: 20.4 us -> 36.7 us  [exchange_rows(): return lax.all_to_all(send, ROW, 0, 0, tiled=True)]
    all_to_all x5 -> x4, starting transfers between devices: 26 us -> 30.5 us  [exchange_rows(): return lax.all_to_all(send, ROW, 0, 0, tiled=True)]
    all_to_all x1 -> x2, blocking collectives: 31.6 us -> 36.1 us  [exchange_rows(): return lax.all_to_all(send, ROW, 0, 0, tiled=True)]
  transfers between devices with their start and end apart: 32 -> 31, of which waited for: 19 -> 21; matrix products, arithmetic and copies ran while one was open for 1% -> 1% of each run, Pallas kernels for 13% -> 15%
where the time goes in v6:
time: 317 us; the launch traced here: 315 us
  waiting for transfers between devices  112 us (35%)
  starting transfers between devices  92.3 us (29%)
  Pallas kernels  48.5 us (15%)
  blocking collectives  36.1 us (11%)
  between operations  15 us (5%)
  other arithmetic  7.24 us (2%)
    ppermute x24, waiting for transfers between devices, turn(): return lax.ppermute(value, axis, [(i, (i + by) % n) for i in range(n)])  75.5 us
    ppermute x24, starting transfers between devices, turn(): return lax.ppermute(value, axis, [(i, (i + by) % n) for i in range(n)])  61.6 us
    pallas_call x6, Pallas kernels, products(): pl.pallas_call(body, out_shape=[jax.ShapeDtypeStruct(piece, jnp.float32),...  48.5 us
    all_to_all x4, waiting for transfers between devices, exchange_rows(): return lax.all_to_all(send, ROW, 0, 0, tiled=True)  36.7 us
    all_to_all x2, blocking collectives, exchange_rows(): return lax.all_to_all(send, ROW, 0, 0, tiled=True)  36.1 us
    all_to_all x4, starting transfers between devices, exchange_rows(): return lax.all_to_all(send, ROW, 0, 0, tiled=True)  30.5 us
  transfers between devices with their start and end apart: 31, of which 21 were waited for; matrix products, arithmetic and copies ran while one was open for 1% of the time, Pallas kernels for 15%

profile of v6, /device:TPU:1, one launch (start us, length us, event | category | flops | bytes accessed | tf_op | source)
XLA Modules:
  0.0 314.6 jit_solution(2237106346614791525)
XLA Ops:
  7.2 1.8 constant_dynamic-update-slice_fusion.7
  9.0 3.9 %collective-permute-start = (bf16[16,32,128]{2,1,0:T(8,128)(2,1)S(1)}, bf16[16,32,128]{2,1,0:T(8,128)(2,1)S(1)}, u32[]{:S(2)}, u32[]{:S(2)}) collective-permute-start(bf16[16,32,128]{2,1,0:T(8,128)(2,1)S(1)} %get-tuple-element.61), channel_id=1, source_target_pairs={{0,2},{2,4},{4,6},{6,0},{1,3},{3,5},{5,7},{7,1},{8,10},{10,12},{12... | collective-permute-start | bytes 393224 | tf_op jit(solution)/shard_map/ppermute | solution.py:149
  12.9 3.1 collective-permute-start.1
  16.0 4.4 %collective-permute-start.2 = (bf16[16,32,128]{2,1,0:T(8,128)(2,1)S(1)}, bf16[16,32,128]{2,1,0:T(8,128)(2,1)S(1)}, u32[]{:S(2)}, u32[]{:S(2)}) collective-permute-start(bf16[16,32,128]{2,1,0:T(8,128)(2,1)S(1)} %get-tuple-element.61), channel_id=1, source_target_pairs={{0,4},{2,6},{4,0},{6,2},{1,5},{3,7},{5,1},{7,3},{8,12},{10,14},{12... | collective-permute-start | bytes 393224 | tf_op jit(solution)/shard_map/ppermute | solution.py:149
  20.4 6.1 %collective-permute-done.1 = bf16[16,32,128]{2,1,0:T(8,128)(2,1)S(1)} collective-permute-done((bf16[16,32,128]{2,1,0:T(8,128)(2,1)S(1)}, bf16[16,32,128]{2,1,0:T(8,128)(2,1)S(1)}, u32[]{:S(2)}, u32[]{:S(2)}) %collective-permute-start.1) | collective-permute-done | bytes 131104 | tf_op jit(solution)/shard_map/ppermute | solution.py:149
  26.5 1.8 collective-permute-done.2
  31.2 12.5 %collective-permute-done.3 = bf16[64,32,128]{2,1,0:T(8,128)(2,1)S(1)} collective-permute-done((bf16[64,32,128]{2,1,0:T(8,128)(2,1)S(1)}, bf16[64,32,128]{2,1,0:T(8,128)(2,1)S(1)}, u32[]{:S(2)}, u32[]{:S(2)}) %collective-permute-start.3) | collective-permute-done | bytes 524320 | tf_op jit(solution)/shard_map/ppermute | solution.py:149
  43.9 2.7 collective-permute-start.6
  46.8 4.3 %collective-permute-done.5 = bf16[32,32,128]{2,1,0:T(8,128)(2,1)S(1)} collective-permute-done((bf16[32,32,128]{2,1,0:T(8,128)(2,1)S(1)}, bf16[32,32,128]{2,1,0:T(8,128)(2,1)S(1)}, u32[]{:S(2)}, u32[]{:S(2)}) %collective-permute-start.5) | collective-permute-done | bytes 262176 | tf_op jit(solution)/shard_map/ppermute | solution.py:149
  51.2 4.1 %collective-permute-start.7 = (bf16[256,32,128]{2,1,0:T(8,128)(2,1)S(1)}, bf16[256,32,128]{2,1,0:T(8,128)(2,1)}, u32[]{:S(2)}, u32[]{:S(2)}) collective-permute-start(bf16[256,32,128]{2,1,0:T(8,128)(2,1)S(1)} %constant_dynamic-update-slice_fusion.refs_0_), channel_id=1, source_target_pairs={{0,1},{1,0},{2,3},{3,2},{4,5},{5,4},{6,7},{7,6},{8,9},{9,8},{10,11... | collective-permute-start | bytes 6291464 | tf_op jit(solution)/shard_map/ppermute | solution.py:149
  55.5 3.8 %collective-permute-done.7.refs_1_ = bf16[256,32,128]{2,1,0:T(8,128)(2,1)} collective-permute-done((bf16[256,32,128]{2,1,0:T(8,128)(2,1)S(1)}, bf16[256,32,128]{2,1,0:T(8,128)(2,1)}, u32[]{:S(2)}, u32[]{:S(2)}) %collective-permute-start.7) | collective-permute-done | bytes 2097184 | tf_op jit(solution)/shard_map/ppermute | solution.py:149
  59.3 10.7 %products.6 = (f32[16,32,128]{2,1,0:T(8,128)S(1)}, bf16[128,32,128]{2,1,0:T(8,128)(2,1)}) custom-call(s32[256]{0:T(256)S(1)} %bitcast.45, s32[256]{0:T(256)S(1)} %bitcast.51, s32[33]{0:T(128)S(1)} %stack.135.place, bf16[256,32,128]{2,1,0:T(8,128)(2,1)S(1)} %constant_dynamic-update-slice_fusion.refs_0_, bf16[256,32,128]{2,1,0:T(8,128)(2,1)} %collective-permute-done.7.refs_1_, ...), custom_call_target="tpu_custom_call" | custom-call | flops 268435456 | bytes 12582912 | tf_op jit(solution)/shard_map/products/pallas_call | solution.py:127
  70.0 8.4 %all-to-all-start = ((bf16[128,32,128]{2,1,0:T(8,128)(2,1)}), bf16[128,32,128]{2,1,0:T(8,128)(2,1)S(1)}, u32[]{:S(2)}, u32[]{:S(2)}) async-start(bf16[128,32,128]{2,1,0:T(8,128)(2,1)} %get-tuple-element.25), calls=%async_computation | async-start | bytes 2097152 | tf_op jit(solution)/shard_map/all_to_all | solution.py:171
  78.5 6.2 %products.7 = (f32[16,32,128]{2,1,0:T(8,128)S(1)}, bf16[128,32,128]{2,1,0:T(8,128)(2,1)S(1)}) custom-call(s32[256]{0:T(256)S(1)} %bitcast.46, s32[256]{0:T(256)S(1)} %bitcast.52, s32[33]{0:T(128)S(1)} %stack.135.place, bf16[512,32,128]{2,1,0:T(8,128)(2,1)} %all-gather.4.cloned.1.call-done.given, bf16[256,128,128]{2,1,0:T(8,128)(2,1)} %bitcast.58), custom_call_target="tpu_custom_call" | custom-call | flops 268435456 | bytes 12582912 | tf_op jit(solution)/shard_map/products/pallas_call | solution.py:127
  84.7 8.9 %all-to-all-done = bf16[128,32,128]{2,1,0:T(8,128)(2,1)S(1)} async-done(((bf16[128,32,128]{2,1,0:T(8,128)(2,1)}), bf16[128,32,128]{2,1,0:T(8,128)(2,1)S(1)}, u32[]{:S(2)}, u32[]{:S(2)}) %all-to-all-start) | async-done | bytes 1048608 | tf_op jit(solution)/shard_map/all_to_all | solution.py:171
  93.6 18.0 %all_to_all.30 = bf16[128,32,128]{2,1,0:T(8,128)(2,1)S(1)} all-to-all(bf16[128,32,128]{2,1,0:T(8,128)(2,1)S(1)} %get-tuple-element.30), channel_id=1, replica_groups=mesh['y'=4,'zl'=2,'x'=4,'zh'=4,'core'=2] {'y','zl'}, dimensions={0} | all-to-all | bytes 2097152 | tf_op jit(solution)/shard_map/all_to_all | solution.py:171
  112.8 3.6 %collective-permute-start.9 = (bf16[16,32,128]{2,1,0:T(8,128)(2,1)S(1)}, bf16[16,32,128]{2,1,0:T(8,128)(2,1)S(1)}, u32[]{:S(2)}, u32[]{:S(2)}) collective-permute-start(bf16[16,32,128]{2,1,0:T(8,128)(2,1)S(1)} %get-tuple-element.32), channel_id=1, source_target_pairs={{0,6},{2,0},{4,2},{6,4},{1,7},{3,1},{5,3},{7,5},{8,14},{10,8},{12,... | collective-permute-start | bytes 393224 | tf_op jit(solution)/shard_map/ppermute | solution.py:149
  116.4 3.8 %collective-permute-start.10 = (bf16[16,32,128]{2,1,0:T(8,128)(2,1)S(1)}, bf16[16,32,128]{2,1,0:T(8,128)(2,1)S(1)}, u32[]{:S(2)}, u32[]{:S(2)}) collective-permute-start(bf16[16,32,128]{2,1,0:T(8,128)(2,1)S(1)} %get-tuple-element.32), channel_id=1, source_target_pairs={{0,4},{2,6},{4,0},{6,2},{1,5},{3,7},{5,1},{7,3},{8,12},{10,14},{12... | collective-permute-start | bytes 393224 | tf_op jit(solution)/shard_map/ppermute | solution.py:149
  120.3 1.8 collective-permute-done.9
  122.2 3.6 %collective-permute-done.10 = bf16[16,32,128]{2,1,0:T(8,128)(2,1)S(1)} collective-permute-done((bf16[16,32,128]{2,1,0:T(8,128)(2,1)S(1)}, bf16[16,32,128]{2,1,0:T(8,128)(2,1)S(1)}, u32[]{:S(2)}, u32[]{:S(2)}) %collective-permute-start.10) | collective-permute-done | bytes 131104 | tf_op jit(solution)/shard_map/ppermute | solution.py:149
  125.9 3.6 %collective-permute-start.12 = (bf16[64,32,128]{2,1,0:T(8,128)(2,1)S(1)}, bf16[64,32,128]{2,1,0:T(8,128)(2,1)S(1)}, u32[]{:S(2)}, u32[]{:S(2)}) collective-permute-start(bf16[64,32,128]{2,1,0:T(8,128)(2,1)S(1)} %get-tuple-element.71), channel_id=1, source_target_pairs={{0,24},{8,0},{16,8},{24,16},{1,25},{9,1},{17,9},{25,17},{2,26},{10... | collective-permute-start | bytes 1572872 | tf_op jit(solution)/shard_map/ppermute | solution.py:149
  129.6 10.1 %collective-permute-done.11 = bf16[64,32,128]{2,1,0:T(8,128)(2,1)S(1)} collective-permute-done((bf16[64,32,128]{2,1,0:T(8,128)(2,1)S(1)}, bf16[64,32,128]{2,1,0:T(8,128)(2,1)S(1)}, u32[]{:S(2)}, u32[]{:S(2)}) %collective-permute-start.11) | collective-permute-done | bytes 524320 | tf_op jit(solution)/shard_map/ppermute | solution.py:149
  139.8 3.5 %collective-permute-start.14 = (bf16[32,32,128]{2,1,0:T(8,128)(2,1)S(1)}, bf16[32,32,128]{2,1,0:T(8,128)(2,1)S(1)}, u32[]{:S(2)}, u32[]{:S(2)}) collective-permute-start(bf16[32,32,128]{2,1,0:T(8,128)(2,1)S(1)} %slice.35), channel_id=1, source_target_pairs={{0,24},{8,0},{16,8},{24,16},{1,25},{9,1},{17,9},{25,17},{2,26},{10... | collective-permute-start | bytes 786440 | tf_op jit(solution)/shard_map/ppermute | solution.py:149
  143.4 2.8 collective-permute-done.13
  146.6 6.2 %collective-permute-start.15 = (bf16[256,32,128]{2,1,0:T(8,128)(2,1)S(1)}, bf16[256,32,128]{2,1,0:T(8,128)(2,1)S(1)}, u32[]{:S(2)}, u32[]{:S(2)}) collective-permute-start(bf16[256,32,128]{2,1,0:T(8,128)(2,1)S(1)} %constant_dynamic-update-slice_fusion.12.refs_0_), channel_id=1, source_target_pairs={{0,1},{1,0},{2,3},{3,2},{4,5},{5,4},{6,7},{7,6},{8,9},{9,8},{10,11... | collective-permute-start | bytes 6291464 | tf_op jit(solution)/shard_map/ppermute | solution.py:149
  152.8 3.8 %collective-permute-done.15.refs_1_ = bf16[256,32,128]{2,1,0:T(8,128)(2,1)S(1)} collective-permute-done((bf16[256,32,128]{2,1,0:T(8,128)(2,1)S(1)}, bf16[256,32,128]{2,1,0:T(8,128)(2,1)S(1)}, u32[]{:S(2)}, u32[]{:S(2)}) %collective-permute-start.15) | collective-permute-done | bytes 2097184 | tf_op jit(solution)/shard_map/ppermute | solution.py:149
  156.6 9.1 %products.8 = (f32[16,32,128]{2,1,0:T(8,128)S(1)}, bf16[128,32,128]{2,1,0:T(8,128)(2,1)}) custom-call(s32[256]{0:T(256)S(1)} %bitcast.47, s32[256]{0:T(256)S(1)} %bitcast.53, s32[33]{0:T(128)S(1)} %stack.135.place, bf16[256,32,128]{2,1,0:T(8,128)(2,1)S(1)} %constant_dynamic-update-slice_fusion.12.refs_0_, ...), custom_call_target="tpu_custom_call" | custom-call | flops 268435456 | bytes 12582912 | tf_op jit(solution)/shard_map/products/pallas_call | solution.py:127
  165.7 10.9 %all-to-all-start.2 = ((bf16[128,32,128]{2,1,0:T(8,128)(2,1)}), bf16[128,32,128]{2,1,0:T(8,128)(2,1)S(1)}, u32[]{:S(2)}, u32[]{:S(2)}) async-start(bf16[128,32,128]{2,1,0:T(8,128)(2,1)} %get-tuple-element.33), calls=%async_computation.2 | async-start | bytes 2097152 | tf_op jit(solution)/shard_map/all_to_all | solution.py:171
  176.7 6.2 %products.9 = (f32[16,32,128]{2,1,0:T(8,128)S(1)}, bf16[128,32,128]{2,1,0:T(8,128)(2,1)S(1)}) custom-call(s32[256]{0:T(256)S(1)} %bitcast.48, s32[256]{0:T(256)S(1)} %bitcast.54, s32[33]{0:T(128)S(1)} %stack.135.place, bf16[512,32,128]{2,1,0:T(8,128)(2,1)} %all-gather.6.cloned.1.call-done.given, bf16[256,128,128]{2,1,0:T(8,128)(2,1)} %bitcast.60), custom_call_target="tpu_custom_call" | custom-call | flops 268435456 | bytes 12582912 | tf_op jit(solution)/shard_map/products/pallas_call | solution.py:127
  182.9 8.9 %all-to-all-done.2 = bf16[128,32,128]{2,1,0:T(8,128)(2,1)S(1)} async-done(((bf16[128,32,128]{2,1,0:T(8,128)(2,1)}), bf16[128,32,128]{2,1,0:T(8,128)(2,1)S(1)}, u32[]{:S(2)}, u32[]{:S(2)}) %all-to-all-start.2) | async-done | bytes 1048608 | tf_op jit(solution)/shard_map/all_to_all | solution.py:171
  191.8 18.1 %all_to_all.31 = bf16[128,32,128]{2,1,0:T(8,128)(2,1)S(1)} all-to-all(bf16[128,32,128]{2,1,0:T(8,128)(2,1)S(1)} %get-tuple-element.38), channel_id=1, replica_groups=mesh['y'=4,'zl'=2,'x'=4,'zh'=4,'core'=2] {'y','zl'}, dimensions={0} | all-to-all | bytes 2097152 | tf_op jit(solution)/shard_map/all_to_all | solution.py:171
  211.7 3.6 %collective-permute-start.17 = (bf16[16,32,128]{2,1,0:T(8,128)(2,1)S(1)}, bf16[16,32,128]{2,1,0:T(8,128)(2,1)S(1)}, u32[]{:S(2)}, u32[]{:S(2)}) collective-permute-start(bf16[16,32,128]{2,1,0:T(8,128)(2,1)S(1)} %get-tuple-element.40), channel_id=1, source_target_pairs={{0,6},{2,0},{4,2},{6,4},{1,7},{3,1},{5,3},{7,5},{8,14},{10,8},{12,... | collective-permute-start | bytes 393224 | tf_op jit(solution)/shard_map/ppermute | solution.py:149
  215.3 2.8 collective-permute-start.18
  219.1 2.0 collective-permute-done.17
  221.2 4.1 %collective-permute-done.18 = bf16[16,32,128]{2,1,0:T(8,128)(2,1)S(1)} collective-permute-done((bf16[16,32,128]{2,1,0:T(8,128)(2,1)S(1)}, bf16[16,32,128]{2,1,0:T(8,128)(2,1)S(1)}, u32[]{:S(2)}, u32[]{:S(2)}) %collective-permute-start.18) | collective-permute-done | bytes 131104 | tf_op jit(solution)/shard_map/ppermute | solution.py:149
  225.4 2.8 collective-permute-start.20
  228.2 10.1 %collective-permute-done.19 = bf16[64,32,128]{2,1,0:T(8,128)(2,1)S(1)} collective-permute-done((bf16[64,32,128]{2,1,0:T(8,128)(2,1)S(1)}, bf16[64,32,128]{2,1,0:T(8,128)(2,1)S(1)}, u32[]{:S(2)}, u32[]{:S(2)}) %collective-permute-start.19) | collective-permute-done | bytes 524320 | tf_op jit(solution)/shard_map/ppermute | solution.py:149
  238.5 2.7 collective-permute-start.22
  241.4 3.5 %collective-permute-done.21 = bf16[32,32,128]{2,1,0:T(8,128)(2,1)S(1)} collective-permute-done((bf16[32,32,128]{2,1,0:T(8,128)(2,1)S(1)}, bf16[32,32,128]{2,1,0:T(8,128)(2,1)S(1)}, u32[]{:S(2)}, u32[]{:S(2)}) %collective-permute-start.21) | collective-permute-done | bytes 262176 | tf_op jit(solution)/shard_map/ppermute | solution.py:149
  245.0 7.5 %collective-permute-start.23 = (bf16[256,32,128]{2,1,0:T(8,128)(2,1)S(1)}, bf16[256,32,128]{2,1,0:T(8,128)(2,1)S(1)}, u32[]{:S(2)}, u32[]{:S(2)}) collective-permute-start(bf16[256,32,128]{2,1,0:T(8,128)(2,1)S(1)} %constant_dynamic-update-slice_fusion.24.refs_0_), channel_id=1, source_target_pairs={{0,1},{1,0},{2,3},{3,2},{4,5},{5,4},{6,7},{7,6},{8,9},{9,8},{10,11... | collective-permute-start | bytes 6291464 | tf_op jit(solution)/shard_map/ppermute | solution.py:149
  252.5 3.8 %collective-permute-done.23.refs_1_ = bf16[256,32,128]{2,1,0:T(8,128)(2,1)S(1)} collective-permute-done((bf16[256,32,128]{2,1,0:T(8,128)(2,1)S(1)}, bf16[256,32,128]{2,1,0:T(8,128)(2,1)S(1)}, u32[]{:S(2)}, u32[]{:S(2)}) %collective-permute-start.23) | collective-permute-done | bytes 2097184 | tf_op jit(solution)/shard_map/ppermute | solution.py:149
  256.3 9.0 %products.10 = (f32[16,32,128]{2,1,0:T(8,128)S(1)}, bf16[128,32,128]{2,1,0:T(8,128)(2,1)}) custom-call(s32[256]{0:T(256)S(1)} %bitcast.49, s32[256]{0:T(256)S(1)} %bitcast.55, s32[33]{0:T(128)S(1)} %stack.135.place, bf16[256,32,128]{2,1,0:T(8,128)(2,1)S(1)} %constant_dynamic-update-slice_fusion.24.refs_0_, ...), custom_call_target="tpu_custom_call" | custom-call | flops 268435456 | bytes 12582912 | tf_op jit(solution)/shard_map/products/pallas_call | solution.py:127
  265.3 7.5 %all-to-all-start.4 = ((bf16[128,32,128]{2,1,0:T(8,128)(2,1)}), bf16[128,32,128]{2,1,0:T(8,128)(2,1)S(1)}, u32[]{:S(2)}, u32[]{:S(2)}) async-start(bf16[128,32,128]{2,1,0:T(8,128)(2,1)} %get-tuple-element.41), calls=%async_computation.4 | async-start | bytes 2097152 | tf_op jit(solution)/shard_map/all_to_all | solution.py:171
  272.9 7.2 %products.11 = (f32[16,32,128]{2,1,0:T(8,128)S(1)}, bf16[128,32,128]{2,1,0:T(8,128)(2,1)}) custom-call(s32[256]{0:T(256)S(1)} %bitcast.50, s32[256]{0:T(256)S(1)} %bitcast.56, s32[33]{0:T(128)S(1)} %stack.135.place, bf16[512,32,128]{2,1,0:T(8,128)(2,1)} %all-gather.8.cloned.1.call-done.given, bf16[256,128,128]{2,1,0:T(8,128)(2,1)} %bitcast.62), custom_call_target="tpu_custom_call" | custom-call | flops 268435456 | bytes 12582912 | tf_op jit(solution)/shard_map/products/pallas_call | solution.py:127
  280.2 8.0 %all-to-all-done.4 = bf16[128,32,128]{2,1,0:T(8,128)(2,1)S(1)} async-done(((bf16[128,32,128]{2,1,0:T(8,128)(2,1)}), bf16[128,32,128]{2,1,0:T(8,128)(2,1)S(1)}, u32[]{:S(2)}, u32[]{:S(2)}) %all-to-all-start.4) | async-done | bytes 1048608 | tf_op jit(solution)/shard_map/all_to_all | solution.py:171
  288.1 3.7 %all-to-all-start.5 = ((bf16[128,32,128]{2,1,0:T(8,128)(2,1)}), bf16[128,32,128]{2,1,0:T(8,128)(2,1)S(1)}, u32[]{:S(2)}, u32[]{:S(2)}) async-start(bf16[128,32,128]{2,1,0:T(8,128)(2,1)} %get-tuple-element.46), calls=%async_computation.5 | async-start | bytes 2097152 | tf_op jit(solution)/shard_map/all_to_all | solution.py:171
  292.7 2.1 multiply_add_fusion
  294.8 10.9 %all-to-all-done.5 = bf16[128,32,128]{2,1,0:T(8,128)(2,1)S(1)} async-done(((bf16[128,32,128]{2,1,0:T(8,128)(2,1)}), bf16[128,32,128]{2,1,0:T(8,128)(2,1)S(1)}, u32[]{:S(2)}, u32[]{:S(2)}) %all-to-all-start.5) | async-done | bytes 1048608 | tf_op jit(solution)/shard_map/all_to_all | solution.py:171
  (85 shorter events, 11.4 us)
Async XLA Ops:
  7.2 71.3 %all-gather.4.cloned.1.call-start = ((), (), s32[]{:S(2)}) async-start(), calls=%async_computation.6 | async-start | bytes 4325376 | tf_op jit(solution)/shard_map/all_gather | solution.py:200
  9.0 11.4 %collective-permute-start = (bf16[16,32,128]{2,1,0:T(8,128)(2,1)S(1)}, bf16[16,32,128]{2,1,0:T(8,128)(2,1)S(1)}, u32[]{:S(2)}, u32[]{:S(2)}) collective-permute-start(bf16[16,32,128]{2,1,0:T(8,128)(2,1)S(1)} %get-tuple-element.61), channel_id=1, source_target_pairs={{0,2},{2,4},{4,6},{6,0},{1,3},{3,5},{5,7},{7,1},{8,10},{10,12},{12... | collective-permute-start | bytes 393224 | tf_op jit(solution)/shard_map/ppermute | solution.py:149
  12.9 13.6 %collective-permute-start.1 = (bf16[16,32,128]{2,1,0:T(8,128)(2,1)S(1)}, bf16[16,32,128]{2,1,0:T(8,128)(2,1)S(1)}, u32[]{:S(2)}, u32[]{:S(2)}) collective-permute-start(bf16[16,32,128]{2,1,0:T(8,128)(2,1)S(1)} %get-tuple-element.61), channel_id=1, source_target_pairs={{0,6},{2,0},{4,2},{6,4},{1,7},{3,1},{5,3},{7,5},{8,14},{10,8},{12,... | collective-permute-start | bytes 393224 | tf_op jit(solution)/shard_map/ppermute | solution.py:149
  16.0 12.3 %collective-permute-start.2 = (bf16[16,32,128]{2,1,0:T(8,128)(2,1)S(1)}, bf16[16,32,128]{2,1,0:T(8,128)(2,1)S(1)}, u32[]{:S(2)}, u32[]{:S(2)}) collective-permute-start(bf16[16,32,128]{2,1,0:T(8,128)(2,1)S(1)} %get-tuple-element.61), channel_id=1, source_target_pairs={{0,4},{2,6},{4,0},{6,2},{1,5},{3,7},{5,1},{7,3},{8,12},{10,14},{12... | collective-permute-start | bytes 393224 | tf_op jit(solution)/shard_map/ppermute | solution.py:149
  28.4 15.3 %collective-permute-start.3 = (bf16[64,32,128]{2,1,0:T(8,128)(2,1)S(1)}, bf16[64,32,128]{2,1,0:T(8,128)(2,1)S(1)}, u32[]{:S(2)}, u32[]{:S(2)}) collective-permute-start(bf16[64,32,128]{2,1,0:T(8,128)(2,1)S(1)} %pad_maximum_fusion), channel_id=1, source_target_pairs={{0,8},{8,16},{16,24},{24,0},{1,9},{9,17},{17,25},{25,1},{2,10},{10... | collective-permute-start | bytes 1572872 | tf_op jit(solution)/shard_map/ppermute | solution.py:149
  29.7 14.2 %collective-permute-start.4 = (bf16[64,32,128]{2,1,0:T(8,128)(2,1)S(1)}, bf16[64,32,128]{2,1,0:T(8,128)(2,1)S(1)}, u32[]{:S(2)}, u32[]{:S(2)}) collective-permute-start(bf16[64,32,128]{2,1,0:T(8,128)(2,1)S(1)} %pad_maximum_fusion), channel_id=1, source_target_pairs={{0,24},{8,0},{16,8},{24,16},{1,25},{9,1},{17,9},{25,17},{2,26},{10... | collective-permute-start | bytes 1572872 | tf_op jit(solution)/shard_map/ppermute | solution.py:149
  43.7 7.4 %collective-permute-start.5 = (bf16[32,32,128]{2,1,0:T(8,128)(2,1)S(1)}, bf16[32,32,128]{2,1,0:T(8,128)(2,1)S(1)}, u32[]{:S(2)}, u32[]{:S(2)}) collective-permute-start(bf16[32,32,128]{2,1,0:T(8,128)(2,1)S(1)} %slice.32), channel_id=1, source_target_pairs={{0,8},{8,16},{16,24},{24,0},{1,9},{9,17},{17,25},{25,1},{2,10},{10... | collective-permute-start | bytes 786440 | tf_op jit(solution)/shard_map/ppermute | solution.py:149
  43.9 15.4 %copy-start = (s32[1,1,256]{2,1,0:T(1,128)S(1)}, s32[1,1,256]{2,1,0:T(1,128)}, u32[]{:S(2)}) copy-start(s32[1,1,256]{2,1,0:T(1,128)} %param.8) | copy-start | bytes 3076
  43.9 15.4 %copy-start.1 = (s32[1,1,256]{2,1,0:T(1,128)S(1)}, s32[1,1,256]{2,1,0:T(1,128)}, u32[]{:S(2)}) copy-start(s32[1,1,256]{2,1,0:T(1,128)} %param.9) | copy-start | bytes 3076
  43.9 7.2 %collective-permute-start.6 = (bf16[32,32,128]{2,1,0:T(8,128)(2,1)S(1)}, bf16[32,32,128]{2,1,0:T(8,128)(2,1)S(1)}, u32[]{:S(2)}, u32[]{:S(2)}) collective-permute-start(bf16[32,32,128]{2,1,0:T(8,128)(2,1)S(1)} %slice.33), channel_id=1, source_target_pairs={{0,24},{8,0},{16,8},{24,16},{1,25},{9,1},{17,9},{25,17},{2,26},{10... | collective-permute-start | bytes 786440 | tf_op jit(solution)/shard_map/ppermute | solution.py:149
  51.2 8.0 %collective-permute-start.7 = (bf16[256,32,128]{2,1,0:T(8,128)(2,1)S(1)}, bf16[256,32,128]{2,1,0:T(8,128)(2,1)}, u32[]{:S(2)}, u32[]{:S(2)}) collective-permute-start(bf16[256,32,128]{2,1,0:T(8,128)(2,1)S(1)} %constant_dynamic-update-slice_fusion.refs_0_), channel_id=1, source_target_pairs={{0,1},{1,0},{2,3},{3,2},{4,5},{5,4},{6,7},{7,6},{8,9},{9,8},{10,11... | collective-permute-start | bytes 6291464 | tf_op jit(solution)/shard_map/ppermute | solution.py:149
  70.0 23.6 %all-to-all-start = ((bf16[128,32,128]{2,1,0:T(8,128)(2,1)}), bf16[128,32,128]{2,1,0:T(8,128)(2,1)S(1)}, u32[]{:S(2)}, u32[]{:S(2)}) async-start(bf16[128,32,128]{2,1,0:T(8,128)(2,1)} %get-tuple-element.25), calls=%async_computation | async-start | bytes 2097152 | tf_op jit(solution)/shard_map/all_to_all | solution.py:171
  78.4 98.2 %all-gather.6.cloned.1.call-start = ((), (), s32[]{:S(2)}) async-start(), calls=%async_computation.7 | async-start | bytes 4325376 | tf_op jit(solution)/shard_map/all_gather | solution.py:216
  84.7 27.0 %copy-start.2 = (f32[16,64,128]{2,1,0:T(8,128)S(1)}, f32[16,64,128]{2,1,0:T(8,128)}, u32[]{:S(2)}) copy-start(f32[16,64,128]{2,1,0:T(8,128)} %param.6) | copy-start | bytes 1572868
  112.5 97.3 %copy-start.4 = (f32[16,32,128]{2,1,0:T(8,128)}, f32[16,32,128]{2,1,0:T(8,128)S(1)}, u32[]{:S(2)}) copy-start(f32[16,32,128]{2,1,0:T(8,128)S(1)} %get-tuple-element.57) | copy-start | bytes 786436
  112.7 98.1 %copy-start.6 = (f32[16,32,128]{2,1,0:T(8,128)}, f32[16,32,128]{2,1,0:T(8,128)S(1)}, u32[]{:S(2)}) copy-start(f32[16,32,128]{2,1,0:T(8,128)S(1)} %get-tuple-element.59) | copy-start | bytes 786436
  112.7 7.5 %collective-permute-start.8 = (bf16[16,32,128]{2,1,0:T(8,128)(2,1)S(1)}, bf16[16,32,128]{2,1,0:T(8,128)(2,1)S(1)}, u32[]{:S(2)}, u32[]{:S(2)}) collective-permute-start(bf16[16,32,128]{2,1,0:T(8,128)(2,1)S(1)} %get-tuple-element.32), channel_id=1, source_target_pairs={{0,2},{2,4},{4,6},{6,0},{1,3},{3,5},{5,7},{7,1},{8,10},{10,12},{12... | collective-permute-start | bytes 393224 | tf_op jit(solution)/shard_map/ppermute | solution.py:149
  112.8 9.3 %collective-permute-start.9 = (bf16[16,32,128]{2,1,0:T(8,128)(2,1)S(1)}, bf16[16,32,128]{2,1,0:T(8,128)(2,1)S(1)}, u32[]{:S(2)}, u32[]{:S(2)}) collective-permute-start(bf16[16,32,128]{2,1,0:T(8,128)(2,1)S(1)} %get-tuple-element.32), channel_id=1, source_target_pairs={{0,6},{2,0},{4,2},{6,4},{1,7},{3,1},{5,3},{7,5},{8,14},{10,8},{12,... | collective-permute-start | bytes 393224 | tf_op jit(solution)/shard_map/ppermute | solution.py:149
  116.4 9.3 %collective-permute-start.10 = (bf16[16,32,128]{2,1,0:T(8,128)(2,1)S(1)}, bf16[16,32,128]{2,1,0:T(8,128)(2,1)S(1)}, u32[]{:S(2)}, u32[]{:S(2)}) collective-permute-start(bf16[16,32,128]{2,1,0:T(8,128)(2,1)S(1)} %get-tuple-element.32), channel_id=1, source_target_pairs={{0,4},{2,6},{4,0},{6,2},{1,5},{3,7},{5,1},{7,3},{8,12},{10,14},{12... | collective-permute-start | bytes 393224 | tf_op jit(solution)/shard_map/ppermute | solution.py:149
  125.8 13.8 %collective-permute-start.11 = (bf16[64,32,128]{2,1,0:T(8,128)(2,1)S(1)}, bf16[64,32,128]{2,1,0:T(8,128)(2,1)S(1)}, u32[]{:S(2)}, u32[]{:S(2)}) collective-permute-start(bf16[64,32,128]{2,1,0:T(8,128)(2,1)S(1)} %get-tuple-element.71), channel_id=1, source_target_pairs={{0,8},{8,16},{16,24},{24,0},{1,9},{9,17},{17,25},{25,1},{2,10},{10... | collective-permute-start | bytes 1572872 | tf_op jit(solution)/shard_map/ppermute | solution.py:149
  125.9 13.9 %collective-permute-start.12 = (bf16[64,32,128]{2,1,0:T(8,128)(2,1)S(1)}, bf16[64,32,128]{2,1,0:T(8,128)(2,1)S(1)}, u32[]{:S(2)}, u32[]{:S(2)}) collective-permute-start(bf16[64,32,128]{2,1,0:T(8,128)(2,1)S(1)} %get-tuple-element.71), channel_id=1, source_target_pairs={{0,24},{8,0},{16,8},{24,16},{1,25},{9,1},{17,9},{25,17},{2,26},{10... | collective-permute-start | bytes 1572872 | tf_op jit(solution)/shard_map/ppermute | solution.py:149
  139.7 6.5 %collective-permute-start.13 = (bf16[32,32,128]{2,1,0:T(8,128)(2,1)S(1)}, bf16[32,32,128]{2,1,0:T(8,128)(2,1)S(1)}, u32[]{:S(2)}, u32[]{:S(2)}) collective-permute-start(bf16[32,32,128]{2,1,0:T(8,128)(2,1)S(1)} %slice.34), channel_id=1, source_target_pairs={{0,8},{8,16},{16,24},{24,0},{1,9},{9,17},{17,25},{25,1},{2,10},{10... | collective-permute-start | bytes 786440 | tf_op jit(solution)/shard_map/ppermute | solution.py:149
  139.8 6.8 %collective-permute-start.14 = (bf16[32,32,128]{2,1,0:T(8,128)(2,1)S(1)}, bf16[32,32,128]{2,1,0:T(8,128)(2,1)S(1)}, u32[]{:S(2)}, u32[]{:S(2)}) collective-permute-start(bf16[32,32,128]{2,1,0:T(8,128)(2,1)S(1)} %slice.35), channel_id=1, source_target_pairs={{0,24},{8,0},{16,8},{24,16},{1,25},{9,1},{17,9},{25,17},{2,26},{10... | collective-permute-start | bytes 786440 | tf_op jit(solution)/shard_map/ppermute | solution.py:149
  146.6 10.0 %collective-permute-start.15 = (bf16[256,32,128]{2,1,0:T(8,128)(2,1)S(1)}, bf16[256,32,128]{2,1,0:T(8,128)(2,1)S(1)}, u32[]{:S(2)}, u32[]{:S(2)}) collective-permute-start(bf16[256,32,128]{2,1,0:T(8,128)(2,1)S(1)} %constant_dynamic-update-slice_fusion.12.refs_0_), channel_id=1, source_target_pairs={{0,1},{1,0},{2,3},{3,2},{4,5},{5,4},{6,7},{7,6},{8,9},{9,8},{10,11... | collective-permute-start | bytes 6291464 | tf_op jit(solution)/shard_map/ppermute | solution.py:149
  165.7 26.1 %all-to-all-start.2 = ((bf16[128,32,128]{2,1,0:T(8,128)(2,1)}), bf16[128,32,128]{2,1,0:T(8,128)(2,1)S(1)}, u32[]{:S(2)}, u32[]{:S(2)}) async-start(bf16[128,32,128]{2,1,0:T(8,128)(2,1)} %get-tuple-element.33), calls=%async_computation.2 | async-start | bytes 2097152 | tf_op jit(solution)/shard_map/all_to_all | solution.py:171
  176.6 96.3 %all-gather.8.cloned.1.call-start = ((), (), s32[]{:S(2)}) async-start(), calls=%async_computation.8 | async-start | bytes 4325376 | tf_op jit(solution)/shard_map/all_gather | solution.py:216
  211.7 7.4 %collective-permute-start.16 = (bf16[16,32,128]{2,1,0:T(8,128)(2,1)S(1)}, bf16[16,32,128]{2,1,0:T(8,128)(2,1)S(1)}, u32[]{:S(2)}, u32[]{:S(2)}) collective-permute-start(bf16[16,32,128]{2,1,0:T(8,128)(2,1)S(1)} %get-tuple-element.40), channel_id=1, source_target_pairs={{0,2},{2,4},{4,6},{6,0},{1,3},{3,5},{5,7},{7,1},{8,10},{10,12},{12... | collective-permute-start | bytes 393224 | tf_op jit(solution)/shard_map/ppermute | solution.py:149
  211.7 9.4 %collective-permute-start.17 = (bf16[16,32,128]{2,1,0:T(8,128)(2,1)S(1)}, bf16[16,32,128]{2,1,0:T(8,128)(2,1)S(1)}, u32[]{:S(2)}, u32[]{:S(2)}) collective-permute-start(bf16[16,32,128]{2,1,0:T(8,128)(2,1)S(1)} %get-tuple-element.40), channel_id=1, source_target_pairs={{0,6},{2,0},{4,2},{6,4},{1,7},{3,1},{5,3},{7,5},{8,14},{10,8},{12,... | collective-permute-start | bytes 393224 | tf_op jit(solution)/shard_map/ppermute | solution.py:149
  215.3 9.9 %collective-permute-start.18 = (bf16[16,32,128]{2,1,0:T(8,128)(2,1)S(1)}, bf16[16,32,128]{2,1,0:T(8,128)(2,1)S(1)}, u32[]{:S(2)}, u32[]{:S(2)}) collective-permute-start(bf16[16,32,128]{2,1,0:T(8,128)(2,1)S(1)} %get-tuple-element.40), channel_id=1, source_target_pairs={{0,4},{2,6},{4,0},{6,2},{1,5},{3,7},{5,1},{7,3},{8,12},{10,14},{12... | collective-permute-start | bytes 393224 | tf_op jit(solution)/shard_map/ppermute | solution.py:149
  225.3 13.0 %collective-permute-start.19 = (bf16[64,32,128]{2,1,0:T(8,128)(2,1)S(1)}, bf16[64,32,128]{2,1,0:T(8,128)(2,1)S(1)}, u32[]{:S(2)}, u32[]{:S(2)}) collective-permute-start(bf16[64,32,128]{2,1,0:T(8,128)(2,1)S(1)} %get-tuple-element.63), channel_id=1, source_target_pairs={{0,8},{8,16},{16,24},{24,0},{1,9},{9,17},{17,25},{25,1},{2,10},{10... | collective-permute-start | bytes 1572872 | tf_op jit(solution)/shard_map/ppermute | solution.py:149
  225.4 13.1 %collective-permute-start.20 = (bf16[64,32,128]{2,1,0:T(8,128)(2,1)S(1)}, bf16[64,32,128]{2,1,0:T(8,128)(2,1)S(1)}, u32[]{:S(2)}, u32[]{:S(2)}) collective-permute-start(bf16[64,32,128]{2,1,0:T(8,128)(2,1)S(1)} %get-tuple-element.63), channel_id=1, source_target_pairs={{0,24},{8,0},{16,8},{24,16},{1,25},{9,1},{17,9},{25,17},{2,26},{10... | collective-permute-start | bytes 1572872 | tf_op jit(solution)/shard_map/ppermute | solution.py:149
  238.4 6.5 %collective-permute-start.21 = (bf16[32,32,128]{2,1,0:T(8,128)(2,1)S(1)}, bf16[32,32,128]{2,1,0:T(8,128)(2,1)S(1)}, u32[]{:S(2)}, u32[]{:S(2)}) collective-permute-start(bf16[32,32,128]{2,1,0:T(8,128)(2,1)S(1)} %slice.36), channel_id=1, source_target_pairs={{0,8},{8,16},{16,24},{24,0},{1,9},{9,17},{17,25},{25,1},{2,10},{10... | collective-permute-start | bytes 786440 | tf_op jit(solution)/shard_map/ppermute | solution.py:149
  238.5 6.4 %collective-permute-start.22 = (bf16[32,32,128]{2,1,0:T(8,128)(2,1)S(1)}, bf16[32,32,128]{2,1,0:T(8,128)(2,1)S(1)}, u32[]{:S(2)}, u32[]{:S(2)}) collective-permute-start(bf16[32,32,128]{2,1,0:T(8,128)(2,1)S(1)} %slice.37), channel_id=1, source_target_pairs={{0,24},{8,0},{16,8},{24,16},{1,25},{9,1},{17,9},{25,17},{2,26},{10... | collective-permute-start | bytes 786440 | tf_op jit(solution)/shard_map/ppermute | solution.py:149
  245.0 11.3 %collective-permute-start.23 = (bf16[256,32,128]{2,1,0:T(8,128)(2,1)S(1)}, bf16[256,32,128]{2,1,0:T(8,128)(2,1)S(1)}, u32[]{:S(2)}, u32[]{:S(2)}) collective-permute-start(bf16[256,32,128]{2,1,0:T(8,128)(2,1)S(1)} %constant_dynamic-update-slice_fusion.24.refs_0_), channel_id=1, source_target_pairs={{0,1},{1,0},{2,3},{3,2},{4,5},{5,4},{6,7},{7,6},{8,9},{9,8},{10,11... | collective-permute-start | bytes 6291464 | tf_op jit(solution)/shard_map/ppermute | solution.py:149
  265.3 22.8 %all-to-all-start.4 = ((bf16[128,32,128]{2,1,0:T(8,128)(2,1)}), bf16[128,32,128]{2,1,0:T(8,128)(2,1)S(1)}, u32[]{:S(2)}, u32[]{:S(2)}) async-start(bf16[128,32,128]{2,1,0:T(8,128)(2,1)} %get-tuple-element.41), calls=%async_computation.4 | async-start | bytes 2097152 | tf_op jit(solution)/shard_map/all_to_all | solution.py:171
  280.1 12.5 %copy-start.9 = (s32[16,128]{1,0:T(8,128)S(1)}, s32[16,128]{1,0:T(8,128)}, u32[]{:S(2)}) copy-start(s32[16,128]{1,0:T(8,128)} %param.10) | copy-start | bytes 24580
  280.2 12.6 %copy-start.3 = (f32[16,64,128]{2,1,0:T(8,128)S(1)}, f32[16,64,128]{2,1,0:T(8,128)}, u32[]{:S(2)}) copy-start(f32[16,64,128]{2,1,0:T(8,128)} %param.6) | copy-start | bytes 1572868
  288.1 17.6 %copy-start.5 = (f32[16,32,128]{2,1,0:T(8,128)S(1)}, f32[16,32,128]{2,1,0:T(8,128)}, u32[]{:S(2)}) copy-start(f32[16,32,128]{2,1,0:T(8,128)} %copy-done.4) | copy-start | bytes 786436
  288.1 17.6 %all-to-all-start.5 = ((bf16[128,32,128]{2,1,0:T(8,128)(2,1)}), bf16[128,32,128]{2,1,0:T(8,128)(2,1)S(1)}, u32[]{:S(2)}, u32[]{:S(2)}) async-start(bf16[128,32,128]{2,1,0:T(8,128)(2,1)} %get-tuple-element.46), calls=%async_computation.5 | async-start | bytes 2097152 | tf_op jit(solution)/shard_map/all_to_all | solution.py:171
  294.8 12.2 %copy-start.7 = (f32[16,32,128]{2,1,0:T(8,128)S(1)}, f32[16,32,128]{2,1,0:T(8,128)}, u32[]{:S(2)}) copy-start(f32[16,32,128]{2,1,0:T(8,128)} %get-tuple-element.50) | copy-start | bytes 786436
  294.8 12.2 %copy-start.8 = (f32[16,32,128]{2,1,0:T(8,128)S(1)}, f32[16,32,128]{2,1,0:T(8,128)}, u32[]{:S(2)}) copy-start(f32[16,32,128]{2,1,0:T(8,128)} %get-tuple-element.51) | copy-start | bytes 786436
Sparse Core Ops, SparseCore 0:
  11.1 64.6 all-gather.3
  112.7 60.9 all-gather.5
  210.9 59.9 all-gather.7

commit v7 on v6

--- a/solution.py
+++ b/solution.py
@@ -134,7 +134,7 @@
             out_specs=[pl.BlockSpec(piece, lambda i, *_: (0, 0, 0)), pl.BlockSpec(send, lambda i, *_: (0, 0, 0))],
             scratch_shapes=scratch,
         ),
-        compiler_params=pltpu.CompilerParams(vmem_limit_bytes=24 << 20),
+        compiler_params=pltpu.CompilerParams(vmem_limit_bytes=(20 if len(given) == 1 else 15) << 20),
         cost_estimate=pl.CostEstimate(
             flops=2 * n * configs * block_len * block_len,
             bytes_accessed=2 * (sources * configs * block_len + n * block_len * block_len),
@@ -163,8 +163,8 @@
 
 def pass_on(near):
     half = near[0].shape[0] // 2
-    near = near + [turn(near[1][:half], "x", 1), turn(near[2][half:], "x", 3)]
-    return jnp.concatenate(near, axis=0)
+    later = [turn(near[1][:half], "x", 1), turn(near[2][half:], "x", 3)]
+    return [jnp.concatenate(near, axis=0), jnp.concatenate(later, axis=0)]
 
 
 def exchange_rows(send):
@@ -203,7 +203,8 @@
     for iteration in range(STEPS):
         last = iteration + 1 == STEPS
         near = pass_on(near)
-        own_b, send_b = products(src, dst, place, [near, turn(near, "core", 1)], blocks, span)
+        far = [turn(piece, "core", 1) for piece in near]
+        own_b, send_b = products(src, dst, place, near + far, blocks, span)
         own_a, send_a = products(src, dst, place, [after(whole, send_b)], blocks, span)
         got_b = after(exchange_rows(send_b), send_a)
         got_a = exchange_rows(after(send_a, got_b))

time: 317 us -> 319 us (level)
  waiting for transfers between devices: 112 us -> 118 us
  local copies, waits for them, and re-layouts: 3.1 us -> 7.43 us
  starting transfers between devices: 92.3 us -> 88 us
  Pallas kernels: 48.5 us -> 45.1 us
    ppermute x24 -> x27, waiting for transfers between devices: 75.5 us -> 81 us  [turn(): return lax.ppermute(value, axis, [(i, (i + by) % n) for i in range(n)])]
    unnamed x39 -> x42, local copies, waits for them, and re-layouts: 2.66 us -> 6.11 us
    pallas_call x6, Pallas kernels: 48.5 us -> 45.1 us  [products(): pl.pallas_call(body, out_shape=[jax.ShapeDtypeStruct(piece, jnp.float32),...]
    ppermute x24 -> x27, starting transfers between devices: 61.6 us -> 58.7 us  [turn(): return lax.ppermute(value, axis, [(i, (i + by) % n) for i in range(n)])]
  transfers between devices with their start and end apart: 31 -> 34, of which waited for: 21 -> 23; matrix products, arithmetic and copies ran while one was open for 1% -> 2% of each run, Pallas kernels for 15% -> 14%
where the time goes in v7:
time: 319 us; the launch traced here: 317 us
  waiting for transfers between devices  118 us (37%)
  starting transfers between devices  88 us (28%)
  Pallas kernels  45.1 us (14%)
  blocking collectives  36.3 us (11%)
  between operations  15 us (5%)
  other arithmetic  8.02 us (3%)
  local copies, waits for them, and re-layouts  7.43 us (2%)
    ppermute x27, waiting for transfers between devices, turn(): return lax.ppermute(value, axis, [(i, (i + by) % n) for i in range(n)])  81 us
    ppermute x27, starting transfers between devices, turn(): return lax.ppermute(value, axis, [(i, (i + by) % n) for i in range(n)])  58.7 us
    pallas_call x6, Pallas kernels, products(): pl.pallas_call(body, out_shape=[jax.ShapeDtypeStruct(piece, jnp.float32),...  45.1 us
    all_to_all x4, waiting for transfers between devices, exchange_rows(): return lax.all_to_all(send, ROW, 0, 0, tiled=True)  36.5 us
    all_to_all x2, blocking collectives, exchange_rows(): return lax.all_to_all(send, ROW, 0, 0, tiled=True)  36.3 us
    all_to_all x4, starting transfers between devices, exchange_rows(): return lax.all_to_all(send, ROW, 0, 0, tiled=True)  29.2 us
  transfers between devices with their start and end apart: 34, of which 23 were waited for; matrix products, arithmetic and copies ran while one was open for 2% of the time, Pallas kernels for 14%

profile of v7, /device:TPU:1, one launch (start us, length us, event | category | flops | bytes accessed | tf_op | source)
XLA Modules:
  0.0 317.5 jit_solution(16812562481176559725)
XLA Ops:
  7.2 1.8 constant_dynamic-update-slice_fusion.5
  9.0 3.9 %collective-permute-start = (bf16[16,32,128]{2,1,0:T(8,128)(2,1)S(1)}, bf16[16,32,128]{2,1,0:T(8,128)(2,1)S(1)}, u32[]{:S(2)}, u32[]{:S(2)}) collective-permute-start(bf16[16,32,128]{2,1,0:T(8,128)(2,1)S(1)} %get-tuple-element.61), channel_id=1, source_target_pairs={{0,2},{2,4},{4,6},{6,0},{1,3},{3,5},{5,7},{7,1},{8,10},{10,12},{12... | collective-permute-start | bytes 393224 | tf_op jit(solution)/shard_map/ppermute | solution.py:149
  12.9 3.1 collective-permute-start.1
  16.0 4.4 %collective-permute-start.2 = (bf16[16,32,128]{2,1,0:T(8,128)(2,1)S(1)}, bf16[16,32,128]{2,1,0:T(8,128)(2,1)S(1)}, u32[]{:S(2)}, u32[]{:S(2)}) collective-permute-start(bf16[16,32,128]{2,1,0:T(8,128)(2,1)S(1)} %get-tuple-element.61), channel_id=1, source_target_pairs={{0,4},{2,6},{4,0},{6,2},{1,5},{3,7},{5,1},{7,3},{8,12},{10,14},{12... | collective-permute-start | bytes 393224 | tf_op jit(solution)/shard_map/ppermute | solution.py:149
  20.4 6.1 %collective-permute-done.1 = bf16[16,32,128]{2,1,0:T(8,128)(2,1)S(1)} collective-permute-done((bf16[16,32,128]{2,1,0:T(8,128)(2,1)S(1)}, bf16[16,32,128]{2,1,0:T(8,128)(2,1)S(1)}, u32[]{:S(2)}, u32[]{:S(2)}) %collective-permute-start.1) | collective-permute-done | bytes 131104 | tf_op jit(solution)/shard_map/ppermute | solution.py:149
  26.5 1.8 collective-permute-done.2
  31.2 12.5 %collective-permute-done.3 = bf16[64,32,128]{2,1,0:T(8,128)(2,1)S(1)} collective-permute-done((bf16[64,32,128]{2,1,0:T(8,128)(2,1)S(1)}, bf16[64,32,128]{2,1,0:T(8,128)(2,1)S(1)}, u32[]{:S(2)}, u32[]{:S(2)}) %collective-permute-start.3) | collective-permute-done | bytes 524320 | tf_op jit(solution)/shard_map/ppermute | solution.py:149
  44.0 1.7 collective-permute-start.7
  46.9 1.7 collective-permute-start.6
  48.6 6.4 %collective-permute-done.5 = bf16[32,32,128]{2,1,0:T(8,128)(2,1)S(1)} collective-permute-done((bf16[32,32,128]{2,1,0:T(8,128)(2,1)S(1)}, bf16[32,32,128]{2,1,0:T(8,128)(2,1)S(1)}, u32[]{:S(2)}, u32[]{:S(2)}) %collective-permute-start.5) | collective-permute-done | bytes 262176 | tf_op jit(solution)/shard_map/ppermute | solution.py:149
  56.8 1.8 collective-permute-start.8
  58.8 1.8 collective-permute-done.8.refs_3_
  60.5 9.3 %products.6 = (f32[16,32,128]{2,1,0:T(8,128)S(1)}, bf16[128,32,128]{2,1,0:T(8,128)(2,1)S(1)}) custom-call(s32[256]{0:T(256)S(1)} %bitcast.45, s32[256]{0:T(256)S(1)} %bitcast.51, s32[33]{0:T(128)S(1)} %stack.135.place, bf16[192,32,128]{2,1,0:T(8,128)(2,1)S(1)} %constant_dynamic-update-slice_fusion.refs_0_, ...), custom_call_target="tpu_custom_call" | custom-call | flops 268435456 | bytes 12582912 | tf_op jit(solution)/shard_map/products/pallas_call | solution.py:127
  70.9 9.2 %all-to-all-start = ((bf16[128,32,128]{2,1,0:T(8,128)(2,1)}), bf16[128,32,128]{2,1,0:T(8,128)(2,1)S(1)}, u32[]{:S(2)}, u32[]{:S(2)}) async-start(bf16[128,32,128]{2,1,0:T(8,128)(2,1)} %copy-done), calls=%async_computation | async-start | bytes 2097152 | tf_op jit(solution)/shard_map/all_to_all | solution.py:171
  80.2 6.2 %products.7 = (f32[16,32,128]{2,1,0:T(8,128)S(1)}, bf16[128,32,128]{2,1,0:T(8,128)(2,1)S(1)}) custom-call(s32[256]{0:T(256)S(1)} %bitcast.46, s32[256]{0:T(256)S(1)} %bitcast.52, s32[33]{0:T(128)S(1)} %stack.135.place, bf16[512,32,128]{2,1,0:T(8,128)(2,1)} %all-gather.4.cloned.1.call-done.given, bf16[256,128,128]{2,1,0:T(8,128)(2,1)} %bitcast.58), custom_call_target="tpu_custom_call" | custom-call | flops 268435456 | bytes 12582912 | tf_op jit(solution)/shard_map/products/pallas_call | solution.py:127
  86.4 8.9 %all-to-all-done = bf16[128,32,128]{2,1,0:T(8,128)(2,1)S(1)} async-done(((bf16[128,32,128]{2,1,0:T(8,128)(2,1)}), bf16[128,32,128]{2,1,0:T(8,128)(2,1)S(1)}, u32[]{:S(2)}, u32[]{:S(2)}) %all-to-all-start) | async-done | bytes 1048608 | tf_op jit(solution)/shard_map/all_to_all | solution.py:171
  95.3 18.1 %all_to_all.30 = bf16[128,32,128]{2,1,0:T(8,128)(2,1)S(1)} all-to-all(bf16[128,32,128]{2,1,0:T(8,128)(2,1)S(1)} %get-tuple-element.30), channel_id=1, replica_groups=mesh['y'=4,'zl'=2,'x'=4,'zh'=4,'core'=2] {'y','zl'}, dimensions={0} | all-to-all | bytes 2097152 | tf_op jit(solution)/shard_map/all_to_all | solution.py:171
  115.2 3.6 %collective-permute-start.10 = (bf16[16,32,128]{2,1,0:T(8,128)(2,1)S(1)}, bf16[16,32,128]{2,1,0:T(8,128)(2,1)S(1)}, u32[]{:S(2)}, u32[]{:S(2)}) collective-permute-start(bf16[16,32,128]{2,1,0:T(8,128)(2,1)S(1)} %get-tuple-element.32), channel_id=1, source_target_pairs={{0,6},{2,0},{4,2},{6,4},{1,7},{3,1},{5,3},{7,5},{8,14},{10,8},{12,... | collective-permute-start | bytes 393224 | tf_op jit(solution)/shard_map/ppermute | solution.py:149
  118.8 2.5 collective-permute-start.11
  121.3 1.6 collective-permute-done.9
  124.1 4.5 %collective-permute-done.11 = bf16[16,32,128]{2,1,0:T(8,128)(2,1)S(1)} collective-permute-done((bf16[16,32,128]{2,1,0:T(8,128)(2,1)S(1)}, bf16[16,32,128]{2,1,0:T(8,128)(2,1)S(1)}, u32[]{:S(2)}, u32[]{:S(2)}) %collective-permute-start.11) | collective-permute-done | bytes 131104 | tf_op jit(solution)/shard_map/ppermute | solution.py:149
  130.1 2.7 collective-permute-start.13
  132.8 10.6 %collective-permute-done.12 = bf16[64,32,128]{2,1,0:T(8,128)(2,1)S(1)} collective-permute-done((bf16[64,32,128]{2,1,0:T(8,128)(2,1)S(1)}, bf16[64,32,128]{2,1,0:T(8,128)(2,1)S(1)}, u32[]{:S(2)}, u32[]{:S(2)}) %collective-permute-start.12) | collective-permute-done | bytes 524320 | tf_op jit(solution)/shard_map/ppermute | solution.py:149
  143.6 3.5 %collective-permute-start.16 = (bf16[192,32,128]{2,1,0:T(8,128)(2,1)S(1)}, bf16[192,32,128]{2,1,0:T(8,128)(2,1)S(1)}, u32[]{:S(2)}, u32[]{:S(2)}) collective-permute-start(bf16[192,32,128]{2,1,0:T(8,128)(2,1)S(1)} %constant_dynamic-update-slice_fusion.12.refs_0_), channel_id=1, source_target_pairs={{0,1},{1,0},{2,3},{3,2},{4,5},{5,4},{6,7},{7,6},{8,9},{9,8},{10,11... | collective-permute-start | bytes 4718600 | tf_op jit(solution)/shard_map/ppermute | solution.py:149
  147.8 2.1 collective-permute-start.15
  149.9 9.2 %collective-permute-done.14 = bf16[32,32,128]{2,1,0:T(8,128)(2,1)S(1)} collective-permute-done((bf16[32,32,128]{2,1,0:T(8,128)(2,1)S(1)}, bf16[32,32,128]{2,1,0:T(8,128)(2,1)S(1)}, u32[]{:S(2)}, u32[]{:S(2)}) %collective-permute-start.14) | collective-permute-done | bytes 262176 | tf_op jit(solution)/shard_map/ppermute | solution.py:149
  162.0 8.1 %products.8 = (f32[16,32,128]{2,1,0:T(8,128)S(1)}, bf16[128,32,128]{2,1,0:T(8,128)(2,1)S(1)}) custom-call(s32[256]{0:T(256)S(1)} %bitcast.47, s32[256]{0:T(256)S(1)} %bitcast.53, s32[33]{0:T(128)S(1)} %stack.135.place, bf16[192,32,128]{2,1,0:T(8,128)(2,1)S(1)} %constant_dynamic-update-slice_fusion.12.refs_0_, ...), custom_call_target="tpu_custom_call" | custom-call | flops 268435456 | bytes 12582912 | tf_op jit(solution)/shard_map/products/pallas_call | solution.py:127
  171.1 5.9 %all-to-all-start.2 = ((bf16[128,32,128]{2,1,0:T(8,128)(2,1)}), bf16[128,32,128]{2,1,0:T(8,128)(2,1)S(1)}, u32[]{:S(2)}, u32[]{:S(2)}) async-start(bf16[128,32,128]{2,1,0:T(8,128)(2,1)} %copy-done.1), calls=%async_computation.2 | async-start | bytes 2097152 | tf_op jit(solution)/shard_map/all_to_all | solution.py:171
  177.1 6.2 %products.9 = (f32[16,32,128]{2,1,0:T(8,128)S(1)}, bf16[128,32,128]{2,1,0:T(8,128)(2,1)S(1)}) custom-call(s32[256]{0:T(256)S(1)} %bitcast.48, s32[256]{0:T(256)S(1)} %bitcast.54, s32[33]{0:T(128)S(1)} %stack.135.place, bf16[512,32,128]{2,1,0:T(8,128)(2,1)} %all-gather.6.cloned.1.call-done.given, bf16[256,128,128]{2,1,0:T(8,128)(2,1)} %bitcast.60), custom_call_target="tpu_custom_call" | custom-call | flops 268435456 | bytes 12582912 | tf_op jit(solution)/shard_map/products/pallas_call | solution.py:127
  183.3 8.9 %all-to-all-done.2 = bf16[128,32,128]{2,1,0:T(8,128)(2,1)S(1)} async-done(((bf16[128,32,128]{2,1,0:T(8,128)(2,1)}), bf16[128,32,128]{2,1,0:T(8,128)(2,1)S(1)}, u32[]{:S(2)}, u32[]{:S(2)}) %all-to-all-start.2) | async-done | bytes 1048608 | tf_op jit(solution)/shard_map/all_to_all | solution.py:171
  192.2 18.2 %all_to_all.31 = bf16[128,32,128]{2,1,0:T(8,128)(2,1)S(1)} all-to-all(bf16[128,32,128]{2,1,0:T(8,128)(2,1)S(1)} %get-tuple-element.38), channel_id=1, replica_groups=mesh['y'=4,'zl'=2,'x'=4,'zh'=4,'core'=2] {'y','zl'}, dimensions={0} | all-to-all | bytes 2097152 | tf_op jit(solution)/shard_map/all_to_all | solution.py:171
  212.2 3.6 %collective-permute-start.19 = (bf16[16,32,128]{2,1,0:T(8,128)(2,1)S(1)}, bf16[16,32,128]{2,1,0:T(8,128)(2,1)S(1)}, u32[]{:S(2)}, u32[]{:S(2)}) collective-permute-start(bf16[16,32,128]{2,1,0:T(8,128)(2,1)S(1)} %get-tuple-element.40), channel_id=1, source_target_pairs={{0,6},{2,0},{4,2},{6,4},{1,7},{3,1},{5,3},{7,5},{8,14},{10,8},{12,... | collective-permute-start | bytes 393224 | tf_op jit(solution)/shard_map/ppermute | solution.py:149
  215.8 4.1 %collective-permute-start.20 = (bf16[16,32,128]{2,1,0:T(8,128)(2,1)S(1)}, bf16[16,32,128]{2,1,0:T(8,128)(2,1)S(1)}, u32[]{:S(2)}, u32[]{:S(2)}) collective-permute-start(bf16[16,32,128]{2,1,0:T(8,128)(2,1)S(1)} %get-tuple-element.40), channel_id=1, source_target_pairs={{0,4},{2,6},{4,0},{6,2},{1,5},{3,7},{5,1},{7,3},{8,12},{10,14},{12... | collective-permute-start | bytes 393224 | tf_op jit(solution)/shard_map/ppermute | solution.py:149
  220.0 1.8 collective-permute-done.19
  221.8 2.6 collective-permute-done.20
  224.4 1.9 collective-permute-start.21
  227.9 9.2 %collective-permute-done.21 = bf16[64,32,128]{2,1,0:T(8,128)(2,1)S(1)} collective-permute-done((bf16[64,32,128]{2,1,0:T(8,128)(2,1)S(1)}, bf16[64,32,128]{2,1,0:T(8,128)(2,1)S(1)}, u32[]{:S(2)}, u32[]{:S(2)}) %collective-permute-start.21) | collective-permute-done | bytes 524320 | tf_op jit(solution)/shard_map/ppermute | solution.py:149
  237.7 4.6 %collective-permute-start.25 = (bf16[192,32,128]{2,1,0:T(8,128)(2,1)S(1)}, bf16[192,32,128]{2,1,0:T(8,128)(2,1)S(1)}, u32[]{:S(2)}, u32[]{:S(2)}) collective-permute-start(bf16[192,32,128]{2,1,0:T(8,128)(2,1)S(1)} %constant_dynamic-update-slice_fusion.24.refs_0_), channel_id=1, source_target_pairs={{0,1},{1,0},{2,3},{3,2},{4,5},{5,4},{6,7},{7,6},{8,9},{9,8},{10,11... | collective-permute-start | bytes 4718600 | tf_op jit(solution)/shard_map/ppermute | solution.py:149
  243.7 1.8 collective-permute-start.24
  245.5 6.4 %collective-permute-done.23 = bf16[32,32,128]{2,1,0:T(8,128)(2,1)S(1)} collective-permute-done((bf16[32,32,128]{2,1,0:T(8,128)(2,1)S(1)}, bf16[32,32,128]{2,1,0:T(8,128)(2,1)S(1)}, u32[]{:S(2)}, u32[]{:S(2)}) %collective-permute-start.23) | collective-permute-done | bytes 262176 | tf_op jit(solution)/shard_map/ppermute | solution.py:149
  253.3 1.6 collective-permute-start.26
  256.5 8.1 %products.10 = (f32[16,32,128]{2,1,0:T(8,128)S(1)}, bf16[128,32,128]{2,1,0:T(8,128)(2,1)S(1)}) custom-call(s32[256]{0:T(256)S(1)} %bitcast.49, s32[256]{0:T(256)S(1)} %bitcast.55, s32[33]{0:T(128)S(1)} %stack.135.place, bf16[192,32,128]{2,1,0:T(8,128)(2,1)S(1)} %constant_dynamic-update-slice_fusion.24.refs_0_, ...), custom_call_target="tpu_custom_call" | custom-call | flops 268435456 | bytes 12582912 | tf_op jit(solution)/shard_map/products/pallas_call | solution.py:127
  265.6 10.4 %all-to-all-start.4 = ((bf16[128,32,128]{2,1,0:T(8,128)(2,1)}), bf16[128,32,128]{2,1,0:T(8,128)(2,1)S(1)}, u32[]{:S(2)}, u32[]{:S(2)}) async-start(bf16[128,32,128]{2,1,0:T(8,128)(2,1)} %copy-done.2), calls=%async_computation.4 | async-start | bytes 2097152 | tf_op jit(solution)/shard_map/all_to_all | solution.py:171
  276.0 7.2 %products.11 = (f32[16,32,128]{2,1,0:T(8,128)S(1)}, bf16[128,32,128]{2,1,0:T(8,128)(2,1)}) custom-call(s32[256]{0:T(256)S(1)} %bitcast.50, s32[256]{0:T(256)S(1)} %bitcast.56, s32[33]{0:T(128)S(1)} %stack.135.place, bf16[512,32,128]{2,1,0:T(8,128)(2,1)} %all-gather.8.cloned.1.call-done.given, bf16[256,128,128]{2,1,0:T(8,128)(2,1)} %bitcast.62), custom_call_target="tpu_custom_call" | custom-call | flops 268435456 | bytes 12582912 | tf_op jit(solution)/shard_map/products/pallas_call | solution.py:127
  283.3 7.9 %all-to-all-done.4 = bf16[128,32,128]{2,1,0:T(8,128)(2,1)S(1)} async-done(((bf16[128,32,128]{2,1,0:T(8,128)(2,1)}), bf16[128,32,128]{2,1,0:T(8,128)(2,1)S(1)}, u32[]{:S(2)}, u32[]{:S(2)}) %all-to-all-start.4) | async-done | bytes 1048608 | tf_op jit(solution)/shard_map/all_to_all | solution.py:171
  291.2 3.6 %all-to-all-start.5 = ((bf16[128,32,128]{2,1,0:T(8,128)(2,1)}), bf16[128,32,128]{2,1,0:T(8,128)(2,1)S(1)}, u32[]{:S(2)}, u32[]{:S(2)}) async-start(bf16[128,32,128]{2,1,0:T(8,128)(2,1)} %get-tuple-element.46), calls=%async_computation.5 | async-start | bytes 2097152 | tf_op jit(solution)/shard_map/all_to_all | solution.py:171
  295.7 2.1 multiply_add_fusion
  297.8 10.9 %all-to-all-done.5 = bf16[128,32,128]{2,1,0:T(8,128)(2,1)S(1)} async-done(((bf16[128,32,128]{2,1,0:T(8,128)(2,1)}), bf16[128,32,128]{2,1,0:T(8,128)(2,1)S(1)}, u32[]{:S(2)}, u32[]{:S(2)}) %all-to-all-start.5) | async-done | bytes 1048608 | tf_op jit(solution)/shard_map/all_to_all | solution.py:171
  (97 shorter events, 28.4 us)
Async XLA Ops:
  7.2 73.0 %all-gather.4.cloned.1.call-start = ((), (), s32[]{:S(2)}) async-start(), calls=%async_computation.6 | async-start | bytes 4325376 | tf_op jit(solution)/shard_map/all_gather | solution.py:200
  9.0 11.4 %collective-permute-start = (bf16[16,32,128]{2,1,0:T(8,128)(2,1)S(1)}, bf16[16,32,128]{2,1,0:T(8,128)(2,1)S(1)}, u32[]{:S(2)}, u32[]{:S(2)}) collective-permute-start(bf16[16,32,128]{2,1,0:T(8,128)(2,1)S(1)} %get-tuple-element.61), channel_id=1, source_target_pairs={{0,2},{2,4},{4,6},{6,0},{1,3},{3,5},{5,7},{7,1},{8,10},{10,12},{12... | collective-permute-start | bytes 393224 | tf_op jit(solution)/shard_map/ppermute | solution.py:149
  12.9 13.6 %collective-permute-start.1 = (bf16[16,32,128]{2,1,0:T(8,128)(2,1)S(1)}, bf16[16,32,128]{2,1,0:T(8,128)(2,1)S(1)}, u32[]{:S(2)}, u32[]{:S(2)}) collective-permute-start(bf16[16,32,128]{2,1,0:T(8,128)(2,1)S(1)} %get-tuple-element.61), channel_id=1, source_target_pairs={{0,6},{2,0},{4,2},{6,4},{1,7},{3,1},{5,3},{7,5},{8,14},{10,8},{12,... | collective-permute-start | bytes 393224 | tf_op jit(solution)/shard_map/ppermute | solution.py:149
  16.0 12.3 %collective-permute-start.2 = (bf16[16,32,128]{2,1,0:T(8,128)(2,1)S(1)}, bf16[16,32,128]{2,1,0:T(8,128)(2,1)S(1)}, u32[]{:S(2)}, u32[]{:S(2)}) collective-permute-start(bf16[16,32,128]{2,1,0:T(8,128)(2,1)S(1)} %get-tuple-element.61), channel_id=1, source_target_pairs={{0,4},{2,6},{4,0},{6,2},{1,5},{3,7},{5,1},{7,3},{8,12},{10,14},{12... | collective-permute-start | bytes 393224 | tf_op jit(solution)/shard_map/ppermute | solution.py:149
  28.4 15.4 %collective-permute-start.3 = (bf16[64,32,128]{2,1,0:T(8,128)(2,1)S(1)}, bf16[64,32,128]{2,1,0:T(8,128)(2,1)S(1)}, u32[]{:S(2)}, u32[]{:S(2)}) collective-permute-start(bf16[64,32,128]{2,1,0:T(8,128)(2,1)S(1)} %pad_maximum_fusion), channel_id=1, source_target_pairs={{0,8},{8,16},{16,24},{24,0},{1,9},{9,17},{17,25},{25,1},{2,10},{10... | collective-permute-start | bytes 1572872 | tf_op jit(solution)/shard_map/ppermute | solution.py:149
  29.7 14.2 %collective-permute-start.4 = (bf16[64,32,128]{2,1,0:T(8,128)(2,1)S(1)}, bf16[64,32,128]{2,1,0:T(8,128)(2,1)S(1)}, u32[]{:S(2)}, u32[]{:S(2)}) collective-permute-start(bf16[64,32,128]{2,1,0:T(8,128)(2,1)S(1)} %pad_maximum_fusion), channel_id=1, source_target_pairs={{0,24},{8,0},{16,8},{24,16},{1,25},{9,1},{17,9},{25,17},{2,26},{10... | collective-permute-start | bytes 1572872 | tf_op jit(solution)/shard_map/ppermute | solution.py:149
  43.8 16.7 %copy-start.3 = (s32[1,1,256]{2,1,0:T(1,128)S(1)}, s32[1,1,256]{2,1,0:T(1,128)}, u32[]{:S(2)}) copy-start(s32[1,1,256]{2,1,0:T(1,128)} %param.8) | copy-start | bytes 3076
  43.9 16.7 %copy-start.4 = (s32[1,1,256]{2,1,0:T(1,128)S(1)}, s32[1,1,256]{2,1,0:T(1,128)}, u32[]{:S(2)}) copy-start(s32[1,1,256]{2,1,0:T(1,128)} %param.9) | copy-start | bytes 3076
  44.0 16.6 %collective-permute-start.7 = (bf16[192,32,128]{2,1,0:T(8,128)(2,1)S(1)}, bf16[192,32,128]{2,1,0:T(8,128)(2,1)S(1)}, u32[]{:S(2)}, u32[]{:S(2)}) collective-permute-start(bf16[192,32,128]{2,1,0:T(8,128)(2,1)S(1)} %constant_dynamic-update-slice_fusion.refs_0_), channel_id=1, source_target_pairs={{0,1},{1,0},{2,3},{3,2},{4,5},{5,4},{6,7},{7,6},{8,9},{9,8},{10,11... | collective-permute-start | bytes 4718600 | tf_op jit(solution)/shard_map/ppermute | solution.py:149
  45.7 9.2 %collective-permute-start.5 = (bf16[32,32,128]{2,1,0:T(8,128)(2,1)S(1)}, bf16[32,32,128]{2,1,0:T(8,128)(2,1)S(1)}, u32[]{:S(2)}, u32[]{:S(2)}) collective-permute-start(bf16[32,32,128]{2,1,0:T(8,128)(2,1)S(1)} %slice.32), channel_id=1, source_target_pairs={{0,8},{8,16},{16,24},{24,0},{1,9},{9,17},{17,25},{25,1},{2,10},{10... | collective-permute-start | bytes 786440 | tf_op jit(solution)/shard_map/ppermute | solution.py:149
  46.9 9.2 %collective-permute-start.6 = (bf16[32,32,128]{2,1,0:T(8,128)(2,1)S(1)}, bf16[32,32,128]{2,1,0:T(8,128)(2,1)S(1)}, u32[]{:S(2)}, u32[]{:S(2)}) collective-permute-start(bf16[32,32,128]{2,1,0:T(8,128)(2,1)S(1)} %slice.33), channel_id=1, source_target_pairs={{0,24},{8,0},{16,8},{24,16},{1,25},{9,1},{17,9},{25,17},{2,26},{10... | collective-permute-start | bytes 786440 | tf_op jit(solution)/shard_map/ppermute | solution.py:149
  56.8 3.7 %collective-permute-start.8 = (bf16[64,32,128]{2,1,0:T(8,128)(2,1)}, bf16[64,32,128]{2,1,0:T(8,128)(2,1)}, u32[]{:S(2)}, u32[]{:S(2)}) collective-permute-start(bf16[64,32,128]{2,1,0:T(8,128)(2,1)} %constant_dynamic-update-slice_fusion.6.refs_1_), channel_id=1, source_target_pairs={{0,1},{1,0},{2,3},{3,2},{4,5},{5,4},{6,7},{7,6},{8,9},{9,8},{10,11... | collective-permute-start | bytes 1572872 | tf_op jit(solution)/shard_map/ppermute | solution.py:149
  69.8 1.0 copy-start
  70.9 24.4 %all-to-all-start = ((bf16[128,32,128]{2,1,0:T(8,128)(2,1)}), bf16[128,32,128]{2,1,0:T(8,128)(2,1)S(1)}, u32[]{:S(2)}, u32[]{:S(2)}) async-start(bf16[128,32,128]{2,1,0:T(8,128)(2,1)} %copy-done), calls=%async_computation | async-start | bytes 2097152 | tf_op jit(solution)/shard_map/all_to_all | solution.py:171
  80.1 97.0 %all-gather.6.cloned.1.call-start = ((), (), s32[]{:S(2)}) async-start(), calls=%async_computation.7 | async-start | bytes 4325376 | tf_op jit(solution)/shard_map/all_gather | solution.py:217
  86.4 26.9 %copy-start.5 = (f32[16,64,128]{2,1,0:T(8,128)S(1)}, f32[16,64,128]{2,1,0:T(8,128)}, u32[]{:S(2)}) copy-start(f32[16,64,128]{2,1,0:T(8,128)} %param.6) | copy-start | bytes 1572868
  115.2 7.7 %collective-permute-start.9 = (bf16[16,32,128]{2,1,0:T(8,128)(2,1)S(1)}, bf16[16,32,128]{2,1,0:T(8,128)(2,1)S(1)}, u32[]{:S(2)}, u32[]{:S(2)}) collective-permute-start(bf16[16,32,128]{2,1,0:T(8,128)(2,1)S(1)} %get-tuple-element.32), channel_id=1, source_target_pairs={{0,2},{2,4},{4,6},{6,0},{1,3},{3,5},{5,7},{7,1},{8,10},{10,12},{12... | collective-permute-start | bytes 393224 | tf_op jit(solution)/shard_map/ppermute | solution.py:149
  115.2 8.9 %collective-permute-start.10 = (bf16[16,32,128]{2,1,0:T(8,128)(2,1)S(1)}, bf16[16,32,128]{2,1,0:T(8,128)(2,1)S(1)}, u32[]{:S(2)}, u32[]{:S(2)}) collective-permute-start(bf16[16,32,128]{2,1,0:T(8,128)(2,1)S(1)} %get-tuple-element.32), channel_id=1, source_target_pairs={{0,6},{2,0},{4,2},{6,4},{1,7},{3,1},{5,3},{7,5},{8,14},{10,8},{12,... | collective-permute-start | bytes 393224 | tf_op jit(solution)/shard_map/ppermute | solution.py:149
  118.8 9.8 %collective-permute-start.11 = (bf16[16,32,128]{2,1,0:T(8,128)(2,1)S(1)}, bf16[16,32,128]{2,1,0:T(8,128)(2,1)S(1)}, u32[]{:S(2)}, u32[]{:S(2)}) collective-permute-start(bf16[16,32,128]{2,1,0:T(8,128)(2,1)S(1)} %get-tuple-element.32), channel_id=1, source_target_pairs={{0,4},{2,6},{4,0},{6,2},{1,5},{3,7},{5,1},{7,3},{8,12},{10,14},{12... | collective-permute-start | bytes 393224 | tf_op jit(solution)/shard_map/ppermute | solution.py:149
  128.7 14.7 %collective-permute-start.12 = (bf16[64,32,128]{2,1,0:T(8,128)(2,1)S(1)}, bf16[64,32,128]{2,1,0:T(8,128)(2,1)S(1)}, u32[]{:S(2)}, u32[]{:S(2)}) collective-permute-start(bf16[64,32,128]{2,1,0:T(8,128)(2,1)S(1)} %get-tuple-element.71), channel_id=1, source_target_pairs={{0,8},{8,16},{16,24},{24,0},{1,9},{9,17},{17,25},{25,1},{2,10},{10... | collective-permute-start | bytes 1572872 | tf_op jit(solution)/shard_map/ppermute | solution.py:149
  130.1 13.4 %collective-permute-start.13 = (bf16[64,32,128]{2,1,0:T(8,128)(2,1)S(1)}, bf16[64,32,128]{2,1,0:T(8,128)(2,1)S(1)}, u32[]{:S(2)}, u32[]{:S(2)}) collective-permute-start(bf16[64,32,128]{2,1,0:T(8,128)(2,1)S(1)} %get-tuple-element.71), channel_id=1, source_target_pairs={{0,24},{8,0},{16,8},{24,16},{1,25},{9,1},{17,9},{25,17},{2,26},{10... | collective-permute-start | bytes 1572872 | tf_op jit(solution)/shard_map/ppermute | solution.py:149
  143.6 18.4 %collective-permute-start.16 = (bf16[192,32,128]{2,1,0:T(8,128)(2,1)S(1)}, bf16[192,32,128]{2,1,0:T(8,128)(2,1)S(1)}, u32[]{:S(2)}, u32[]{:S(2)}) collective-permute-start(bf16[192,32,128]{2,1,0:T(8,128)(2,1)S(1)} %constant_dynamic-update-slice_fusion.12.refs_0_), channel_id=1, source_target_pairs={{0,1},{1,0},{2,3},{3,2},{4,5},{5,4},{6,7},{7,6},{8,9},{9,8},{10,11... | collective-permute-start | bytes 4718600 | tf_op jit(solution)/shard_map/ppermute | solution.py:149
  147.1 12.1 %collective-permute-start.14 = (bf16[32,32,128]{2,1,0:T(8,128)(2,1)S(1)}, bf16[32,32,128]{2,1,0:T(8,128)(2,1)S(1)}, u32[]{:S(2)}, u32[]{:S(2)}) collective-permute-start(bf16[32,32,128]{2,1,0:T(8,128)(2,1)S(1)} %slice.34), channel_id=1, source_target_pairs={{0,8},{8,16},{16,24},{24,0},{1,9},{9,17},{17,25},{25,1},{2,10},{10... | collective-permute-start | bytes 786440 | tf_op jit(solution)/shard_map/ppermute | solution.py:149
  147.8 11.4 %collective-permute-start.15 = (bf16[32,32,128]{2,1,0:T(8,128)(2,1)S(1)}, bf16[32,32,128]{2,1,0:T(8,128)(2,1)S(1)}, u32[]{:S(2)}, u32[]{:S(2)}) collective-permute-start(bf16[32,32,128]{2,1,0:T(8,128)(2,1)S(1)} %slice.35), channel_id=1, source_target_pairs={{0,24},{8,0},{16,8},{24,16},{1,25},{9,1},{17,9},{25,17},{2,26},{10... | collective-permute-start | bytes 786440 | tf_op jit(solution)/shard_map/ppermute | solution.py:149
  159.3 2.7 collective-permute-start.17
  170.1 1.0 copy-start.1
  171.1 21.1 %all-to-all-start.2 = ((bf16[128,32,128]{2,1,0:T(8,128)(2,1)}), bf16[128,32,128]{2,1,0:T(8,128)(2,1)S(1)}, u32[]{:S(2)}, u32[]{:S(2)}) async-start(bf16[128,32,128]{2,1,0:T(8,128)(2,1)} %copy-done.1), calls=%async_computation.2 | async-start | bytes 2097152 | tf_op jit(solution)/shard_map/all_to_all | solution.py:171
  177.0 99.0 %all-gather.8.cloned.1.call-start = ((), (), s32[]{:S(2)}) async-start(), calls=%async_computation.8 | async-start | bytes 4325376 | tf_op jit(solution)/shard_map/all_gather | solution.py:217
  183.3 27.1 %copy-start.7 = (f32[16,32,128]{2,1,0:T(8,128)S(1)}, f32[16,32,128]{2,1,0:T(8,128)}, u32[]{:S(2)}) copy-start(f32[16,32,128]{2,1,0:T(8,128)} %get-tuple-element.57) | copy-start | bytes 786436
  210.4 1.0 copy-start.9
  212.2 7.7 %collective-permute-start.18 = (bf16[16,32,128]{2,1,0:T(8,128)(2,1)S(1)}, bf16[16,32,128]{2,1,0:T(8,128)(2,1)S(1)}, u32[]{:S(2)}, u32[]{:S(2)}) collective-permute-start(bf16[16,32,128]{2,1,0:T(8,128)(2,1)S(1)} %get-tuple-element.40), channel_id=1, source_target_pairs={{0,2},{2,4},{4,6},{6,0},{1,3},{3,5},{5,7},{7,1},{8,10},{10,12},{12... | collective-permute-start | bytes 393224 | tf_op jit(solution)/shard_map/ppermute | solution.py:149
  212.2 9.5 %collective-permute-start.19 = (bf16[16,32,128]{2,1,0:T(8,128)(2,1)S(1)}, bf16[16,32,128]{2,1,0:T(8,128)(2,1)S(1)}, u32[]{:S(2)}, u32[]{:S(2)}) collective-permute-start(bf16[16,32,128]{2,1,0:T(8,128)(2,1)S(1)} %get-tuple-element.40), channel_id=1, source_target_pairs={{0,6},{2,0},{4,2},{6,4},{1,7},{3,1},{5,3},{7,5},{8,14},{10,8},{12,... | collective-permute-start | bytes 393224 | tf_op jit(solution)/shard_map/ppermute | solution.py:149
  215.8 8.5 %collective-permute-start.20 = (bf16[16,32,128]{2,1,0:T(8,128)(2,1)S(1)}, bf16[16,32,128]{2,1,0:T(8,128)(2,1)S(1)}, u32[]{:S(2)}, u32[]{:S(2)}) collective-permute-start(bf16[16,32,128]{2,1,0:T(8,128)(2,1)S(1)} %get-tuple-element.40), channel_id=1, source_target_pairs={{0,4},{2,6},{4,0},{6,2},{1,5},{3,7},{5,1},{7,3},{8,12},{10,14},{12... | collective-permute-start | bytes 393224 | tf_op jit(solution)/shard_map/ppermute | solution.py:149
  224.4 12.7 %collective-permute-start.21 = (bf16[64,32,128]{2,1,0:T(8,128)(2,1)S(1)}, bf16[64,32,128]{2,1,0:T(8,128)(2,1)S(1)}, u32[]{:S(2)}, u32[]{:S(2)}) collective-permute-start(bf16[64,32,128]{2,1,0:T(8,128)(2,1)S(1)} %get-tuple-element.63), channel_id=1, source_target_pairs={{0,8},{8,16},{16,24},{24,0},{1,9},{9,17},{17,25},{25,1},{2,10},{10... | collective-permute-start | bytes 1572872 | tf_op jit(solution)/shard_map/ppermute | solution.py:149
  226.3 11.3 %collective-permute-start.22 = (bf16[64,32,128]{2,1,0:T(8,128)(2,1)S(1)}, bf16[64,32,128]{2,1,0:T(8,128)(2,1)S(1)}, u32[]{:S(2)}, u32[]{:S(2)}) collective-permute-start(bf16[64,32,128]{2,1,0:T(8,128)(2,1)S(1)} %get-tuple-element.63), channel_id=1, source_target_pairs={{0,24},{8,0},{16,8},{24,16},{1,25},{9,1},{17,9},{25,17},{2,26},{10... | collective-permute-start | bytes 1572872 | tf_op jit(solution)/shard_map/ppermute | solution.py:149
  237.7 18.8 %collective-permute-start.25 = (bf16[192,32,128]{2,1,0:T(8,128)(2,1)S(1)}, bf16[192,32,128]{2,1,0:T(8,128)(2,1)S(1)}, u32[]{:S(2)}, u32[]{:S(2)}) collective-permute-start(bf16[192,32,128]{2,1,0:T(8,128)(2,1)S(1)} %constant_dynamic-update-slice_fusion.24.refs_0_), channel_id=1, source_target_pairs={{0,1},{1,0},{2,3},{3,2},{4,5},{5,4},{6,7},{7,6},{8,9},{9,8},{10,11... | collective-permute-start | bytes 4718600 | tf_op jit(solution)/shard_map/ppermute | solution.py:149
  242.3 9.6 %collective-permute-start.23 = (bf16[32,32,128]{2,1,0:T(8,128)(2,1)S(1)}, bf16[32,32,128]{2,1,0:T(8,128)(2,1)S(1)}, u32[]{:S(2)}, u32[]{:S(2)}) collective-permute-start(bf16[32,32,128]{2,1,0:T(8,128)(2,1)S(1)} %slice.36), channel_id=1, source_target_pairs={{0,8},{8,16},{16,24},{24,0},{1,9},{9,17},{17,25},{25,1},{2,10},{10... | collective-permute-start | bytes 786440 | tf_op jit(solution)/shard_map/ppermute | solution.py:149
  243.7 9.6 %collective-permute-start.24 = (bf16[32,32,128]{2,1,0:T(8,128)(2,1)S(1)}, bf16[32,32,128]{2,1,0:T(8,128)(2,1)S(1)}, u32[]{:S(2)}, u32[]{:S(2)}) collective-permute-start(bf16[32,32,128]{2,1,0:T(8,128)(2,1)S(1)} %slice.37), channel_id=1, source_target_pairs={{0,24},{8,0},{16,8},{24,16},{1,25},{9,1},{17,9},{25,17},{2,26},{10... | collective-permute-start | bytes 786440 | tf_op jit(solution)/shard_map/ppermute | solution.py:149
  253.3 3.2 collective-permute-start.26
  264.5 1.0 copy-start.2
  265.6 25.7 %all-to-all-start.4 = ((bf16[128,32,128]{2,1,0:T(8,128)(2,1)}), bf16[128,32,128]{2,1,0:T(8,128)(2,1)S(1)}, u32[]{:S(2)}, u32[]{:S(2)}) async-start(bf16[128,32,128]{2,1,0:T(8,128)(2,1)} %copy-done.2), calls=%async_computation.4 | async-start | bytes 2097152 | tf_op jit(solution)/shard_map/all_to_all | solution.py:171
  283.3 12.4 %copy-start.12 = (s32[16,128]{1,0:T(8,128)S(1)}, s32[16,128]{1,0:T(8,128)}, u32[]{:S(2)}) copy-start(s32[16,128]{1,0:T(8,128)} %param.10) | copy-start | bytes 24580
  283.3 12.4 %copy-start.6 = (f32[16,64,128]{2,1,0:T(8,128)S(1)}, f32[16,64,128]{2,1,0:T(8,128)}, u32[]{:S(2)}) copy-start(f32[16,64,128]{2,1,0:T(8,128)} %param.6) | copy-start | bytes 1572868
  291.2 17.5 %all-to-all-start.5 = ((bf16[128,32,128]{2,1,0:T(8,128)(2,1)}), bf16[128,32,128]{2,1,0:T(8,128)(2,1)S(1)}, u32[]{:S(2)}, u32[]{:S(2)}) async-start(bf16[128,32,128]{2,1,0:T(8,128)(2,1)} %get-tuple-element.46), calls=%async_computation.5 | async-start | bytes 2097152 | tf_op jit(solution)/shard_map/all_to_all | solution.py:171
  294.8 13.9 %copy-start.8 = (f32[16,32,128]{2,1,0:T(8,128)S(1)}, f32[16,32,128]{2,1,0:T(8,128)}, u32[]{:S(2)}) copy-start(f32[16,32,128]{2,1,0:T(8,128)} %get-tuple-element.57) | copy-start | bytes 786436
  297.8 12.1 %copy-start.10 = (f32[16,32,128]{2,1,0:T(8,128)S(1)}, f32[16,32,128]{2,1,0:T(8,128)}, u32[]{:S(2)}) copy-start(f32[16,32,128]{2,1,0:T(8,128)} %get-tuple-element.50) | copy-start | bytes 786436
  297.8 12.1 %copy-start.11 = (f32[16,32,128]{2,1,0:T(8,128)S(1)}, f32[16,32,128]{2,1,0:T(8,128)}, u32[]{:S(2)}) copy-start(f32[16,32,128]{2,1,0:T(8,128)} %get-tuple-element.51) | copy-start | bytes 786436
Sparse Core Ops, SparseCore 0:
  11.1 64.6 all-gather.3
  114.4 59.8 all-gather.5
  211.5 61.2 all-gather.7

commit v8 on v6

--- a/solution.py
+++ b/solution.py
@@ -13,6 +13,7 @@
 GROUPS = 8
 AHEAD = 3
 TURNS = (0, 1, 3, 2)
+Z_TURNS = (0, 2, 1, 3)
 
 
 def poisson_weights(horizon):
@@ -154,7 +155,7 @@
 
 
 def spread_z(mine):
-    return [mine] + [turn(mine, "zh", by) for by in TURNS[1:]]
+    return [mine] + [turn(mine, "zh", by) for by in Z_TURNS[1:]]
 
 
 def spread_x(column):
@@ -183,7 +184,7 @@
     src = blk_src[0, 0]
     dst = blk_dst[0, 0]
     span = x_init.shape[0]
-    half = x_init.shape[1] // 2
+    half = x_init.shape[1] * 40 // 64
     weights = poisson_weights(horizon)
     reward_f = reward.astype(jnp.float32)[:, None, :]
     x, zh, core = (lax.axis_index(a) for a in COL)
@@ -191,7 +192,7 @@
     place = [row]
     for other in range(2):
         for by_x in TURNS:
-            for by_z in TURNS:
+            for by_z in Z_TURNS:
                 place.append((((x - by_x) % 4) * 4 + (zh - by_z) % 4) * 2 + (core + other) % 2)
     place = jnp.stack(place).astype(jnp.int32)
     state_a, state_b = x_init[:, :half], x_init[:, half:]

time: 317 us -> 314 us (level)
  starting transfers between devices: 92.3 us -> 64 us
  waiting for transfers between devices: 112 us -> 129 us
  blocking collectives: 36.1 us -> 43.3 us
  local copies, waits for them, and re-layouts: 3.1 us -> 8.71 us
  Pallas kernels: 48.5 us -> 44.9 us
    all_to_all x4, waiting for transfers between devices: 36.7 us -> 15.3 us  [exchange_rows(): return lax.all_to_all(send, ROW, 0, 0, tiled=True)]
    all_gather x1, waiting for transfers between devices: 0.02 us -> 17.4 us  [shards(): lax.all_gather(state_a.astype(jnp.bfloat16), COL, axis=0, tiled=True)]
    all_to_all x4, starting transfers between devices: 30.5 us -> 14.6 us  [exchange_rows(): return lax.all_to_all(send, ROW, 0, 0, tiled=True)]
    all_gather x2, waiting for transfers between devices: 0.03 us -> 15.8 us  [shards(): whole = lax.all_gather(low_a, COL, axis=0, tiled=True)]
    ppermute x24, starting transfers between devices: 61.6 us -> 49.3 us  [turn(): return lax.ppermute(value, axis, [(i, (i + by) % n) for i in range(n)])]
    all_to_all x2, blocking collectives: 36.1 us -> 43.3 us  [exchange_rows(): return lax.all_to_all(send, ROW, 0, 0, tiled=True)]
    ppermute x24, waiting for transfers between devices: 75.5 us -> 80.3 us  [turn(): return lax.ppermute(value, axis, [(i, (i + by) % n) for i in range(n)])]
    unnamed x39 -> x51, local copies, waits for them, and re-layouts: 2.66 us -> 6.62 us
  transfers between devices with their start and end apart: 31 -> 31, of which waited for: 21 -> 22; matrix products, arithmetic and copies ran while one was open for 1% -> 2% of each run, Pallas kernels for 15% -> 14%
where the time goes in v8:
time: 314 us; the launch traced here: 313 us
  waiting for transfers between devices  129 us (41%)
  starting transfers between devices  64 us (20%)
  Pallas kernels  44.9 us (14%)
  blocking collectives  43.3 us (14%)
  between operations  15.1 us (5%)
  local copies, waits for them, and re-layouts  8.71 us (3%)
  other arithmetic  8.29 us (3%)
    ppermute x24, waiting for transfers between devices, turn(): return lax.ppermute(value, axis, [(i, (i + by) % n) for i in range(n)])  80.3 us
    ppermute x24, starting transfers between devices, turn(): return lax.ppermute(value, axis, [(i, (i + by) % n) for i in range(n)])  49.3 us
    pallas_call x6, Pallas kernels, products(): pl.pallas_call(body, out_shape=[jax.ShapeDtypeStruct(piece, jnp.float32),...  44.9 us
    all_to_all x2, blocking collectives, exchange_rows(): return lax.all_to_all(send, ROW, 0, 0, tiled=True)  43.3 us
    all_gather x1, waiting for transfers between devices, shards(): lax.all_gather(state_a.astype(jnp.bfloat16), COL, axis=0, tiled=True)  17.4 us
    all_gather x2, waiting for transfers between devices, shards(): whole = lax.all_gather(low_a, COL, axis=0, tiled=True)  15.8 us
    all_to_all x4, waiting for transfers between devices, exchange_rows(): return lax.all_to_all(send, ROW, 0, 0, tiled=True)  15.3 us
    all_to_all x4, starting transfers between devices, exchange_rows(): return lax.all_to_all(send, ROW, 0, 0, tiled=True)  14.6 us
  transfers between devices with their start and end apart: 31, of which 22 were waited for; matrix products, arithmetic and copies ran while one was open for 2% of the time, Pallas kernels for 14%

profile of v8, /device:TPU:1, one launch (start us, length us, event | category | flops | bytes accessed | tf_op | source)
XLA Modules:
  0.0 313.1 jit_solution(16489361017106376256)
XLA Ops:
  7.2 1.7 slice.44
  9.9 7.8 %collective-permute-start = (bf16[16,24,128]{2,1,0:T(8,128)(2,1)S(1)}, bf16[16,24,128]{2,1,0:T(8,128)(2,1)S(1)}, u32[]{:S(2)}, u32[]{:S(2)}) collective-permute-start(bf16[16,24,128]{2,1,0:T(8,128)(2,1)S(1)} %get-tuple-element.61), channel_id=1, source_target_pairs={{0,4},{2,6},{4,0},{6,2},{1,5},{3,7},{5,1},{7,3},{8,12},{10,14},{12... | collective-permute-start | bytes 294920 | tf_op jit(solution)/shard_map/ppermute | solution.py:150
  18.9 2.4 collective-permute-start.2
  21.3 3.1 collective-permute-done.1
  24.3 3.4 %collective-permute-done.2 = bf16[16,24,128]{2,1,0:T(8,128)(2,1)S(1)} collective-permute-done((bf16[16,24,128]{2,1,0:T(8,128)(2,1)S(1)}, bf16[16,24,128]{2,1,0:T(8,128)(2,1)S(1)}, u32[]{:S(2)}, u32[]{:S(2)}) %collective-permute-start.2) | collective-permute-done | bytes 98336 | tf_op jit(solution)/shard_map/ppermute | solution.py:150
  30.6 11.1 %collective-permute-done.3 = bf16[64,24,128]{2,1,0:T(8,128)(2,1)S(1)} collective-permute-done((bf16[64,24,128]{2,1,0:T(8,128)(2,1)S(1)}, bf16[64,24,128]{2,1,0:T(8,128)(2,1)S(1)}, u32[]{:S(2)}, u32[]{:S(2)}) %collective-permute-start.3) | collective-permute-done | bytes 393248 | tf_op jit(solution)/shard_map/ppermute | solution.py:150
  41.9 2.7 collective-permute-start.6
  44.8 3.9 %collective-permute-done.5 = bf16[32,24,128]{2,1,0:T(8,128)(2,1)S(1)} collective-permute-done((bf16[32,24,128]{2,1,0:T(8,128)(2,1)S(1)}, bf16[32,24,128]{2,1,0:T(8,128)(2,1)S(1)}, u32[]{:S(2)}, u32[]{:S(2)}) %collective-permute-start.5) | collective-permute-done | bytes 196640 | tf_op jit(solution)/shard_map/ppermute | solution.py:150
  48.8 1.8 collective-permute-start.7
  50.7 2.9 collective-permute-done.7.refs_1_
  53.6 8.1 %products.6 = (f32[16,24,128]{2,1,0:T(8,128)S(1)}, bf16[128,24,128]{2,1,0:T(8,128)(2,1)S(1)}) custom-call(s32[256]{0:T(256)S(1)} %bitcast.45, s32[256]{0:T(256)S(1)} %bitcast.51, s32[33]{0:T(128)S(1)} %stack.135.place, bf16[256,24,128]{2,1,0:T(8,128)(2,1)S(1)} %constant_dynamic-update-slice_fusion.refs_0_, ...), custom_call_target="tpu_custom_call" | custom-call | flops 201326592 | bytes 11534336 | tf_op jit(solution)/shard_map/products/pallas_call | solution.py:128
  62.6 3.7 %all-to-all-start = ((bf16[128,24,128]{2,1,0:T(8,128)(2,1)}), bf16[128,24,128]{2,1,0:T(8,128)(2,1)S(1)}, u32[]{:S(2)}, u32[]{:S(2)}) async-start(bf16[128,24,128]{2,1,0:T(8,128)(2,1)} %copy-done), calls=%async_computation | async-start | bytes 1572864 | tf_op jit(solution)/shard_map/all_to_all | solution.py:172
  66.4 17.4 %all-gather.4.cloned.1.call-done.given = bf16[512,40,128]{2,1,0:T(8,128)(2,1)} async-done(((bf16[16,40,128]{2,1,0:T(8,128)(2,1)}), bf16[512,40,128]{2,1,0:T(8,128)(2,1)}) %all-gather.4.cloned.1.call-update) | async-done | bytes 5242896 | tf_op jit(solution)/shard_map/all_gather | solution.py:201
  83.8 6.6 %products.7 = (f32[16,40,128]{2,1,0:T(8,128)S(1)}, bf16[128,40,128]{2,1,0:T(8,128)(2,1)S(1)}) custom-call(s32[256]{0:T(256)S(1)} %bitcast.46, s32[256]{0:T(256)S(1)} %bitcast.52, s32[33]{0:T(128)S(1)} %stack.135.place, bf16[512,40,128]{2,1,0:T(8,128)(2,1)} %all-gather.4.cloned.1.call-done.given, bf16[256,128,128]{2,1,0:T(8,128)(2,1)} %bitcast.58), custom_call_target="tpu_custom_call" | custom-call | flops 335544320 | bytes 13631488 | tf_op jit(solution)/shard_map/products/pallas_call | solution.py:128
  91.3 22.0 %all_to_all.30 = bf16[128,40,128]{2,1,0:T(8,128)(2,1)S(1)} all-to-all(bf16[128,40,128]{2,1,0:T(8,128)(2,1)S(1)} %get-tuple-element.30), channel_id=1, replica_groups=mesh['y'=4,'zl'=2,'x'=4,'zh'=4,'core'=2] {'y','zl'}, dimensions={0} | all-to-all | bytes 2621440 | tf_op jit(solution)/shard_map/all_to_all | solution.py:172
  115.5 1.7 collective-permute-start.8
  117.2 2.6 collective-permute-start.9
  120.8 2.4 collective-permute-done.8
  123.3 5.1 %collective-permute-done.9 = bf16[16,24,128]{2,1,0:T(8,128)(2,1)S(1)} collective-permute-done((bf16[16,24,128]{2,1,0:T(8,128)(2,1)S(1)}, bf16[16,24,128]{2,1,0:T(8,128)(2,1)S(1)}, u32[]{:S(2)}, u32[]{:S(2)}) %collective-permute-start.9) | collective-permute-done | bytes 98336 | tf_op jit(solution)/shard_map/ppermute | solution.py:150
  128.4 2.7 collective-permute-done.10
  131.2 1.7 collective-permute-start.11
  133.9 10.6 %collective-permute-done.11 = bf16[64,24,128]{2,1,0:T(8,128)(2,1)S(1)} collective-permute-done((bf16[64,24,128]{2,1,0:T(8,128)(2,1)S(1)}, bf16[64,24,128]{2,1,0:T(8,128)(2,1)S(1)}, u32[]{:S(2)}, u32[]{:S(2)}) %collective-permute-start.11) | collective-permute-done | bytes 393248 | tf_op jit(solution)/shard_map/ppermute | solution.py:150
  145.0 2.4 collective-permute-start.14
  147.6 3.9 %collective-permute-done.13 = bf16[32,24,128]{2,1,0:T(8,128)(2,1)S(1)} collective-permute-done((bf16[32,24,128]{2,1,0:T(8,128)(2,1)S(1)}, bf16[32,24,128]{2,1,0:T(8,128)(2,1)S(1)}, u32[]{:S(2)}, u32[]{:S(2)}) %collective-permute-start.13) | collective-permute-done | bytes 196640 | tf_op jit(solution)/shard_map/ppermute | solution.py:150
  151.6 4.6 %collective-permute-start.15 = (bf16[256,24,128]{2,1,0:T(8,128)(2,1)S(1)}, bf16[256,24,128]{2,1,0:T(8,128)(2,1)S(1)}, u32[]{:S(2)}, u32[]{:S(2)}) collective-permute-start(bf16[256,24,128]{2,1,0:T(8,128)(2,1)S(1)} %constant_dynamic-update-slice_fusion.12.refs_0_), channel_id=1, source_target_pairs={{0,1},{1,0},{2,3},{3,2},{4,5},{5,4},{6,7},{7,6},{8,9},{9,8},{10,11... | collective-permute-start | bytes 4718600 | tf_op jit(solution)/shard_map/ppermute | solution.py:150
  156.2 3.0 collective-permute-done.15.refs_1_
  159.2 8.1 %products.8 = (f32[16,24,128]{2,1,0:T(8,128)S(1)}, bf16[128,24,128]{2,1,0:T(8,128)(2,1)S(1)}) custom-call(s32[256]{0:T(256)S(1)} %bitcast.47, s32[256]{0:T(256)S(1)} %bitcast.53, s32[33]{0:T(128)S(1)} %stack.135.place, bf16[256,24,128]{2,1,0:T(8,128)(2,1)S(1)} %constant_dynamic-update-slice_fusion.12.refs_0_, ...), custom_call_target="tpu_custom_call" | custom-call | flops 201326592 | bytes 11534336 | tf_op jit(solution)/shard_map/products/pallas_call | solution.py:128
  168.2 3.5 %all-to-all-start.2 = ((bf16[128,24,128]{2,1,0:T(8,128)(2,1)}), bf16[128,24,128]{2,1,0:T(8,128)(2,1)S(1)}, u32[]{:S(2)}, u32[]{:S(2)}) async-start(bf16[128,24,128]{2,1,0:T(8,128)(2,1)} %copy-done.1), calls=%async_computation.2 | async-start | bytes 1572864 | tf_op jit(solution)/shard_map/all_to_all | solution.py:172
  171.8 7.9 %all-gather.6.cloned.1.call-done.given = bf16[512,40,128]{2,1,0:T(8,128)(2,1)} async-done(((bf16[16,40,128]{2,1,0:T(8,128)(2,1)}), bf16[512,40,128]{2,1,0:T(8,128)(2,1)}) %all-gather.6.cloned.1.call-update) | async-done | bytes 5242896 | tf_op jit(solution)/shard_map/all_gather | solution.py:217
  179.7 6.6 %products.9 = (f32[16,40,128]{2,1,0:T(8,128)S(1)}, bf16[128,40,128]{2,1,0:T(8,128)(2,1)S(1)}) custom-call(s32[256]{0:T(256)S(1)} %bitcast.48, s32[256]{0:T(256)S(1)} %bitcast.54, s32[33]{0:T(128)S(1)} %stack.135.place, bf16[512,40,128]{2,1,0:T(8,128)(2,1)} %all-gather.6.cloned.1.call-done.given, bf16[256,128,128]{2,1,0:T(8,128)(2,1)} %bitcast.60), custom_call_target="tpu_custom_call" | custom-call | flops 335544320 | bytes 13631488 | tf_op jit(solution)/shard_map/products/pallas_call | solution.py:128
  187.2 21.3 %all_to_all.31 = bf16[128,40,128]{2,1,0:T(8,128)(2,1)S(1)} all-to-all(bf16[128,40,128]{2,1,0:T(8,128)(2,1)S(1)} %get-tuple-element.38), channel_id=1, replica_groups=mesh['y'=4,'zl'=2,'x'=4,'zh'=4,'core'=2] {'y','zl'}, dimensions={0} | all-to-all | bytes 2621440 | tf_op jit(solution)/shard_map/all_to_all | solution.py:172
  211.9 3.0 collective-permute-start.17
  215.5 2.5 collective-permute-done.16
  218.1 4.7 %collective-permute-done.17 = bf16[16,24,128]{2,1,0:T(8,128)(2,1)S(1)} collective-permute-done((bf16[16,24,128]{2,1,0:T(8,128)(2,1)S(1)}, bf16[16,24,128]{2,1,0:T(8,128)(2,1)S(1)}, u32[]{:S(2)}, u32[]{:S(2)}) %collective-permute-start.17) | collective-permute-done | bytes 98336 | tf_op jit(solution)/shard_map/ppermute | solution.py:150
  222.8 3.4 %collective-permute-done.18 = bf16[16,24,128]{2,1,0:T(8,128)(2,1)S(1)} collective-permute-done((bf16[16,24,128]{2,1,0:T(8,128)(2,1)S(1)}, bf16[16,24,128]{2,1,0:T(8,128)(2,1)S(1)}, u32[]{:S(2)}, u32[]{:S(2)}) %collective-permute-start.18) | collective-permute-done | bytes 98336 | tf_op jit(solution)/shard_map/ppermute | solution.py:150
  226.2 2.7 collective-permute-start.19
  229.0 10.4 %collective-permute-done.19 = bf16[64,24,128]{2,1,0:T(8,128)(2,1)S(1)} collective-permute-done((bf16[64,24,128]{2,1,0:T(8,128)(2,1)S(1)}, bf16[64,24,128]{2,1,0:T(8,128)(2,1)S(1)}, u32[]{:S(2)}, u32[]{:S(2)}) %collective-permute-start.19) | collective-permute-done | bytes 393248 | tf_op jit(solution)/shard_map/ppermute | solution.py:150
  240.1 2.1 collective-permute-start.22
  242.4 3.8 %collective-permute-done.21 = bf16[32,24,128]{2,1,0:T(8,128)(2,1)S(1)} collective-permute-done((bf16[32,24,128]{2,1,0:T(8,128)(2,1)S(1)}, bf16[32,24,128]{2,1,0:T(8,128)(2,1)S(1)}, u32[]{:S(2)}, u32[]{:S(2)}) %collective-permute-start.21) | collective-permute-done | bytes 196640 | tf_op jit(solution)/shard_map/ppermute | solution.py:150
  246.3 4.7 %collective-permute-start.23 = (bf16[256,24,128]{2,1,0:T(8,128)(2,1)S(1)}, bf16[256,24,128]{2,1,0:T(8,128)(2,1)S(1)}, u32[]{:S(2)}, u32[]{:S(2)}) collective-permute-start(bf16[256,24,128]{2,1,0:T(8,128)(2,1)S(1)} %constant_dynamic-update-slice_fusion.24.refs_0_), channel_id=1, source_target_pairs={{0,1},{1,0},{2,3},{3,2},{4,5},{5,4},{6,7},{7,6},{8,9},{9,8},{10,11... | collective-permute-start | bytes 4718600 | tf_op jit(solution)/shard_map/ppermute | solution.py:150
  251.0 3.0 collective-permute-done.23.refs_1_
  254.1 8.1 %products.10 = (f32[16,24,128]{2,1,0:T(8,128)S(1)}, bf16[128,24,128]{2,1,0:T(8,128)(2,1)S(1)}) custom-call(s32[256]{0:T(256)S(1)} %bitcast.49, s32[256]{0:T(256)S(1)} %bitcast.55, s32[33]{0:T(128)S(1)} %stack.135.place, bf16[256,24,128]{2,1,0:T(8,128)(2,1)S(1)} %constant_dynamic-update-slice_fusion.24.refs_0_, ...), custom_call_target="tpu_custom_call" | custom-call | flops 201326592 | bytes 11534336 | tf_op jit(solution)/shard_map/products/pallas_call | solution.py:128
  263.1 3.5 %all-to-all-start.4 = ((bf16[128,24,128]{2,1,0:T(8,128)(2,1)}), bf16[128,24,128]{2,1,0:T(8,128)(2,1)S(1)}, u32[]{:S(2)}, u32[]{:S(2)}) async-start(bf16[128,24,128]{2,1,0:T(8,128)(2,1)} %copy-done.2), calls=%async_computation.4 | async-start | bytes 1572864 | tf_op jit(solution)/shard_map/all_to_all | solution.py:172
  266.6 7.8 %all-gather.8.cloned.1.call-done.given = bf16[512,40,128]{2,1,0:T(8,128)(2,1)} async-done(((bf16[16,40,128]{2,1,0:T(8,128)(2,1)}), bf16[512,40,128]{2,1,0:T(8,128)(2,1)}) %all-gather.8.cloned.1.call-update) | async-done | bytes 5242896 | tf_op jit(solution)/shard_map/all_gather | solution.py:217
  274.5 7.6 %products.11 = (f32[16,40,128]{2,1,0:T(8,128)S(1)}, bf16[128,40,128]{2,1,0:T(8,128)(2,1)}) custom-call(s32[256]{0:T(256)S(1)} %bitcast.50, s32[256]{0:T(256)S(1)} %bitcast.56, s32[33]{0:T(128)S(1)} %stack.135.place, bf16[512,40,128]{2,1,0:T(8,128)(2,1)} %all-gather.8.cloned.1.call-done.given, bf16[256,128,128]{2,1,0:T(8,128)(2,1)} %bitcast.62), custom_call_target="tpu_custom_call" | custom-call | flops 335544320 | bytes 13631488 | tf_op jit(solution)/shard_map/products/pallas_call | solution.py:128
  282.1 3.8 %all-to-all-start.5 = ((bf16[128,40,128]{2,1,0:T(8,128)(2,1)}), bf16[128,40,128]{2,1,0:T(8,128)(2,1)S(1)}, u32[]{:S(2)}, u32[]{:S(2)}) async-start(bf16[128,40,128]{2,1,0:T(8,128)(2,1)} %get-tuple-element.46), calls=%async_computation.5 | async-start | bytes 2621440 | tf_op jit(solution)/shard_map/all_to_all | solution.py:172
  286.8 2.0 multiply_add_fusion.1
  288.8 15.3 %all-to-all-done.5 = bf16[128,40,128]{2,1,0:T(8,128)(2,1)S(1)} async-done(((bf16[128,40,128]{2,1,0:T(8,128)(2,1)}), bf16[128,40,128]{2,1,0:T(8,128)(2,1)S(1)}, u32[]{:S(2)}, u32[]{:S(2)}) %all-to-all-start.5) | async-done | bytes 1310752 | tf_op jit(solution)/shard_map/all_to_all | solution.py:172
  (98 shorter events, 22.9 us)
Async XLA Ops:
  7.2 76.6 %all-gather.4.cloned.1.call-start = ((), (), s32[]{:S(2)}) async-start(), calls=%async_computation.6 | async-start | bytes 5406720 | tf_op jit(solution)/shard_map/all_gather | solution.py:201
  9.9 11.4 %collective-permute-start = (bf16[16,24,128]{2,1,0:T(8,128)(2,1)S(1)}, bf16[16,24,128]{2,1,0:T(8,128)(2,1)S(1)}, u32[]{:S(2)}, u32[]{:S(2)}) collective-permute-start(bf16[16,24,128]{2,1,0:T(8,128)(2,1)S(1)} %get-tuple-element.61), channel_id=1, source_target_pairs={{0,4},{2,6},{4,0},{6,2},{1,5},{3,7},{5,1},{7,3},{8,12},{10,14},{12... | collective-permute-start | bytes 294920 | tf_op jit(solution)/shard_map/ppermute | solution.py:150
  17.7 6.6 %collective-permute-start.1 = (bf16[16,24,128]{2,1,0:T(8,128)(2,1)S(1)}, bf16[16,24,128]{2,1,0:T(8,128)(2,1)S(1)}, u32[]{:S(2)}, u32[]{:S(2)}) collective-permute-start(bf16[16,24,128]{2,1,0:T(8,128)(2,1)S(1)} %get-tuple-element.61), channel_id=1, source_target_pairs={{0,2},{2,4},{4,6},{6,0},{1,3},{3,5},{5,7},{7,1},{8,10},{10,12},{12... | collective-permute-start | bytes 294920 | tf_op jit(solution)/shard_map/ppermute | solution.py:150
  18.9 8.8 %collective-permute-start.2 = (bf16[16,24,128]{2,1,0:T(8,128)(2,1)S(1)}, bf16[16,24,128]{2,1,0:T(8,128)(2,1)S(1)}, u32[]{:S(2)}, u32[]{:S(2)}) collective-permute-start(bf16[16,24,128]{2,1,0:T(8,128)(2,1)S(1)} %get-tuple-element.61), channel_id=1, source_target_pairs={{0,6},{2,0},{4,2},{6,4},{1,7},{3,1},{5,3},{7,5},{8,14},{10,8},{12,... | collective-permute-start | bytes 294920 | tf_op jit(solution)/shard_map/ppermute | solution.py:150
  27.8 14.0 %collective-permute-start.3 = (bf16[64,24,128]{2,1,0:T(8,128)(2,1)S(1)}, bf16[64,24,128]{2,1,0:T(8,128)(2,1)S(1)}, u32[]{:S(2)}, u32[]{:S(2)}) collective-permute-start(bf16[64,24,128]{2,1,0:T(8,128)(2,1)S(1)} %pad_maximum_fusion.2), channel_id=1, source_target_pairs={{0,8},{8,16},{16,24},{24,0},{1,9},{9,17},{17,25},{25,1},{2,10},{10... | collective-permute-start | bytes 1179656 | tf_op jit(solution)/shard_map/ppermute | solution.py:150
  29.1 12.8 %collective-permute-start.4 = (bf16[64,24,128]{2,1,0:T(8,128)(2,1)S(1)}, bf16[64,24,128]{2,1,0:T(8,128)(2,1)S(1)}, u32[]{:S(2)}, u32[]{:S(2)}) collective-permute-start(bf16[64,24,128]{2,1,0:T(8,128)(2,1)S(1)} %pad_maximum_fusion.2), channel_id=1, source_target_pairs={{0,24},{8,0},{16,8},{24,16},{1,25},{9,1},{17,9},{25,17},{2,26},{10... | collective-permute-start | bytes 1179656 | tf_op jit(solution)/shard_map/ppermute | solution.py:150
  41.8 11.8 %copy-start.3 = (s32[1,1,256]{2,1,0:T(1,128)S(1)}, s32[1,1,256]{2,1,0:T(1,128)}, u32[]{:S(2)}) copy-start(s32[1,1,256]{2,1,0:T(1,128)} %param.8) | copy-start | bytes 3076
  41.8 11.8 %copy-start.4 = (s32[1,1,256]{2,1,0:T(1,128)S(1)}, s32[1,1,256]{2,1,0:T(1,128)}, u32[]{:S(2)}) copy-start(s32[1,1,256]{2,1,0:T(1,128)} %param.9) | copy-start | bytes 3076
  41.8 6.9 %collective-permute-start.5 = (bf16[32,24,128]{2,1,0:T(8,128)(2,1)S(1)}, bf16[32,24,128]{2,1,0:T(8,128)(2,1)S(1)}, u32[]{:S(2)}, u32[]{:S(2)}) collective-permute-start(bf16[32,24,128]{2,1,0:T(8,128)(2,1)S(1)} %slice.32), channel_id=1, source_target_pairs={{0,8},{8,16},{16,24},{24,0},{1,9},{9,17},{17,25},{25,1},{2,10},{10... | collective-permute-start | bytes 589832 | tf_op jit(solution)/shard_map/ppermute | solution.py:150
  41.9 6.8 %collective-permute-start.6 = (bf16[32,24,128]{2,1,0:T(8,128)(2,1)S(1)}, bf16[32,24,128]{2,1,0:T(8,128)(2,1)S(1)}, u32[]{:S(2)}, u32[]{:S(2)}) collective-permute-start(bf16[32,24,128]{2,1,0:T(8,128)(2,1)S(1)} %slice.33), channel_id=1, source_target_pairs={{0,24},{8,0},{16,8},{24,16},{1,25},{9,1},{17,9},{25,17},{2,26},{10... | collective-permute-start | bytes 589832 | tf_op jit(solution)/shard_map/ppermute | solution.py:150
  48.8 4.9 %collective-permute-start.7 = (bf16[256,24,128]{2,1,0:T(8,128)(2,1)S(1)}, bf16[256,24,128]{2,1,0:T(8,128)(2,1)S(1)}, u32[]{:S(2)}, u32[]{:S(2)}) collective-permute-start(bf16[256,24,128]{2,1,0:T(8,128)(2,1)S(1)} %constant_dynamic-update-slice_fusion.refs_0_), channel_id=1, source_target_pairs={{0,1},{1,0},{2,3},{3,2},{4,5},{5,4},{6,7},{7,6},{8,9},{9,8},{10,11... | collective-permute-start | bytes 4718600 | tf_op jit(solution)/shard_map/ppermute | solution.py:150
  61.7 0.9 copy-start
  62.6 27.7 %all-to-all-start = ((bf16[128,24,128]{2,1,0:T(8,128)(2,1)}), bf16[128,24,128]{2,1,0:T(8,128)(2,1)S(1)}, u32[]{:S(2)}, u32[]{:S(2)}) async-start(bf16[128,24,128]{2,1,0:T(8,128)(2,1)} %copy-done), calls=%async_computation | async-start | bytes 1572864 | tf_op jit(solution)/shard_map/all_to_all | solution.py:172
  66.3 113.4 %all-gather.6.cloned.1.call-start = ((), (), s32[]{:S(2)}) async-start(), calls=%async_computation.7 | async-start | bytes 5406720 | tf_op jit(solution)/shard_map/all_gather | solution.py:217
  90.4 0.9 copy-start.9
  91.3 22.0 %copy-start.5 = (f32[16,64,128]{2,1,0:T(8,128)S(1)}, f32[16,64,128]{2,1,0:T(8,128)}, u32[]{:S(2)}) copy-start(f32[16,64,128]{2,1,0:T(8,128)} %param.6) | copy-start | bytes 1572868
  113.3 1.2 copy-start.10
  115.5 94.0 %copy-start.12 = (f32[16,24,128]{2,1,0:T(8,128)}, f32[16,24,128]{2,1,0:T(8,128)S(1)}, u32[]{:S(2)}) copy-start(f32[16,24,128]{2,1,0:T(8,128)S(1)} %get-tuple-element.59) | copy-start | bytes 589828
  115.5 7.7 %collective-permute-start.8 = (bf16[16,24,128]{2,1,0:T(8,128)(2,1)S(1)}, bf16[16,24,128]{2,1,0:T(8,128)(2,1)S(1)}, u32[]{:S(2)}, u32[]{:S(2)}) collective-permute-start(bf16[16,24,128]{2,1,0:T(8,128)(2,1)S(1)} %get-tuple-element.32), channel_id=1, source_target_pairs={{0,4},{2,6},{4,0},{6,2},{1,5},{3,7},{5,1},{7,3},{8,12},{10,14},{12... | collective-permute-start | bytes 294920 | tf_op jit(solution)/shard_map/ppermute | solution.py:150
  117.2 11.1 %collective-permute-start.9 = (bf16[16,24,128]{2,1,0:T(8,128)(2,1)S(1)}, bf16[16,24,128]{2,1,0:T(8,128)(2,1)S(1)}, u32[]{:S(2)}, u32[]{:S(2)}) collective-permute-start(bf16[16,24,128]{2,1,0:T(8,128)(2,1)S(1)} %get-tuple-element.32), channel_id=1, source_target_pairs={{0,2},{2,4},{4,6},{6,0},{1,3},{3,5},{5,7},{7,1},{8,10},{10,12},{12... | collective-permute-start | bytes 294920 | tf_op jit(solution)/shard_map/ppermute | solution.py:150
  119.9 11.3 %collective-permute-start.10 = (bf16[16,24,128]{2,1,0:T(8,128)(2,1)S(1)}, bf16[16,24,128]{2,1,0:T(8,128)(2,1)S(1)}, u32[]{:S(2)}, u32[]{:S(2)}) collective-permute-start(bf16[16,24,128]{2,1,0:T(8,128)(2,1)S(1)} %get-tuple-element.32), channel_id=1, source_target_pairs={{0,6},{2,0},{4,2},{6,4},{1,7},{3,1},{5,3},{7,5},{8,14},{10,8},{12,... | collective-permute-start | bytes 294920 | tf_op jit(solution)/shard_map/ppermute | solution.py:150
  131.2 13.4 %collective-permute-start.11 = (bf16[64,24,128]{2,1,0:T(8,128)(2,1)S(1)}, bf16[64,24,128]{2,1,0:T(8,128)(2,1)S(1)}, u32[]{:S(2)}, u32[]{:S(2)}) collective-permute-start(bf16[64,24,128]{2,1,0:T(8,128)(2,1)S(1)} %get-tuple-element.70), channel_id=1, source_target_pairs={{0,8},{8,16},{16,24},{24,0},{1,9},{9,17},{17,25},{25,1},{2,10},{10... | collective-permute-start | bytes 1179656 | tf_op jit(solution)/shard_map/ppermute | solution.py:150
  132.9 12.1 %collective-permute-start.12 = (bf16[64,24,128]{2,1,0:T(8,128)(2,1)S(1)}, bf16[64,24,128]{2,1,0:T(8,128)(2,1)S(1)}, u32[]{:S(2)}, u32[]{:S(2)}) collective-permute-start(bf16[64,24,128]{2,1,0:T(8,128)(2,1)S(1)} %get-tuple-element.70), channel_id=1, source_target_pairs={{0,24},{8,0},{16,8},{24,16},{1,25},{9,1},{17,9},{25,17},{2,26},{10... | collective-permute-start | bytes 1179656 | tf_op jit(solution)/shard_map/ppermute | solution.py:150
  144.6 6.9 %collective-permute-start.13 = (bf16[32,24,128]{2,1,0:T(8,128)(2,1)S(1)}, bf16[32,24,128]{2,1,0:T(8,128)(2,1)S(1)}, u32[]{:S(2)}, u32[]{:S(2)}) collective-permute-start(bf16[32,24,128]{2,1,0:T(8,128)(2,1)S(1)} %slice.34), channel_id=1, source_target_pairs={{0,8},{8,16},{16,24},{24,0},{1,9},{9,17},{17,25},{25,1},{2,10},{10... | collective-permute-start | bytes 589832 | tf_op jit(solution)/shard_map/ppermute | solution.py:150
  145.0 6.5 %collective-permute-start.14 = (bf16[32,24,128]{2,1,0:T(8,128)(2,1)S(1)}, bf16[32,24,128]{2,1,0:T(8,128)(2,1)S(1)}, u32[]{:S(2)}, u32[]{:S(2)}) collective-permute-start(bf16[32,24,128]{2,1,0:T(8,128)(2,1)S(1)} %slice.35), channel_id=1, source_target_pairs={{0,24},{8,0},{16,8},{24,16},{1,25},{9,1},{17,9},{25,17},{2,26},{10... | collective-permute-start | bytes 589832 | tf_op jit(solution)/shard_map/ppermute | solution.py:150
  151.6 7.6 %collective-permute-start.15 = (bf16[256,24,128]{2,1,0:T(8,128)(2,1)S(1)}, bf16[256,24,128]{2,1,0:T(8,128)(2,1)S(1)}, u32[]{:S(2)}, u32[]{:S(2)}) collective-permute-start(bf16[256,24,128]{2,1,0:T(8,128)(2,1)S(1)} %constant_dynamic-update-slice_fusion.12.refs_0_), channel_id=1, source_target_pairs={{0,1},{1,0},{2,3},{3,2},{4,5},{5,4},{6,7},{7,6},{8,9},{9,8},{10,11... | collective-permute-start | bytes 4718600 | tf_op jit(solution)/shard_map/ppermute | solution.py:150
  167.3 0.9 copy-start.1
  168.2 18.1 %all-to-all-start.2 = ((bf16[128,24,128]{2,1,0:T(8,128)(2,1)}), bf16[128,24,128]{2,1,0:T(8,128)(2,1)S(1)}, u32[]{:S(2)}, u32[]{:S(2)}) async-start(bf16[128,24,128]{2,1,0:T(8,128)(2,1)} %copy-done.1), calls=%async_computation.2 | async-start | bytes 1572864 | tf_op jit(solution)/shard_map/all_to_all | solution.py:172
  171.7 102.7 %all-gather.8.cloned.1.call-start = ((), (), s32[]{:S(2)}) async-start(), calls=%async_computation.8 | async-start | bytes 5406720 | tf_op jit(solution)/shard_map/all_gather | solution.py:217
  186.3 22.2 %copy-start.11 = (f32[16,40,128]{2,1,0:T(8,128)S(1)}, f32[16,40,128]{2,1,0:T(8,128)}, u32[]{:S(2)}) copy-start(f32[16,40,128]{2,1,0:T(8,128)} %get-tuple-element.57) | copy-start | bytes 983044
  186.3 0.9 copy-start.7
  208.5 1.2 copy-start.8
  210.4 7.6 %collective-permute-start.16 = (bf16[16,24,128]{2,1,0:T(8,128)(2,1)S(1)}, bf16[16,24,128]{2,1,0:T(8,128)(2,1)S(1)}, u32[]{:S(2)}, u32[]{:S(2)}) collective-permute-start(bf16[16,24,128]{2,1,0:T(8,128)(2,1)S(1)} %get-tuple-element.40), channel_id=1, source_target_pairs={{0,4},{2,6},{4,0},{6,2},{1,5},{3,7},{5,1},{7,3},{8,12},{10,14},{12... | collective-permute-start | bytes 294920 | tf_op jit(solution)/shard_map/ppermute | solution.py:150
  211.9 10.9 %collective-permute-start.17 = (bf16[16,24,128]{2,1,0:T(8,128)(2,1)S(1)}, bf16[16,24,128]{2,1,0:T(8,128)(2,1)S(1)}, u32[]{:S(2)}, u32[]{:S(2)}) collective-permute-start(bf16[16,24,128]{2,1,0:T(8,128)(2,1)S(1)} %get-tuple-element.40), channel_id=1, source_target_pairs={{0,2},{2,4},{4,6},{6,0},{1,3},{3,5},{5,7},{7,1},{8,10},{10,12},{12... | collective-permute-start | bytes 294920 | tf_op jit(solution)/shard_map/ppermute | solution.py:150
  214.9 11.3 %collective-permute-start.18 = (bf16[16,24,128]{2,1,0:T(8,128)(2,1)S(1)}, bf16[16,24,128]{2,1,0:T(8,128)(2,1)S(1)}, u32[]{:S(2)}, u32[]{:S(2)}) collective-permute-start(bf16[16,24,128]{2,1,0:T(8,128)(2,1)S(1)} %get-tuple-element.40), channel_id=1, source_target_pairs={{0,6},{2,0},{4,2},{6,4},{1,7},{3,1},{5,3},{7,5},{8,14},{10,8},{12,... | collective-permute-start | bytes 294920 | tf_op jit(solution)/shard_map/ppermute | solution.py:150
  226.2 13.1 %collective-permute-start.19 = (bf16[64,24,128]{2,1,0:T(8,128)(2,1)S(1)}, bf16[64,24,128]{2,1,0:T(8,128)(2,1)S(1)}, u32[]{:S(2)}, u32[]{:S(2)}) collective-permute-start(bf16[64,24,128]{2,1,0:T(8,128)(2,1)S(1)} %get-tuple-element.62), channel_id=1, source_target_pairs={{0,8},{8,16},{16,24},{24,0},{1,9},{9,17},{17,25},{25,1},{2,10},{10... | collective-permute-start | bytes 1179656 | tf_op jit(solution)/shard_map/ppermute | solution.py:150
  228.9 11.2 %collective-permute-start.20 = (bf16[64,24,128]{2,1,0:T(8,128)(2,1)S(1)}, bf16[64,24,128]{2,1,0:T(8,128)(2,1)S(1)}, u32[]{:S(2)}, u32[]{:S(2)}) collective-permute-start(bf16[64,24,128]{2,1,0:T(8,128)(2,1)S(1)} %get-tuple-element.62), channel_id=1, source_target_pairs={{0,24},{8,0},{16,8},{24,16},{1,25},{9,1},{17,9},{25,17},{2,26},{10... | collective-permute-start | bytes 1179656 | tf_op jit(solution)/shard_map/ppermute | solution.py:150
  239.4 6.8 %collective-permute-start.21 = (bf16[32,24,128]{2,1,0:T(8,128)(2,1)S(1)}, bf16[32,24,128]{2,1,0:T(8,128)(2,1)S(1)}, u32[]{:S(2)}, u32[]{:S(2)}) collective-permute-start(bf16[32,24,128]{2,1,0:T(8,128)(2,1)S(1)} %slice.36), channel_id=1, source_target_pairs={{0,8},{8,16},{16,24},{24,0},{1,9},{9,17},{17,25},{25,1},{2,10},{10... | collective-permute-start | bytes 589832 | tf_op jit(solution)/shard_map/ppermute | solution.py:150
  240.1 6.1 %collective-permute-start.22 = (bf16[32,24,128]{2,1,0:T(8,128)(2,1)S(1)}, bf16[32,24,128]{2,1,0:T(8,128)(2,1)S(1)}, u32[]{:S(2)}, u32[]{:S(2)}) collective-permute-start(bf16[32,24,128]{2,1,0:T(8,128)(2,1)S(1)} %slice.37), channel_id=1, source_target_pairs={{0,24},{8,0},{16,8},{24,16},{1,25},{9,1},{17,9},{25,17},{2,26},{10... | collective-permute-start | bytes 589832 | tf_op jit(solution)/shard_map/ppermute | solution.py:150
  246.3 7.8 %collective-permute-start.23 = (bf16[256,24,128]{2,1,0:T(8,128)(2,1)S(1)}, bf16[256,24,128]{2,1,0:T(8,128)(2,1)S(1)}, u32[]{:S(2)}, u32[]{:S(2)}) collective-permute-start(bf16[256,24,128]{2,1,0:T(8,128)(2,1)S(1)} %constant_dynamic-update-slice_fusion.24.refs_0_), channel_id=1, source_target_pairs={{0,1},{1,0},{2,3},{3,2},{4,5},{5,4},{6,7},{7,6},{8,9},{9,8},{10,11... | collective-permute-start | bytes 4718600 | tf_op jit(solution)/shard_map/ppermute | solution.py:150
  262.1 0.9 copy-start.2
  263.1 19.0 %all-to-all-start.4 = ((bf16[128,24,128]{2,1,0:T(8,128)(2,1)}), bf16[128,24,128]{2,1,0:T(8,128)(2,1)S(1)}, u32[]{:S(2)}, u32[]{:S(2)}) async-start(bf16[128,24,128]{2,1,0:T(8,128)(2,1)} %copy-done.2), calls=%async_computation.4 | async-start | bytes 1572864 | tf_op jit(solution)/shard_map/all_to_all | solution.py:172
  282.1 4.7 %copy-start.15 = (s32[16,128]{1,0:T(8,128)S(1)}, s32[16,128]{1,0:T(8,128)}, u32[]{:S(2)}) copy-start(s32[16,128]{1,0:T(8,128)} %param.10) | copy-start | bytes 24580
  282.1 4.7 %copy-start.6 = (f32[16,64,128]{2,1,0:T(8,128)S(1)}, f32[16,64,128]{2,1,0:T(8,128)}, u32[]{:S(2)}) copy-start(f32[16,64,128]{2,1,0:T(8,128)} %param.6) | copy-start | bytes 1572868
  282.1 21.9 %all-to-all-start.5 = ((bf16[128,40,128]{2,1,0:T(8,128)(2,1)}), bf16[128,40,128]{2,1,0:T(8,128)(2,1)S(1)}, u32[]{:S(2)}, u32[]{:S(2)}) async-start(bf16[128,40,128]{2,1,0:T(8,128)(2,1)} %get-tuple-element.46), calls=%async_computation.5 | async-start | bytes 2621440 | tf_op jit(solution)/shard_map/all_to_all | solution.py:172
  304.1 1.4 copy-start.13
  304.1 1.4 copy-start.14
Sparse Core Ops, SparseCore 0:
  11.1 72.6 all-gather.3
  114.4 65.2 all-gather.5
  209.6 64.8 all-gather.7
